TPU v7x, 256 devices: a whole 4x4x8 slice. The times are simulated.
256 devices in a mesh: dap: 128 (over x_lo, y, z, core), dp: 2 (over x_hi).
Axes of the slice: x: 4 (x_hi: 2, x_lo: 2; x = x_hi * 2 + x_lo), y: 4, z: 8, core: 2. Of those that a mesh axis runs over, the one named last changes fastest.
Arguments:
- alignment_embedding: bfloat16 [256, 128, 256], P('dp', 'dap'), parts along dimension 0, may hold values from -6 to 6
- alignment_existing_flags: int32 [256, 128], P('dp', 'dap'), parts along dimension 0, may hold values 0 or 1
- couple_embedding: bfloat16 [256, 128, 128], P(('dp', 'dap')), parts along dimension 0, may hold values from -6 to 6
- alignment_scaling_factor: float32 [256], replicated, may hold values from 0.1 to 1.9
- couple_scaling_factor: float32 [128], replicated, may hold values from 0.1 to 1.9
- request_matrix: bfloat16 [256, 256], replicated, may hold values from -0.375 to 0.375
- lookup_matrix: bfloat16 [256, 256], replicated, may hold values from -0.375 to 0.375
- content_matrix: bfloat16 [256, 256], replicated, may hold values from -0.375 to 0.375
- switch_matrix: bfloat16 [256, 256], replicated, may hold values from -0.375 to 0.375
- final_projection_matrix: bfloat16 [256, 256], replicated, may hold values from -0.375 to 0.375
- couple_to_headterm_matrix: bfloat16 [128, 8], replicated, may hold values from -30 to 30
- increment_adjoint: bfloat16 [256, 128, 256], P('dp', 'dap'), parts along dimension 0, may hold values from -48 to 48
Outputs:
- alignment_increment: bfloat16 [256, 128, 256], P('dp', 'dap'), parts along dimension 0
- alignment_adjoint: bfloat16 [256, 128, 256], P('dp', 'dap'), parts along dimension 0
- couple_adjoint: bfloat16 [256, 128, 128], P(('dp', 'dap')), parts along dimension 0
- d_w_query: float32 [512, 256], P('dp'), parts along dimension 0
- d_w_key: float32 [512, 256], P('dp'), parts along dimension 0
- d_w_value: float32 [512, 256], P('dp'), parts along dimension 0
- d_w_gate: float32 [512, 256], P('dp'), parts along dimension 0
- d_w_out: float32 [512, 256], P('dp'), parts along dimension 0
- couple_headterm_adjoint: float32 [256, 8], P('dp'), parts along dimension 0
- d_msa_gain: float32 [512], P('dp'), parts along dimension 0
- couple_scaling_adjoint: float32 [256], P('dp'), parts along dimension 0
There are 2 independent parts, one for each index of `dp`. A program takes and returns all parts, laid end to end along the dimension named above; an argument that names none is the same for every part. Nothing has to cross between parts.
All inputs are finite; a program needn't handle non-finite values. No bound on the sum of `alignment_existing_flags` on one device may be relied on, other than what follows from the above.
Results may differ from a plain program's by a relative error of at most 0.012.
The roundings to bfloat16 on the way count: a program that leaves them out, or rounds other values in their place, can miss the bound.
Values may be sent and summed in bfloat16 or wider, within the bound.
No kernel may reach another device: no remote copies, remote signals or barrier semaphores. Data moves between devices by JAX's collectives and lax.ppermute only.
A program may use at most 64 MiB of HBM per device.

v0:
```python
import jax
import jax.numpy as jnp
from jax import lax
from jax.sharding import PartitionSpec as P

ALIGN_FEATURES = 256
HEAD_NUMBER = 8
HEAD_DIMENSION = 32


EPS = 1e-05


def standardise_features(value, gain):
    mean = jnp.mean(value, axis=-1, keepdims=True)
    centered = value - mean
    variance = jnp.mean(centered * centered, axis=-1, keepdims=True)
    reciprocal_spread = lax.rsqrt(variance + EPS)
    standardised_lines = centered * reciprocal_spread
    return (standardised_lines, reciprocal_spread, standardised_lines * gain)


def standardise_features_adjoint(upstream_gradient, standardised_lines, reciprocal_spread, gain):
    rescaled_request = upstream_gradient * gain
    return reciprocal_spread * (
        rescaled_request
        - jnp.mean(rescaled_request, axis=-1, keepdims=True)
        - standardised_lines
        * jnp.mean(rescaled_request * standardised_lines, axis=-1, keepdims=True)
    )


def tensor_product(left, right):
    return lax.dot_general(
        left, right, (((0,), (0,)), ((), ())), preferred_element_type=jnp.float32
    )


def onward_one_line(
    alignment_line_content,
    line_filter_flags,
    couple_headwise_terms,
    alignment_scaling_factor,
    request_matrix,
    lookup_matrix,
    content_matrix,
    switch_matrix,
    final_projection_matrix,
):
    element_number = alignment_line_content.shape[0]
    standardised_lines, reciprocal_spread, rescaled_request = standardise_features(
        alignment_line_content.astype(jnp.float32), alignment_scaling_factor
    )
    input_arrays = rescaled_request.astype(jnp.bfloat16)
    query = (
        jnp.dot(input_arrays, request_matrix, preferred_element_type=jnp.float32)
        * HEAD_DIMENSION ** (-0.5)
    ).astype(jnp.bfloat16)
    keys = jnp.dot(input_arrays, lookup_matrix, preferred_element_type=jnp.float32).astype(
        jnp.bfloat16
    )
    values = jnp.dot(input_arrays, content_matrix, preferred_element_type=jnp.float32).astype(
        jnp.bfloat16
    )
    gate_sigmoid = jax.nn.sigmoid(
        jnp.dot(input_arrays, switch_matrix, preferred_element_type=jnp.float32)
    )
    query = query.reshape(element_number, HEAD_NUMBER, HEAD_DIMENSION)
    keys = keys.reshape(element_number, HEAD_NUMBER, HEAD_DIMENSION)
    values = values.reshape(element_number, HEAD_NUMBER, HEAD_DIMENSION)
    scores = jnp.einsum("ihd,jhd->ihj", query, keys, preferred_element_type=jnp.float32)
    scores = (
        scores
        + couple_headwise_terms.astype(jnp.float32)
        + (1000000000.0 * (line_filter_flags.astype(jnp.float32) - 1.0))[None, None, :]
    )
    probs = jax.nn.softmax(scores, axis=-1)
    probs_low = probs.astype(jnp.bfloat16)
    attention_probs = jnp.einsum(
        "ihj,jhd->ihd", probs_low, values, preferred_element_type=jnp.float32
    ).reshape(element_number, HEAD_NUMBER * HEAD_DIMENSION)
    weighted_values = (gate_sigmoid * attention_probs).astype(jnp.bfloat16)
    alignment_increment = jnp.dot(
        weighted_values, final_projection_matrix, preferred_element_type=jnp.float32
    ).astype(jnp.bfloat16)
    kept_intermediates = (
        standardised_lines,
        reciprocal_spread,
        input_arrays,
        query,
        keys,
        values,
        gate_sigmoid,
        attention_probs,
        weighted_values,
        probs,
    )
    return (alignment_increment, kept_intermediates)


def reverse_one_line(
    line_adjoint_routine,
    kept_intermediates,
    alignment_scaling_factor,
    request_matrix,
    lookup_matrix,
    content_matrix,
    switch_matrix,
    final_projection_matrix,
):
    (
        standardised_lines,
        reciprocal_spread,
        input_arrays,
        query,
        keys,
        values,
        gate_sigmoid,
        attention_probs,
        weighted_values,
        probs,
    ) = kept_intermediates
    element_number = line_adjoint_routine.shape[0]
    probs_low = probs.astype(jnp.bfloat16)
    upstream_gradient = lax.dot_general(
        line_adjoint_routine,
        final_projection_matrix,
        (((1,), (1,)), ((), ())),
        preferred_element_type=jnp.float32,
    )
    d_attn = (upstream_gradient * gate_sigmoid).astype(jnp.bfloat16)
    gate_logit_gradient = (
        upstream_gradient * attention_probs * gate_sigmoid * (1.0 - gate_sigmoid)
    ).astype(jnp.bfloat16)
    d_attn_heads = d_attn.reshape(element_number, HEAD_NUMBER, HEAD_DIMENSION)
    d_probs = jnp.einsum("ihd,jhd->ihj", d_attn_heads, values, preferred_element_type=jnp.float32)
    affinity_adjoint = probs * (d_probs - jnp.sum(probs * d_probs, axis=-1, keepdims=True))
    d_low = affinity_adjoint.astype(jnp.bfloat16)
    query_gradient = (
        (
            jnp.einsum("ihj,jhd->ihd", d_low, keys, preferred_element_type=jnp.float32)
            * HEAD_DIMENSION ** (-0.5)
        )
        .astype(jnp.bfloat16)
        .reshape(element_number, HEAD_NUMBER * HEAD_DIMENSION)
    )
    key_gradient = (
        jnp.einsum("ihj,ihd->jhd", d_low, query, preferred_element_type=jnp.float32)
        .astype(jnp.bfloat16)
        .reshape(element_number, HEAD_NUMBER * HEAD_DIMENSION)
    )
    value_gradient = (
        jnp.einsum("ihj,ihd->jhd", probs_low, d_attn_heads, preferred_element_type=jnp.float32)
        .astype(jnp.bfloat16)
        .reshape(element_number, HEAD_NUMBER * HEAD_DIMENSION)
    )
    backward_result = (((1,), (1,)), ((), ()))
    argument_adjoints = lax.dot_general(
        query_gradient, request_matrix, backward_result, preferred_element_type=jnp.float32
    )
    argument_adjoints = argument_adjoints + lax.dot_general(
        key_gradient, lookup_matrix, backward_result, preferred_element_type=jnp.float32
    )
    argument_adjoints = argument_adjoints + lax.dot_general(
        value_gradient, content_matrix, backward_result, preferred_element_type=jnp.float32
    )
    argument_adjoints = argument_adjoints + lax.dot_general(
        gate_logit_gradient, switch_matrix, backward_result, preferred_element_type=jnp.float32
    )
    line_adjoint = standardise_features_adjoint(
        argument_adjoints, standardised_lines, reciprocal_spread, alignment_scaling_factor
    ).astype(jnp.bfloat16)
    matrix_adjoints = (
        tensor_product(input_arrays, query_gradient),
        tensor_product(input_arrays, key_gradient),
        tensor_product(input_arrays, value_gradient),
        tensor_product(input_arrays, gate_logit_gradient),
        tensor_product(weighted_values, line_adjoint_routine),
        jnp.sum(argument_adjoints * standardised_lines, axis=0),
    )
    return (line_adjoint, affinity_adjoint, matrix_adjoints)


def on_device(
    alignment_embedding,
    alignment_existing_flags,
    couple_embedding,
    alignment_scaling_factor,
    couple_scaling_factor,
    request_matrix,
    lookup_matrix,
    content_matrix,
    switch_matrix,
    final_projection_matrix,
    couple_to_headterm_matrix,
    increment_adjoint,
):
    filter_shared = alignment_existing_flags.astype(jnp.bfloat16)
    alignment_line_embedding, alignment_line_flags = (
        lax.all_to_all(alignment_embedding, "dap", split_axis=0, concat_axis=1, tiled=True),
        lax.all_to_all(filter_shared, "dap", split_axis=0, concat_axis=1, tiled=True),
    )
    pair_hat, pair_inv, pair_scaled = standardise_features(
        couple_embedding.astype(jnp.float32), couple_scaling_factor
    )
    pair_ln = pair_scaled.astype(jnp.bfloat16)
    bias_rows = jnp.einsum(
        "ijc,ch->ihj", pair_ln, couple_to_headterm_matrix, preferred_element_type=jnp.float32
    ).astype(jnp.bfloat16)
    couple_headwise_terms = lax.all_gather(bias_rows, "dap", axis=0, tiled=True)

    def onward_loop_step(carry, loop_elements):
        alignment_increment, kept_intermediates = onward_one_line(
            loop_elements[0],
            loop_elements[1],
            couple_headwise_terms,
            alignment_scaling_factor,
            request_matrix,
            lookup_matrix,
            content_matrix,
            switch_matrix,
            final_projection_matrix,
        )
        return (carry, (alignment_increment, kept_intermediates))

    unused_value, (row_updates, all_saved_residuals) = lax.scan(
        onward_loop_step, None, (alignment_line_embedding, alignment_line_flags)
    )
    update_out = lax.all_to_all(row_updates, "dap", split_axis=1, concat_axis=0, tiled=True)
    seq_grad = lax.all_to_all(increment_adjoint, "dap", split_axis=0, concat_axis=1, tiled=True)
    amino_positions = alignment_line_embedding.shape[1]
    span_length = HEAD_NUMBER * HEAD_DIMENSION
    blank_matrix = (
        jnp.zeros((ALIGN_FEATURES, span_length), jnp.float32),
        jnp.zeros((ALIGN_FEATURES, span_length), jnp.float32),
        jnp.zeros((ALIGN_FEATURES, span_length), jnp.float32),
        jnp.zeros((ALIGN_FEATURES, span_length), jnp.float32),
        jnp.zeros((span_length, ALIGN_FEATURES), jnp.float32),
        jnp.zeros((ALIGN_FEATURES,), jnp.float32),
    )

    def backward_step(carry, loop_elements):
        bias_sum, subtotal_list = carry
        line_adjoint, affinity_adjoint, matrix_adjoints = reverse_one_line(
            loop_elements[0],
            loop_elements[1],
            alignment_scaling_factor,
            request_matrix,
            lookup_matrix,
            content_matrix,
            switch_matrix,
            final_projection_matrix,
        )
        subtotal_list = tuple((a + b for a, b in zip(subtotal_list, matrix_adjoints)))
        return ((bias_sum + affinity_adjoint, subtotal_list), line_adjoint)

    beginning_shift = (
        jnp.zeros((amino_positions, HEAD_NUMBER, amino_positions), jnp.float32),
        blank_matrix,
    )
    (bias_term, subtotal_list), line_adjoint_list = lax.scan(
        backward_step, beginning_shift, (seq_grad, all_saved_residuals)
    )
    additive_term_adjoint = lax.psum_scatter(bias_term, "dap", scatter_dimension=0, tiled=True)
    d_pln = jnp.einsum(
        "ihj,ch->ijc",
        additive_term_adjoint,
        couple_to_headterm_matrix.astype(jnp.float32),
        precision=lax.Precision.HIGHEST,
    )
    w_bias_part = jnp.einsum(
        "ijc,ihj->ch",
        pair_ln.astype(jnp.float32),
        additive_term_adjoint,
        precision=lax.Precision.HIGHEST,
    )
    pair_gain_part = jnp.sum(d_pln * pair_hat, axis=(0, 1))
    couple_adjoint = standardise_features_adjoint(
        d_pln, pair_hat, pair_inv, couple_scaling_factor
    ).astype(jnp.bfloat16)
    totals = lax.psum(
        (
            subtotal_list[0],
            subtotal_list[1],
            subtotal_list[2],
            subtotal_list[3],
            subtotal_list[4],
            w_bias_part,
            subtotal_list[5],
            pair_gain_part,
        ),
        "dap",
    )
    alignment_adjoint = lax.all_to_all(
        line_adjoint_list, "dap", split_axis=1, concat_axis=0, tiled=True
    )
    return (
        update_out,
        alignment_adjoint,
        couple_adjoint,
        totals[0],
        totals[1],
        totals[2],
        totals[3],
        totals[4],
        totals[5],
        totals[6],
        totals[7],
    )


def solution(mesh):
    in_specs = (
        P("dp", "dap", None),
        P("dp", "dap"),
        P(("dp", "dap"), None, None),
        P(),
        P(),
        P(),
        P(),
        P(),
        P(),
        P(),
        P(),
        P("dp", "dap", None),
    )
    out_specs = (
        P("dp", "dap", None),
        P("dp", "dap", None),
        P(("dp", "dap"), None, None),
        P("dp", None),
        P("dp", None),
        P("dp", None),
        P("dp", None),
        P("dp", None),
        P("dp", None),
        P("dp"),
        P("dp"),
    )
    return jax.shard_map(
        on_device, mesh=mesh, in_specs=in_specs, out_specs=out_specs, check_vma=False
    )
```

profile of v0, /device:TPU:1, one launch (start us, length us, event | category | flops | bytes accessed | tf_op | source)
XLA Modules:
  0.0 1599.9 jit_solution(11764958021694046716)
XLA Ops:
  8.7 15.0 all-to-all-start.1
  24.7 158.3 %all-gather = bf16[1024,128]{1,0:T(8,128)(2,1)S(1)} all-gather(bf16[8,128]{1,0:T(8,128)(2,1)S(1)} %fusion.11), channel_id=2, replica_groups=mesh['dap'=128,'dp'=2] {'dap'}, dimensions={0}, use_global_device_ids=true | all-gather | bytes 264192 | tf_op jit(solution)/shard_map/all_gather | solution.py:210
  184.9 5.3 all-to-all-start
  190.3 0.8 copy-done.11
  192.6 1.0 multiply_reduce_fusion.2
  193.6 7.3 all-to-all-done
  200.9 5.8 all-to-all-start.3
  211.5 5.9 all-to-all-done.3
  219.1 1.0 copy.89
  220.1 1.0 fusion.67
  221.1 1.0 fusion.65
  222.1 1.0 fusion.63
  223.1 1.0 fusion.69
  224.1 0.9 fusion.50
  225.3 1.0 reduce.10
  227.0 7.7 all-to-all-start.2
  235.9 1.0 reduce.11
  237.6 7.8 all-to-all-done.2
  245.4 5.7 all-to-all-start.4
  253.1 8.9 all-to-all-done.4
  262.7 1037.9 %all-reduce.5.cloned.1.call-done = (f32[128,8,128]{2,1,0:T(8,128)}, f32[256,256]{1,0:T(8,128)}, f32[256,256]{1,0:T(8,128)}, f32[256,256]{1,0:T(8,128)}, f32[256,256]{1,0:T(8,128)}, /*index=5*/f32[256,256]{1,0:T(8,128)}) async-done(((f32[128,8,128]{2,1,0:T(8,128)}, f32[256,256]{1,0:T(8,128)}, f32[256,256]{1,0:T(8,128)}, f32[256,256]{1,0:T(8,128)}, f32[256,256]{1,0:T(8,128)}, ...) | async-done | bytes 1835024
  1300.6 1.7 fusion.46
  1302.3 1.5 fusion.57
  1304.8 283.4 %all-reduce.1 = (f32[128,8]{0,1:T(8,128)}, f32[256]{0:T(256)}, f32[128]{0:T(128)}) all-reduce(f32[128,8]{0,1:T(8,128)S(1)} %fusion.57, f32[256]{0:T(256)S(1)} %get-tuple-element.196, f32[128]{0:T(128)S(1)} %get-tuple-element.199), channel_id=1, replica_groups=mesh['dap'=128,'dp'=2] {'dap'}, use_global_device_ids=true, to_apply=%region_17.18 | all-reduce | flops 1408 | bytes 11264 | tf_op jit(solution)/shard_map/psum | solution.py:281
  (100 shorter events, 23.4 us)
Async XLA Ops:
  7.2 210.4 %copy-start = (bf16[256,256]{1,0:T(8,128)(2,1)S(1)}, bf16[256,256]{1,0:T(8,128)(2,1)}, u32[]{:S(2)}) copy-start(bf16[256,256]{1,0:T(8,128)(2,1)} %param.20) | copy-start | bytes 393220
  8.7 15.0 copy-start.13
  8.7 176.2 %all-to-all-start.1 = ((bf16[128,1,1]{2,1,0:T(2,128)(2,1)}), bf16[128,1,1]{2,1,0:T(2,128)(2,1)S(1)}, u32[]{:S(2)}, u32[]{:S(2)}) async-start(bf16[128,1,1]{2,1,0:T(2,128)(2,1)} %copy.78), calls=%async_computation.1 | async-start | bytes 131072 | tf_op jit(solution)/shard_map/all_to_all | solution.py:201
  23.8 0.7 copy-start.15
  23.9 0.7 copy-start.14
  24.7 158.8 %copy-start.10 = (bf16[128,1,256]{2,0,1:T(8,128)(2,1)S(1)}, bf16[128,1,256]{2,0,1:T(8,128)(2,1)}, u32[]{:S(2)}) copy-start(bf16[128,1,256]{2,0,1:T(8,128)(2,1)} %param.12) | copy-start | bytes 196612
  184.9 16.0 %all-to-all-start = ((bf16[128,2,128]{2,1,0:T(2,128)(2,1)}), bf16[128,2,128]{2,1,0:T(2,128)(2,1)S(1)}, u32[]{:S(2)}, u32[]{:S(2)}) async-start(bf16[128,2,128]{2,1,0:T(2,128)(2,1)} %reshape.335), calls=%async_computation | async-start | bytes 131072 | tf_op jit(solution)/shard_map/all_to_all | solution.py:200
  190.2 0.8 copy-start.11
  200.9 16.5 %all-to-all-start.3 = ((bf16[128,2,128]{2,1,0:T(2,128)(2,1)}), bf16[128,2,128]{2,1,0:T(2,128)(2,1)S(1)}, u32[]{:S(2)}, u32[]{:S(2)}) async-start(bf16[128,2,128]{2,1,0:T(2,128)(2,1)} %reshape.339), calls=%async_computation.3 | async-start | bytes 131072 | tf_op jit(solution)/shard_map/all_to_all | solution.py:230
  206.7 1093.9 %all-reduce.5.cloned.1.call-start = ((), (), s32[]{:S(2)}) async-start(), calls=%async_computation.5 | async-start | bytes 3670016
  206.8 0.9 copy-start.8
  207.1 0.7 copy-start.12
  208.0 0.9 copy-start.7
  209.1 0.9 copy-start.9
  211.5 5.9 copy-start.1
  227.0 18.4 %all-to-all-start.2 = ((bf16[128,2,128]{2,1,0:T(2,128)(2,1)}), bf16[128,2,128]{2,1,0:T(2,128)(2,1)S(1)}, u32[]{:S(2)}, u32[]{:S(2)}) async-start(bf16[128,2,128]{2,1,0:T(2,128)(2,1)} %reshape.337), calls=%async_computation.2 | async-start | bytes 131072 | tf_op jit(solution)/shard_map/all_to_all | solution.py:229
  245.4 16.6 %all-to-all-start.4 = ((bf16[128,2,128]{2,1,0:T(2,128)(2,1)}), bf16[128,2,128]{2,1,0:T(2,128)(2,1)S(1)}, u32[]{:S(2)}, u32[]{:S(2)}) async-start(bf16[128,2,128]{2,1,0:T(2,128)(2,1)} %reshape.341), calls=%async_computation.4 | async-start | bytes 131072 | tf_op jit(solution)/shard_map/all_to_all | solution.py:294
  251.1 0.7 copy-start.16
  1300.6 287.6 %copy-start.6 = (f32[256,256]{1,0:T(8,128)S(1)}, f32[256,256]{1,0:T(8,128)}, u32[]{:S(2)}) copy-start(f32[256,256]{1,0:T(8,128)} %get-tuple-element.228) | copy-start | bytes 786436
  1588.2 1.0 copy-start.5
  1589.2 1.0 copy-start.4
  1590.2 1.0 copy-start.3
  1591.3 1.0 copy-start.2
Sparse Core Ops, SparseCore 0:
  225.2 1075.3 all-reduce.4
where the time goes:
time: 1600 us
  waiting for transfers between devices  1070 us (67%)
  blocking collectives  442 us (28%)
  starting transfers between devices  39.5 us (2%)
  local copies, waits for them, and re-layouts  18 us (1%)
    unnamed x2, waiting for transfers between devices  1040 us
    psum x1, blocking collectives, on_device(): lax.psum((subtotal_list[0], subtotal_list[1], subtotal_list[2], subtotal_...  283 us
    all_gather x1, blocking collectives, on_device(): couple_headwise_terms = lax.all_gather(bias_rows, 'dap', axis=0, tiled=True)  158 us
  transfers between devices with their start and end apart: 6, of which 5 were waited for; matrix products, arithmetic and copies ran while one was open for 1% of the time, Pallas kernels for 0%

commit v1 on v0

v1 whole, which is shorter than its diff:
```python
import jax
import jax.numpy as jnp
from jax import lax
from jax.sharding import PartitionSpec as P

ALIGN_FEATURES = 256
CZ = 128
HEADS = 8
HEAD_DIM = 32
LANES = 128
EPS = 1e-05

F32 = jnp.float32
BF16 = jnp.bfloat16


def layer_norm(value, gain):
    mean = jnp.mean(value, axis=-1, keepdims=True)
    centered = value - mean
    variance = jnp.mean(centered * centered, axis=-1, keepdims=True)
    inv = lax.rsqrt(variance + EPS)
    hat = centered * inv
    return hat, inv, hat * gain


def layer_norm_adjoint(upstream, hat, inv, gain):
    ug = upstream * gain
    return inv * (
        ug
        - jnp.mean(ug, axis=-1, keepdims=True)
        - hat * jnp.mean(ug * hat, axis=-1, keepdims=True)
    )


def dot(a, b):
    return jnp.dot(a, b, preferred_element_type=F32)


def dot_nt(a, b):
    return lax.dot_general(a, b, (((1,), (1,)), ((), ())), preferred_element_type=F32)


def dot_tn(a, b):
    return lax.dot_general(a, b, (((0,), (0,)), ((), ())), preferred_element_type=F32)


def exchange(x):
    return lax.all_to_all(x, "dap", split_axis=0, concat_axis=0, tiled=True)


def one_sequence(msa, grad, mask, bias, gain, wq, wk, wv, wg, wo):
    n = msa.shape[0]
    hat, inv, scaled = layer_norm(msa.astype(F32), gain)
    x = scaled.astype(BF16)
    q = (dot(x, wq) * HEAD_DIM ** (-0.5)).astype(BF16).reshape(n, HEADS, HEAD_DIM)
    k = dot(x, wk).astype(BF16).reshape(n, HEADS, HEAD_DIM)
    v = dot(x, wv).astype(BF16).reshape(n, HEADS, HEAD_DIM)
    gate = jax.nn.sigmoid(dot(x, wg))
    scores = jnp.einsum("ihd,jhd->hij", q, k, preferred_element_type=F32)
    scores = scores + bias.astype(F32) + (1e9 * (mask.astype(F32) - 1.0))[None, None, :]
    p32 = jax.nn.softmax(scores, axis=-1)
    p = p32.astype(BF16)
    attn = jnp.einsum("hij,jhd->ihd", p, v, preferred_element_type=F32).reshape(n, -1)
    weighted = (gate * attn).astype(BF16)
    update = dot(weighted, wo).astype(BF16)
    dw = dot_nt(grad, wo)
    d_attn = (dw * gate).astype(BF16)
    d_glog = (dw * attn * gate * (1.0 - gate)).astype(BF16)
    d_attn_h = d_attn.reshape(n, HEADS, HEAD_DIM)
    d_p = jnp.einsum("ihd,jhd->hij", d_attn_h, v, preferred_element_type=F32)
    d_s = p32 * (d_p - jnp.sum(p32 * d_p, axis=-1, keepdims=True))
    d_sb = d_s.astype(BF16)
    d_q = (
        (jnp.einsum("hij,jhd->ihd", d_sb, k, preferred_element_type=F32) * HEAD_DIM ** (-0.5))
        .astype(BF16)
        .reshape(n, -1)
    )
    d_k = jnp.einsum("hij,ihd->jhd", d_sb, q, preferred_element_type=F32).astype(BF16).reshape(n, -1)
    d_v = jnp.einsum("hij,ihd->jhd", p, d_attn_h, preferred_element_type=F32).astype(BF16).reshape(n, -1)
    d_x = dot_nt(d_q, wq) + dot_nt(d_k, wk) + dot_nt(d_v, wv) + dot_nt(d_glog, wg)
    adjoint = layer_norm_adjoint(d_x, hat, inv, gain).astype(BF16)
    weights = (
        dot_tn(x, d_q),
        dot_tn(x, d_k),
        dot_tn(x, d_v),
        dot_tn(x, d_glog),
        dot_tn(weighted, grad),
    )
    d_gain = jnp.sum(d_x * hat, axis=0)
    return update, adjoint, d_s, weights, d_gain


def on_device(msa, flags, pair, gain, pair_gain, wq, wk, wv, wg, wo, w_bias, grad):
    n = msa.shape[0]
    pair_hat, pair_inv, pair_scaled = layer_norm(pair[0].astype(F32), pair_gain)
    pair_ln = pair_scaled.astype(BF16)
    bias_rows = lax.dot_general(
        w_bias, pair_ln, (((0,), (1,)), ((), ())), preferred_element_type=F32
    ).astype(BF16)
    send = jnp.concatenate(
        [
            msa.reshape(n, 2, LANES),
            grad.reshape(n, 2, LANES),
            jnp.broadcast_to(flags.astype(BF16)[:, :, None], (n, 4, LANES)),
            jnp.broadcast_to(bias_rows[None], (n, HEADS, LANES)),
        ],
        axis=1,
    )
    got = exchange(send)
    update, adjoint, d_s, weights, d_gain = one_sequence(
        got[:, 0:2].reshape(n, ALIGN_FEATURES),
        got[:, 2:4].reshape(n, ALIGN_FEATURES),
        got[:, 4, 0],
        got[:, 8:16].transpose(1, 0, 2),
        gain, wq, wk, wv, wg, wo,
    )
    w_rows = 5 * ALIGN_FEATURES * 2 // n
    send = jnp.concatenate(
        [
            update.reshape(n, 2, LANES),
            adjoint.reshape(n, 2, LANES),
            d_s.astype(F32).transpose(1, 0, 2).astype(BF16),
            jnp.stack(weights).astype(BF16).reshape(n, w_rows, LANES),
        ],
        axis=1,
    )
    got = exchange(send)
    update_out = got[:, 0:2].reshape(n, 1, ALIGN_FEATURES)
    adjoint_out = got[:, 2:4].reshape(n, 1, ALIGN_FEATURES)
    sums = jnp.sum(got[:, 4:].astype(F32), axis=0)
    d_bias = sums[:HEADS]
    d_pln = lax.dot_general(
        d_bias, w_bias.astype(F32), (((0,), (1,)), ((), ())), precision=lax.Precision.HIGHEST
    )
    w_bias_part = lax.dot_general(
        d_bias, pair_ln.astype(F32), (((1,), (0,)), ((), ())), precision=lax.Precision.HIGHEST
    )
    pair_gain_part = jnp.sum(d_pln * pair_hat, axis=0, keepdims=True)
    couple_adjoint = layer_norm_adjoint(d_pln, pair_hat, pair_inv, pair_gain).astype(BF16)[None]
    shard = jnp.concatenate(
        [
            sums[HEADS:],
            w_bias_part,
            pair_gain_part,
            d_gain.reshape(2, LANES),
            jnp.zeros((1, LANES), F32),
        ],
        axis=0,
    ).astype(BF16)
    got = exchange(jnp.broadcast_to(shard[None], (n,) + shard.shape))
    totals = got[:, :w_rows].astype(F32).reshape(5, ALIGN_FEATURES, ALIGN_FEATURES)
    small = jnp.sum(got[:, w_rows:].astype(F32), axis=0)
    return (
        update_out,
        adjoint_out,
        couple_adjoint,
        totals[0],
        totals[1],
        totals[2],
        totals[3],
        totals[4],
        small[:HEADS].T,
        small[HEADS + 1 : HEADS + 3].reshape(ALIGN_FEATURES),
        small[HEADS],
    )


def solution(mesh):
    rows = P("dp", "dap", None)
    pair = P(("dp", "dap"), None, None)
    in_specs = (rows, P("dp", "dap"), pair) + (P(),) * 8 + (rows,)
    out_specs = (rows, rows, pair) + (P("dp", None),) * 6 + (P("dp"), P("dp"))
    return jax.shard_map(
        on_device, mesh=mesh, in_specs=in_specs, out_specs=out_specs, check_vma=False
    )
```

time: 1600 us -> 129 us (0.08)
  waiting for transfers between devices: 1070 us -> 26.6 us
  blocking collectives: 442 us -> 68.7 us
  starting transfers between devices: 39.5 us -> 7.66 us
    unnamed x2 -> x0, waiting for transfers between devices: 1040 us -> none
    psum x1 -> x0, blocking collectives: 283 us -> none  [on_device(): lax.psum((subtotal_list[0], subtotal_list[1], subtotal_list[2], subtotal_...]
    all_gather x1 -> x0, blocking collectives: 158 us -> none  [on_device(): couple_headwise_terms = lax.all_gather(bias_rows, 'dap', axis=0, tiled=True)]
    all_to_all x0 -> x2, blocking collectives: none -> 68.7 us  [exchange(): return lax.all_to_all(x, 'dap', split_axis=0, concat_axis=0, tiled=True)]
    all_to_all x5 -> x1, starting transfers between devices: 39.5 us -> 7.66 us  [exchange(): return lax.all_to_all(x, 'dap', split_axis=0, concat_axis=0, tiled=True)]
  transfers between devices with their start and end apart: 6 -> 1, of which waited for: 5 -> 1; matrix products, arithmetic and copies ran while one was open for 1% -> 2% of each run, Pallas kernels for 0% -> 0%
where the time goes in v1:
time: 129 us; the launch traced here: 128 us
  blocking collectives  68.7 us (53%)
  waiting for transfers between devices  26.6 us (21%)
  local copies, waits for them, and re-layouts  10.8 us (8%)
  other arithmetic  7.71 us (6%)
  starting transfers between devices  7.66 us (6%)
  matrix products  5.88 us (5%)
    all_to_all x2, blocking collectives, exchange(): return lax.all_to_all(x, 'dap', split_axis=0, concat_axis=0, tiled=True)  68.7 us
    all_to_all x1, waiting for transfers between devices, exchange(): return lax.all_to_all(x, 'dap', split_axis=0, concat_axis=0, tiled=True)  26.6 us
    all_to_all x1, starting transfers between devices, exchange(): return lax.all_to_all(x, 'dap', split_axis=0, concat_axis=0, tiled=True)  7.66 us
  transfers between devices with their start and end apart: 1, of which 1 were waited for; matrix products, arithmetic and copies ran while one was open for 2% of the time, Pallas kernels for 0%

profile of v1, /device:TPU:1, one launch (start us, length us, event | category | flops | bytes accessed | tf_op | source)
XLA Modules:
  0.0 128.5 jit_solution(9252124359388174)
XLA Ops:
  0.7 0.7 convert_bitcast_fusion.4
  1.4 0.9 copy.72
  2.3 0.9 reshape.230
  3.2 0.9 reshape.231
  4.0 0.9 fusion.15
  5.2 0.4 pad_maximum_fusion.1
  5.6 33.2 %all_to_all.15 = bf16[128,16,128]{2,1,0:T(8,128)(2,1)S(1)} all-to-all(bf16[128,16,128]{2,1,0:T(8,128)(2,1)S(1)} %pad_maximum_fusion.1), channel_id=1, replica_groups=mesh['dap'=128,'dp'=2] {'dap'}, dimensions={0} | all-to-all | bytes 1048576 | tf_op jit(solution)/shard_map/all_to_all | solution.py:48
  38.9 1.0 convert_reduce_fusion.2
  39.9 1.8 %multiply_reduce_fusion.3 = f32[128]{0:T(128)S(1)} fusion(f32[128]{0:T(128)S(1)} %broadcast_multiply_fusion.2, bf16[128,16,128]{2,1,0:T(8,128)(2,1)S(1)} %all_to_all.15), kind=kLoop, calls=%fused_computation.73 | loop fusion | flops 130944 | bytes 66560 | tf_op jit(solution)/shard_map/reduce_sum | solution.py:20
  43.7 1.0 fusion.52
  50.1 0.6 pad_maximum_fusion
  50.7 35.5 %all_to_all.16 = bf16[128,32,128]{2,1,0:T(8,128)(2,1)S(1)} all-to-all(bf16[128,32,128]{2,1,0:T(8,128)(2,1)S(1)} %pad_maximum_fusion), channel_id=1, replica_groups=mesh['dap'=128,'dp'=2] {'dap'}, dimensions={0} | all-to-all | bytes 2097152 | tf_op jit(solution)/shard_map/all_to_all | solution.py:48
  86.2 0.4 convert_reduce_fusion
  87.4 1.1 broadcast_in_dim.17
  88.5 7.7 %all-to-all-start.2 = ((bf16[128,32,128]{2,1,0:T(8,128)(2,1)}), bf16[128,32,128]{2,1,0:T(8,128)(2,1)S(1)}, u32[]{:S(2)}, u32[]{:S(2)}) async-start(bf16[128,32,128]{2,1,0:T(8,128)(2,1)} %broadcast_in_dim.17), calls=%async_computation.2 | async-start | bytes 2097152 | tf_op jit(solution)/shard_map/all_to_all | solution.py:48
  96.3 0.7 reshape.244
  97.0 0.7 copy.85
  97.8 0.7 reshape.243
  98.4 26.6 %all-to-all-done.2 = bf16[128,32,128]{2,1,0:T(8,128)(2,1)S(1)} async-done(((bf16[128,32,128]{2,1,0:T(8,128)(2,1)}), bf16[128,32,128]{2,1,0:T(8,128)(2,1)S(1)}, u32[]{:S(2)}, u32[]{:S(2)}) %all-to-all-start.2) | async-done | bytes 1048608 | tf_op jit(solution)/shard_map/all_to_all | solution.py:48
  125.2 0.5 slice_bitcast_fusion.7
  125.7 0.6 slice_bitcast_fusion.6
  126.3 0.6 slice_bitcast_fusion.5
  127.0 0.4 reshape.250
  127.4 1.1 slice_bitcast_fusion
  (76 shorter events, 8.6 us)
Async XLA Ops:
  0.6 42.7 %copy-start = (bf16[256,256]{1,0:T(8,128)(2,1)S(1)}, bf16[256,256]{1,0:T(8,128)(2,1)}, u32[]{:S(2)}) copy-start(bf16[256,256]{1,0:T(8,128)(2,1)} %param.21) | copy-start | bytes 393220
  5.2 36.9 %copy-start.5 = (f32[256]{0:T(256)S(1)}, f32[256]{0:T(256)}, u32[]{:S(2)}) copy-start(f32[256]{0:T(256)} %param.15) | copy-start | bytes 3076
  5.6 36.7 %copy-start.1 = (bf16[256,256]{1,0:T(8,128)(2,1)S(1)}, bf16[256,256]{1,0:T(8,128)(2,1)}, u32[]{:S(2)}) copy-start(bf16[256,256]{1,0:T(8,128)(2,1)} %param.18) | copy-start | bytes 393220
  5.6 37.0 %copy-start.3 = (bf16[256,256]{1,0:T(8,128)(2,1)S(1)}, bf16[256,256]{1,0:T(8,128)(2,1)}, u32[]{:S(2)}) copy-start(bf16[256,256]{1,0:T(8,128)(2,1)} %param.17) | copy-start | bytes 393220
  5.6 37.2 %copy-start.2 = (bf16[256,256]{1,0:T(8,128)(2,1)S(1)}, bf16[256,256]{1,0:T(8,128)(2,1)}, u32[]{:S(2)}) copy-start(bf16[256,256]{1,0:T(8,128)(2,1)} %param.19) | copy-start | bytes 393220
  38.9 4.3 %copy-start.4 = (bf16[256,256]{1,0:T(8,128)(2,1)S(1)}, bf16[256,256]{1,0:T(8,128)(2,1)}, u32[]{:S(2)}) copy-start(bf16[256,256]{1,0:T(8,128)(2,1)} %param.20) | copy-start | bytes 393220
  50.7 35.9 %copy-start.6 = (f32[128]{0:T(128)S(1)}, f32[128]{0:T(128)}, u32[]{:S(2)}) copy-start(f32[128]{0:T(128)} %param.16) | copy-start | bytes 1540
  50.7 36.1 %copy-start.7 = (bf16[128,8]{0,1:T(8,128)(2,1)S(1)}, bf16[128,8]{0,1:T(8,128)(2,1)}, u32[]{:S(2)}) copy-start(bf16[128,8]{0,1:T(8,128)(2,1)} %param.22) | copy-start | bytes 6148
  88.5 36.5 %all-to-all-start.2 = ((bf16[128,32,128]{2,1,0:T(8,128)(2,1)}), bf16[128,32,128]{2,1,0:T(8,128)(2,1)S(1)}, u32[]{:S(2)}, u32[]{:S(2)}) async-start(bf16[128,32,128]{2,1,0:T(8,128)(2,1)} %broadcast_in_dim.17), calls=%async_computation.2 | async-start | bytes 2097152 | tf_op jit(solution)/shard_map/all_to_all | solution.py:48

commit v2 on v1

v2 whole, which is shorter than its diff:
```python
import jax
import jax.numpy as jnp
from jax import lax
from jax.experimental import pallas as pl
from jax.experimental.pallas import tpu as pltpu
from jax.sharding import PartitionSpec as P

FEATURES = 256
HEADS = 8
HEAD_DIM = 32
LANES = 128
CORES = 2
CHIPS = 64
N = CORES * CHIPS
SCALE = HEAD_DIM ** (-0.5)
EPS = 1e-05

F32 = jnp.float32
BF16 = jnp.bfloat16

IN_ROWS = 16
PART_ROWS = 40
SUM_ROWS = 32

VMEM = pl.BlockSpec(memory_space=pltpu.VMEM)
SMEM = pl.BlockSpec(memory_space=pltpu.SMEM)


def dot(a, b):
    return jnp.dot(a, b, preferred_element_type=F32)


def dot_nt(a, b):
    return lax.dot_general(a, b, (((1,), (1,)), ((), ())), preferred_element_type=F32)


def dot_tn(a, b):
    return lax.dot_general(a, b, (((0,), (0,)), ((), ())), preferred_element_type=F32)


def layer_norm(value, gain):
    mean = jnp.mean(value, axis=-1, keepdims=True)
    centered = value - mean
    variance = jnp.mean(centered * centered, axis=-1, keepdims=True)
    inv = lax.rsqrt(variance + EPS)
    hat = centered * inv
    return hat, inv, hat * gain


def layer_norm_adjoint(upstream, hat, inv, gain):
    ug = upstream * gain
    return inv * (
        ug
        - jnp.mean(ug, axis=-1, keepdims=True)
        - hat * jnp.mean(ug * hat, axis=-1, keepdims=True)
    )


def split(x):
    high = x.astype(BF16)
    rest = x - high.astype(F32)
    mid = rest.astype(BF16)
    return high, mid, (rest - mid.astype(F32)).astype(BF16)


def by_core(rows):
    return jnp.concatenate(
        [rows[pl.ds(c, CHIPS, stride=CORES), :] for c in range(CORES)], axis=0
    )


def call(kernel, out_shape, scratch, *operands):
    return pl.pallas_call(
        kernel,
        out_shape=out_shape,
        in_specs=[SMEM] + [VMEM] * (len(operands) - 1),
        out_specs=jax.tree.map(lambda _: VMEM, out_shape),
        scratch_shapes=scratch,
    )(*operands)


def entry_kernel(pos, msa, grad, flags, pair, gain, w_bias, out, stage, rows):
    for r, value in enumerate((msa, grad)):
        value = value[...].astype(F32)
        stage[pl.ds(2 * r, N, stride=8), :] = value[:, :LANES]
        stage[pl.ds(2 * r + 1, N, stride=8), :] = value[:, LANES:]
    stage[pl.ds(4, N, stride=8), :] = jnp.broadcast_to(flags[...].astype(F32), (N, LANES))
    for r in range(5, 8):
        stage[pl.ds(r, N, stride=8), :] = jnp.zeros((N, LANES), F32)
    out[:, 0:8, :] = stage[...].reshape(N, 8, LANES).astype(BF16)
    rows[...] = pair[0].astype(F32)
    _, _, scaled = layer_norm(by_core(rows), gain[...])
    bias = dot_nt(w_bias[...], scaled.astype(BF16)).astype(BF16)
    out[:, 8:16, :] = jnp.broadcast_to(bias[None], (N, HEADS, LANES))


def sequence_kernel(
    pos, got, gain_ref, wq_ref, wk_ref, wv_ref, wg_ref, wo_ref, own, other, rows, mine, theirs
):
    first = pos[0] == 0
    rows[...] = got[...].astype(F32).reshape(N * IN_ROWS, LANES)

    def row(r):
        return jnp.concatenate(
            [rows[pl.ds(c * IN_ROWS + r, CHIPS, stride=CORES * IN_ROWS), :] for c in range(CORES)],
            axis=0,
        )

    def halves(value):
        return (
            jnp.where(first, value[:CHIPS], value[CHIPS:]),
            jnp.where(first, value[CHIPS:], value[:CHIPS]),
        )

    gain = gain_ref[...]
    msa = jnp.concatenate([row(0), row(1)], axis=1)
    grad = jnp.concatenate([row(2), row(3)], axis=1).astype(BF16)
    lane = lax.broadcasted_iota(jnp.int32, (8, LANES), 1)
    pick = jnp.where(lane == pos[1], 1.0, 0.0).astype(BF16)
    flags = dot_nt(pick, row(4).astype(BF16))[:1]
    masking = 1e9 * (flags - 1.0)
    hat, inv, scaled = layer_norm(msa, gain)
    x = scaled.astype(BF16)
    wo = wo_ref[...]
    q = (dot(x, wq_ref[...]) * SCALE).astype(BF16)
    k = dot(x, wk_ref[...]).astype(BF16)
    v = dot(x, wv_ref[...]).astype(BF16)
    gate = jax.nn.sigmoid(dot(x, wg_ref[...]))
    dw = dot_nt(grad, wo)
    d_attn = (dw * gate).astype(BF16)
    lane = lax.broadcasted_iota(jnp.int32, (1, LANES), 1)
    q_t = q.T
    da_t = d_attn.T
    attn = []
    d_q = []
    dk_t = []
    dv_t = []
    for g in range(2):
        cols = slice(g * LANES, (g + 1) * LANES)
        qg, kg, vg, dg = q[:, cols], k[:, cols], v[:, cols], d_attn[:, cols]
        attn_g = jnp.zeros((N, LANES), F32)
        dq_g = jnp.zeros((N, LANES), F32)
        for s in range(4):
            h = 4 * g + s
            keep = jnp.where((lane >= s * HEAD_DIM) & (lane < (s + 1) * HEAD_DIM), 1.0, 0.0)
            keep = keep.astype(BF16)
            scores = dot_nt(qg * keep, kg) + row(8 + h) + masking
            e = jnp.exp(scores - jnp.max(scores, axis=-1, keepdims=True))
            p32 = e * (1.0 / jnp.sum(e, axis=-1, keepdims=True))
            p = p32.astype(BF16)
            attn_g += dot(p, vg * keep)
            d_p = dot_nt(dg * keep, vg)
            d_s = p32 * (d_p - jnp.sum(p32 * d_p, axis=-1, keepdims=True))
            a, b = halves(d_s)
            mine[pl.ds(h, CHIPS, stride=HEADS), :] = a
            theirs[pl.ds(h, CHIPS, stride=HEADS), :] = b
            d_sb = d_s.astype(BF16)
            dq_g += dot(d_sb, kg * keep)
            head = slice(h * HEAD_DIM, (h + 1) * HEAD_DIM)
            dk_t.append(dot(q_t[head], d_sb))
            dv_t.append(dot(da_t[head], p))
        attn.append(attn_g)
        d_q.append(dq_g)
    own[:, 8:16, :] = mine[...].reshape(CHIPS, HEADS, LANES)
    other[:, 8:16, :] = theirs[...].reshape(CHIPS, HEADS, LANES).astype(BF16)
    attn = jnp.concatenate(attn, axis=1)
    d_q = (jnp.concatenate(d_q, axis=1) * SCALE).astype(BF16)
    d_k = jnp.concatenate(dk_t, axis=0).astype(BF16).T
    d_v = jnp.concatenate(dv_t, axis=0).astype(BF16).T
    weighted = (gate * attn).astype(BF16)
    update = dot(weighted, wo)
    d_g = (dw * attn * gate * (1.0 - gate)).astype(BF16)
    d_x = (
        dot_nt(d_q, wq_ref[...])
        + dot_nt(d_k, wk_ref[...])
        + dot_nt(d_v, wv_ref[...])
        + dot_nt(d_g, wg_ref[...])
    )
    adjoint = layer_norm_adjoint(d_x, hat, inv, gain)
    zeros = jnp.zeros((CHIPS, LANES), F32)
    for r, value in enumerate(
        (update[:, :LANES], update[:, LANES:], adjoint[:, :LANES], adjoint[:, LANES:])
    ):
        a, b = halves(value)
        mine[pl.ds(r, CHIPS, stride=8), :] = a
        mine[pl.ds(4 + r, CHIPS, stride=8), :] = zeros
        theirs[pl.ds(r, CHIPS, stride=8), :] = zeros
        theirs[pl.ds(4 + r, CHIPS, stride=8), :] = b
    own[:, 0:8, :] = mine[...].reshape(CHIPS, 8, LANES)
    other[:, 0:8, :] = theirs[...].reshape(CHIPS, 8, LANES).astype(BF16)
    x_t = x.T
    w_t = weighted.T
    d_gain = jnp.broadcast_to(jnp.sum(d_x * hat, axis=0, keepdims=True), (LANES, FEATURES)).T
    low = lax.broadcasted_iota(jnp.int32, (1, 8, 1), 1) < 4
    pairs = ((x_t, d_q), (x_t, d_k), (x_t, d_v), (x_t, d_g), (w_t, grad))
    for ref, is_own in ((own, True), (other, False)):
        low_half = first == is_own
        mats = [dot(a, jnp.where(low_half, b[:, :LANES], b[:, LANES:])) for a, b in pairs]
        mats.append(d_gain)
        for t in range(3):
            a = mats[2 * t].reshape(CHIPS // 2, 8, LANES)
            b = mats[2 * t + 1].reshape(CHIPS // 2, 8, LANES)
            even = jnp.where(low, a, pltpu.roll(b, 4, 1)).astype(ref.dtype)
            odd = jnp.where(low, pltpu.roll(a, 4, 1), b).astype(ref.dtype)
            both = jnp.stack([even, odd], axis=1).reshape(CHIPS, 8, LANES)
            ref[:, 16 + 8 * t : 24 + 8 * t, :] = both


def owner_kernel(pos, got, pair, gain_ref, w_ref, couple, out, rows):
    total = jnp.sum(got[:, 8:, :].astype(F32), axis=0)
    d_bias = total[:HEADS]
    gain = gain_ref[...]
    rows[...] = pair[0].astype(F32)
    hat, inv, scaled = layer_norm(by_core(rows), gain)
    pair_ln = scaled.astype(BF16)
    w_bias = w_ref[...]
    d_pln = jnp.zeros((N, LANES), F32)
    head = jnp.zeros((HEADS, LANES), F32)
    for part in reversed(split(d_bias)):
        d_pln += dot_tn(part, w_bias)
        head += dot(part, pair_ln)
    adjoint = layer_norm_adjoint(d_pln, hat, inv, gain)
    for c in range(CORES):
        rows[pl.ds(c, CHIPS, stride=CORES), :] = adjoint[c * CHIPS : (c + 1) * CHIPS]
    couple[0] = rows[...].astype(BF16)
    pair_gain = jnp.sum(d_pln * hat, axis=0, keepdims=True)
    lane = lax.broadcasted_iota(jnp.int32, (4, LANES), 1)
    spot = lax.broadcasted_iota(jnp.int32, (4, LANES), 0) + 4 * pos[2] - LANES * pos[0]
    msa_gain = jnp.sum(jnp.where(lane == spot, total[28:32], 0.0), axis=0, keepdims=True)
    shard = jnp.concatenate(
        [total[8:28], pair_gain, msa_gain, jnp.zeros((2, LANES), F32), head], axis=0
    )
    out[...] = jnp.broadcast_to(shard.astype(BF16)[None], (CHIPS, SUM_ROWS, LANES))


def rows_kernel(pos, got, update, adjoint, stage, rows):
    stage[...] = got[:, 0:8, :].astype(F32).reshape(CHIPS * 8, LANES)
    first = pos[0] == 0
    for index, out in enumerate((update, adjoint)):
        for half in range(2):
            r = 2 * index + half
            same = stage[pl.ds(r, CHIPS, stride=8), :]
            cross = stage[pl.ds(4 + r, CHIPS, stride=8), :]
            rows[pl.ds(0, CHIPS, stride=CORES), :] = jnp.where(first, same, cross)
            rows[pl.ds(1, CHIPS, stride=CORES), :] = jnp.where(first, cross, same)
            out[:, half * LANES : (half + 1) * LANES] = rows[...].astype(BF16)


def final_kernel(pos, mine, theirs, *outs):
    first = pos[0] == 0
    low = lax.broadcasted_iota(jnp.int32, (1, 8, 1), 1) < 4
    weights, (head, msa_gain, pair_gain) = outs[:5], outs[5:]
    tail = [ref[:, 16:32, :].astype(F32) for ref in (mine, theirs)]
    sums = [jnp.sum(t[:, 4:], axis=0) for t in tail]
    head[...] = sums[0][4:12] + sums[1][4:12]
    pair_gain[...] = sums[0][0:1] + sums[1][0:1]
    msa_gain[:, :LANES] = jnp.where(first, sums[0][1:2], sums[1][1:2])
    msa_gain[:, LANES:] = jnp.where(first, sums[1][1:2], sums[0][1:2])
    for t in range(3):
        blocks = []
        for ref in (mine, theirs):
            tile = ref[:, 8 * t : 8 * t + 8, :].astype(F32).reshape(CHIPS // 2, 2, 8, LANES)
            even, odd = tile[:, 0], tile[:, 1]
            a = jnp.where(low, even, pltpu.roll(odd, 4, 1)).reshape(FEATURES, LANES)
            b = jnp.where(low, pltpu.roll(even, 4, 1), odd).reshape(FEATURES, LANES)
            blocks.append((a, b))
        for w in range(2):
            if 2 * t + w < 5:
                same, cross = blocks[0][w], blocks[1][w]
                weights[2 * t + w][:, :LANES] = jnp.where(first, same, cross)
                weights[2 * t + w][:, LANES:] = jnp.where(first, cross, same)


def on_device(msa, flags, pair, gain, pair_gain, wq, wk, wv, wg, wo, w_bias, grad):
    index = lax.axis_index("dap")
    pos = jnp.stack([index % CORES, index, index // CORES]).astype(jnp.int32)
    same_core = [[CORES * m + c for m in range(CHIPS)] for c in range(CORES)]
    partner = [(i, i ^ 1) for i in range(N)]

    def exchange(x, groups=None):
        return lax.all_to_all(
            x, "dap", split_axis=0, concat_axis=0, tiled=True, axis_index_groups=groups
        )

    w_bias = w_bias.T
    gain = gain.reshape(1, FEATURES)
    pair_gain = pair_gain.reshape(1, LANES)
    sent = call(
        entry_kernel,
        jax.ShapeDtypeStruct((N, IN_ROWS, LANES), BF16),
        [pltpu.VMEM((N * 8, LANES), F32), pltpu.VMEM((N, LANES), F32)],
        pos, msa.reshape(N, FEATURES), grad.reshape(N, FEATURES), flags.reshape(1, N),
        pair, pair_gain, w_bias,
    )
    got = exchange(sent)
    part = (CHIPS, PART_ROWS, LANES)
    own, other = call(
        sequence_kernel,
        (jax.ShapeDtypeStruct(part, F32), jax.ShapeDtypeStruct(part, BF16)),
        [pltpu.VMEM((N * IN_ROWS, LANES), F32)] + [pltpu.VMEM((CHIPS * 8, LANES), F32)] * 2,
        pos, got, gain, wq, wk, wv, wg, wo,
    )
    paired = (own + lax.ppermute(other, "dap", partner).astype(F32)).astype(BF16)
    got = exchange(paired, same_core)
    couple, shard = call(
        owner_kernel,
        (
            jax.ShapeDtypeStruct((1, N, LANES), BF16),
            jax.ShapeDtypeStruct((CHIPS, SUM_ROWS, LANES), BF16),
        ),
        [pltpu.VMEM((N, LANES), F32)],
        pos, got, pair, pair_gain, w_bias,
    )
    mine = exchange(shard, same_core)
    row_shape = jax.ShapeDtypeStruct((N, FEATURES), BF16)
    update, adjoint = call(
        rows_kernel,
        (row_shape, row_shape),
        [pltpu.VMEM((CHIPS * 8, LANES), F32), pltpu.VMEM((N, LANES), F32)],
        pos, got,
    )
    theirs = lax.ppermute(mine, "dap", partner)
    square = jax.ShapeDtypeStruct((FEATURES, FEATURES), F32)
    *weights, head, msa_gain, pair_gain = call(
        final_kernel,
        (square,) * 5
        + (
            jax.ShapeDtypeStruct((HEADS, LANES), F32),
            jax.ShapeDtypeStruct((1, FEATURES), F32),
            jax.ShapeDtypeStruct((1, LANES), F32),
        ),
        [],
        pos, mine, theirs,
    )
    return (
        update.reshape(N, 1, FEATURES),
        adjoint.reshape(N, 1, FEATURES),
        couple,
        *weights,
        head.T,
        msa_gain.reshape(FEATURES),
        pair_gain.reshape(LANES),
    )


def solution(mesh):
    rows = P("dp", "dap", None)
    pair = P(("dp", "dap"), None, None)
    in_specs = (rows, P("dp", "dap"), pair) + (P(),) * 8 + (rows,)
    out_specs = (rows, rows, pair) + (P("dp", None),) * 6 + (P("dp"), P("dp"))
    return jax.shard_map(
        on_device, mesh=mesh, in_specs=in_specs, out_specs=out_specs, check_vma=False
    )
```

time: 129 us -> 107 us (0.83)
  waiting for transfers between devices: 26.6 us -> 1.94 us
  Pallas kernels: 0 us -> 16.4 us
  blocking collectives: 68.7 us -> 81.4 us
  local copies, waits for them, and re-layouts: 10.8 us -> 0.79 us
  matrix products: 5.88 us -> 0 us
  other arithmetic: 7.71 us -> 2.07 us
  starting transfers between devices: 7.66 us -> 3.73 us
    all_to_all x1 -> x0, waiting for transfers between devices: 26.6 us -> none  [exchange(): return lax.all_to_all(x, 'dap', split_axis=0, concat_axis=0, tiled=True)]
    pallas_call x0 -> x5, Pallas kernels: none -> 16.4 us  [call(): pl.pallas_call(kernel, out_shape=out_shape, in_specs=[SMEM] + [VMEM] * (l...]
    all_to_all x2 -> x3, blocking collectives: 68.7 us -> 81.4 us  [exchange(): lax.all_to_all(x, 'dap', split_axis=0, concat_axis=0, tiled=True, axis_in...]
    all_to_all x1 -> x0, starting transfers between devices: 7.66 us -> none  [exchange(): return lax.all_to_all(x, 'dap', split_axis=0, concat_axis=0, tiled=True)]
    dot_general x24 -> x0, matrix products: 5.88 us -> none  [the longest x5 1.1 us: dot_nt(): lax.dot_general(a, b, (((1,), (1,)), ((), ())), preferred_element_type=F32)]
    reshape x9 -> x0, local copies, waits for them, and re-layouts: 4.2 us -> none  [the longest x1 0.87 us: on_device(): msa.reshape(n, 2, LANES)]
    reduce_sum x7 -> x0, other arithmetic: 3.75 us -> none  [the longest x2 1.89 us: layer_norm(): variance = jnp.mean(centered * centered, axis=-1, keepdims=True)]
    ppermute x0 -> x2, starting transfers between devices: none -> 3.73 us  [the longest x1 3.32 us: on_device(): theirs = lax.ppermute(mine, 'dap', partner)]
  transfers between devices with their start and end apart: 1 -> 2, of which waited for: 1 -> 1; matrix products, arithmetic and copies ran while one was open for 2% -> 0% of each run, Pallas kernels for 0% -> 2%
where the time goes in v2:
time: 107 us
  blocking collectives  81.4 us (76%)
  Pallas kernels  16.4 us (15%)
  starting transfers between devices  3.73 us (3%)
  other arithmetic  2.07 us (2%)
  waiting for transfers between devices  1.94 us (2%)
    all_to_all x3, blocking collectives, exchange(): lax.all_to_all(x, 'dap', split_axis=0, concat_axis=0, tiled=True, axis_in...  81.4 us
    pallas_call x5, Pallas kernels, call(): pl.pallas_call(kernel, out_shape=out_shape, in_specs=[SMEM] + [VMEM] * (l...  16.4 us
    ppermute x1, starting transfers between devices, on_device(): theirs = lax.ppermute(mine, 'dap', partner)  3.32 us
  transfers between devices with their start and end apart: 2, of which 1 were waited for; matrix products, arithmetic and copies ran while one was open for 0% of the time, Pallas kernels for 2%

profile of v2, /device:TPU:1, one launch (start us, length us, event | category | flops | bytes accessed | tf_op | source)
XLA Modules:
  0.0 107.0 jit_solution(14094451525035696423)
XLA Ops:
  0.7 0.6 pad_add_fusion.pos
  1.3 2.1 %shard_map.203 = bf16[128,16,128]{2,1,0:T(8,128)(2,1)} custom-call(s32[3]{0:T(128)} %pad_add_fusion.pos, bf16[128,256]{1,0:T(8,128)(2,1)} %bitcast.14, bf16[128,256]{1,0:T(8,128)(2,1)} %bitcast.15, s32[1,128]{1,0:T(1,128)} %bitcast.21, bf16[1,128,128]{2,1,0:T(8,128)(2,1)} %pair.3, f32[1,128]{1,0:T(1,128)} %bitcast.18, bf16[8,128]{1,0:T(8,128)(2,1)} %bitcast.16), custom_call_target="tpu_custom_call" | custom-call | tf_op jit(solution)/shard_map/pallas_call | solution.py:73
  3.3 33.4 %all_to_all.15.got = bf16[128,16,128]{2,1,0:T(8,128)(2,1)} all-to-all(bf16[128,16,128]{2,1,0:T(8,128)(2,1)} %shard_map.203), channel_id=1, replica_groups=mesh['dap'=128,'dp'=2] {'dap'}, dimensions={0} | all-to-all | bytes 1048576 | tf_op jit(solution)/shard_map/all_to_all | solution.py:281
  36.7 7.8 %shard_map.204 = (f32[64,40,128]{2,1,0:T(8,128)}, bf16[64,40,128]{2,1,0:T(8,128)(2,1)}) custom-call(s32[3]{0:T(128)} %pad_add_fusion.pos, bf16[128,16,128]{2,1,0:T(8,128)(2,1)} %all_to_all.15.got, f32[1,256]{1,0:T(1,128)} %bitcast.20, bf16[256,256]{1,0:T(8,128)(2,1)} %wq_ref.1, bf16[256,256]{1,0:T(8,128)(2,1)} %wk_ref.1, bf16[256,256]{1,0:T(8,128)(2,1)} %wv_ref.1, ...), custom_call_target="tpu_custom_call" | custom-call | tf_op jit(solution)/shard_map/pallas_call | solution.py:73
  44.6 0.4 collective-permute-start
  45.0 1.9 %collective-permute-done = bf16[64,40,128]{2,1,0:T(8,128)(2,1)S(1)} collective-permute-done((bf16[64,40,128]{2,1,0:T(8,128)(2,1)}, bf16[64,40,128]{2,1,0:T(8,128)(2,1)S(1)}, u32[]{:S(2)}, u32[]{:S(2)}) %collective-permute-start) | collective-permute-done | bytes 655392 | tf_op jit(solution)/shard_map/ppermute | solution.py:303
  46.9 1.5 %add_convert_fusion = bf16[64,40,128]{2,1,0:T(8,128)(2,1)S(1)} fusion(f32[64,40,128]{2,1,0:T(8,128)} %get-tuple-element.25, bf16[64,40,128]{2,1,0:T(8,128)(2,1)S(1)} %collective-permute-done), kind=kLoop, calls=%fused_computation | loop fusion | flops 983040 | bytes 2621440 | tf_op jit(solution)/shard_map/convert_element_type | solution.py:303
  48.4 25.9 %all_to_all.16.got = bf16[64,40,128]{2,1,0:T(8,128)(2,1)} all-to-all(bf16[64,40,128]{2,1,0:T(8,128)(2,1)S(1)} %add_convert_fusion), channel_id=1, replica_groups={{0,4,8,12,16,20,24,28,32,36,40,44,48,52,56,60,64,68,72,76,80,84,88,92,9..., dimensions={0} | all-to-all | bytes 1310720 | tf_op jit(solution)/shard_map/all_to_all | solution.py:281
  74.3 2.3 %shard_map.206 = (bf16[1,128,128]{2,1,0:T(8,128)(2,1)}, bf16[64,32,128]{2,1,0:T(8,128)(2,1)}) custom-call(s32[3]{0:T(128)} %pad_add_fusion.pos, bf16[64,40,128]{2,1,0:T(8,128)(2,1)} %all_to_all.16.got, bf16[1,128,128]{2,1,0:T(8,128)(2,1)} %pair.3, f32[1,128]{1,0:T(1,128)} %bitcast.19, bf16[8,128]{1,0:T(8,128)(2,1)} %bitcast.17), custom_call_target="tpu_custom_call" | custom-call | tf_op jit(solution)/shard_map/pallas_call | solution.py:73
  76.6 22.1 %all_to_all.17.mine = bf16[64,32,128]{2,1,0:T(8,128)(2,1)S(1)} all-to-all(bf16[64,32,128]{2,1,0:T(8,128)(2,1)} %get-tuple-element.30), channel_id=1, replica_groups={{0,4,8,12,16,20,24,28,32,36,40,44,48,52,56,60,64,68,72,76,80,84,88,92,9..., dimensions={0} | all-to-all | bytes 1048576 | tf_op jit(solution)/shard_map/all_to_all | solution.py:281
  98.7 0.0 copy-start
  98.7 3.3 %collective-permute-start.1 = (bf16[64,32,128]{2,1,0:T(8,128)(2,1)S(1)}, bf16[64,32,128]{2,1,0:T(8,128)(2,1)S(1)}, u32[]{:S(2)}, u32[]{:S(2)}) collective-permute-start(bf16[64,32,128]{2,1,0:T(8,128)(2,1)S(1)} %all_to_all.17.mine), channel_id=1, source_target_pairs={{0,2},{2,0},{4,6},{6,4},{8,10},{10,8},{12,14},{14,12},{16,18},{18,... | collective-permute-start | bytes 1572872 | tf_op jit(solution)/shard_map/ppermute | solution.py:322
  102.0 1.8 %shard_map.205 = (bf16[128,256]{1,0:T(8,128)(2,1)}, bf16[128,256]{1,0:T(8,128)(2,1)}) custom-call(s32[3]{0:T(128)} %pad_add_fusion.pos, bf16[64,40,128]{2,1,0:T(8,128)(2,1)} %all_to_all.16.got), custom_call_target="tpu_custom_call" | custom-call | tf_op jit(solution)/shard_map/pallas_call | solution.py:73
  103.8 0.0 collective-permute-done.1.theirs
  103.8 0.0 copy-done
  103.8 0.0 copy-start.1
  103.8 0.8 copy-done.1
  104.6 2.4 %shard_map.207 = (f32[256,256]{1,0:T(8,128)}, f32[256,256]{1,0:T(8,128)}, f32[256,256]{1,0:T(8,128)}, f32[256,256]{1,0:T(8,128)}, f32[256,256]{1,0:T(8,128)}, /*...) custom-call(s32[3]{0:T(128)} %pad_add_fusion.pos, bf16[64,32,128]{2,1,0:T(8,128)(2,1)} %copy-done, ...), custom_call_target="tpu_custom_call" | custom-call | tf_op jit(solution)/shard_map/pallas_call | solution.py:73
Async XLA Ops:
  44.6 2.3 %collective-permute-start = (bf16[64,40,128]{2,1,0:T(8,128)(2,1)}, bf16[64,40,128]{2,1,0:T(8,128)(2,1)S(1)}, u32[]{:S(2)}, u32[]{:S(2)}) collective-permute-start(bf16[64,40,128]{2,1,0:T(8,128)(2,1)} %get-tuple-element.26), channel_id=1, source_target_pairs={{0,2},{2,0},{4,6},{6,4},{8,10},{10,8},{12,14},{14,12},{16,18},{18,... | collective-permute-start | bytes 1966088 | tf_op jit(solution)/shard_map/ppermute | solution.py:303
  98.7 5.2 %copy-start = (bf16[64,32,128]{2,1,0:T(8,128)(2,1)}, bf16[64,32,128]{2,1,0:T(8,128)(2,1)S(1)}, u32[]{:S(2)}) copy-start(bf16[64,32,128]{2,1,0:T(8,128)(2,1)S(1)} %all_to_all.17.mine) | copy-start | bytes 1572868
  98.7 5.2 %collective-permute-start.1 = (bf16[64,32,128]{2,1,0:T(8,128)(2,1)S(1)}, bf16[64,32,128]{2,1,0:T(8,128)(2,1)S(1)}, u32[]{:S(2)}, u32[]{:S(2)}) collective-permute-start(bf16[64,32,128]{2,1,0:T(8,128)(2,1)S(1)} %all_to_all.17.mine), channel_id=1, source_target_pairs={{0,2},{2,0},{4,6},{6,4},{8,10},{10,8},{12,14},{14,12},{16,18},{18,... | collective-permute-start | bytes 1572872 | tf_op jit(solution)/shard_map/ppermute | solution.py:322
  103.8 0.8 copy-start.1

commit v3 on v2

--- a/solution.py
+++ b/solution.py
@@ -18,12 +18,13 @@
 F32 = jnp.float32
 BF16 = jnp.bfloat16
 
-IN_ROWS = 16
+IN_ROWS = 24
 PART_ROWS = 40
 SUM_ROWS = 32
 
 VMEM = pl.BlockSpec(memory_space=pltpu.VMEM)
 SMEM = pl.BlockSpec(memory_space=pltpu.SMEM)
+HBM = pl.BlockSpec(memory_space=pltpu.HBM)
 
 
 def dot(a, b):
@@ -69,42 +70,60 @@
     )
 
 
-def call(kernel, out_shape, scratch, *operands):
+def call(kernel, out_shape, scratch, *operands, first=SMEM, rest=VMEM, mib=12):
     return pl.pallas_call(
         kernel,
         out_shape=out_shape,
-        in_specs=[SMEM] + [VMEM] * (len(operands) - 1),
+        in_specs=[first] + [rest] * (len(operands) - 1),
         out_specs=jax.tree.map(lambda _: VMEM, out_shape),
         scratch_shapes=scratch,
+        compiler_params=pltpu.CompilerParams(vmem_limit_bytes=mib * 1024 * 1024),
     )(*operands)
 
 
-def entry_kernel(pos, msa, grad, flags, pair, gain, w_bias, out, stage, rows):
-    for r, value in enumerate((msa, grad)):
-        value = value[...].astype(F32)
-        stage[pl.ds(2 * r, N, stride=8), :] = value[:, :LANES]
-        stage[pl.ds(2 * r + 1, N, stride=8), :] = value[:, LANES:]
-    stage[pl.ds(4, N, stride=8), :] = jnp.broadcast_to(flags[...].astype(F32), (N, LANES))
-    for r in range(5, 8):
-        stage[pl.ds(r, N, stride=8), :] = jnp.zeros((N, LANES), F32)
-    out[:, 0:8, :] = stage[...].reshape(N, 8, LANES).astype(BF16)
+def entry_kernel(
+    msa_hbm, grad_hbm, flags_hbm, pair_hbm, gain_hbm, w_hbm,
+    out, msa, grad, flags, pair, gain, w_bias, stage, rows, sems
+):
+    refs = (
+        (pair_hbm, pair), (gain_hbm, gain), (w_hbm, w_bias),
+        (msa_hbm, msa), (grad_hbm, grad), (flags_hbm, flags),
+    )
+    copies = [pltpu.make_async_copy(a, b, sems.at[i]) for i, (a, b) in enumerate(refs)]
+    for copy in copies:
+        copy.start()
+    for copy in copies[:3]:
+        copy.wait()
     rows[...] = pair[0].astype(F32)
     _, _, scaled = layer_norm(by_core(rows), gain[...])
     bias = dot_nt(w_bias[...], scaled.astype(BF16)).astype(BF16)
-    out[:, 8:16, :] = jnp.broadcast_to(bias[None], (N, HEADS, LANES))
+    out[:, 8:16, :] = jnp.broadcast_to(bias[None], (CHIPS, HEADS, LANES))
+    for copy in copies[3:]:
+        copy.wait()
+    for r, ref in enumerate((msa, grad)):
+        value = ref[...].astype(F32)
+        stage[pl.ds(2 * r, N, stride=4), :] = value[:, :LANES]
+        stage[pl.ds(2 * r + 1, N, stride=4), :] = value[:, LANES:]
+    out[:, 0:8, :] = stage[...].reshape(CHIPS, 8, LANES).astype(BF16)
+    present = jnp.broadcast_to(flags[...].astype(F32), (8, LANES)).astype(BF16)
+    out[:, 16:24, :] = jnp.broadcast_to(present[None], (CHIPS, 8, LANES))
 
 
 def sequence_kernel(
-    pos, got, gain_ref, wq_ref, wk_ref, wv_ref, wg_ref, wo_ref, own, other, rows, mine, theirs
+    pos, near, far, gain_ref, wq_ref, wk_ref, wv_ref, wg_ref, wo_ref, own, other, rows, mine, theirs
 ):
-    first = pos[0] == 0
-    rows[...] = got[...].astype(F32).reshape(N * IN_ROWS, LANES)
+    core = pos[0]
+    first = core == 0
+    rows[core] = near[...].astype(F32).reshape(CHIPS * IN_ROWS, LANES)
+    rows[1 - core] = far[...].astype(F32).reshape(CHIPS * IN_ROWS, LANES)
 
     def row(r):
         return jnp.concatenate(
-            [rows[pl.ds(c * IN_ROWS + r, CHIPS, stride=CORES * IN_ROWS), :] for c in range(CORES)],
-            axis=0,
+            [rows.at[c][pl.ds(r, CHIPS, stride=IN_ROWS), :] for c in range(CORES)], axis=0
         )
+
+    def line(r):
+        return jnp.where(first, row(r), row(4 + r))
 
     def halves(value):
         return (
@@ -113,11 +132,11 @@
         )
 
     gain = gain_ref[...]
-    msa = jnp.concatenate([row(0), row(1)], axis=1)
-    grad = jnp.concatenate([row(2), row(3)], axis=1).astype(BF16)
+    msa = jnp.concatenate([line(0), line(1)], axis=1)
+    grad = jnp.concatenate([line(2), line(3)], axis=1).astype(BF16)
     lane = lax.broadcasted_iota(jnp.int32, (8, LANES), 1)
     pick = jnp.where(lane == pos[1], 1.0, 0.0).astype(BF16)
-    flags = dot_nt(pick, row(4).astype(BF16))[:1]
+    flags = dot_nt(pick, row(16).astype(BF16))[:1]
     masking = 1e9 * (flags - 1.0)
     hat, inv, scaled = layer_norm(msa, gain)
     x = scaled.astype(BF16)
@@ -277,7 +296,7 @@
     same_core = [[CORES * m + c for m in range(CHIPS)] for c in range(CORES)]
     partner = [(i, i ^ 1) for i in range(N)]
 
-    def exchange(x, groups=None):
+    def exchange(x, groups):
         return lax.all_to_all(
             x, "dap", split_axis=0, concat_axis=0, tiled=True, axis_index_groups=groups
         )
@@ -287,18 +306,30 @@
     pair_gain = pair_gain.reshape(1, LANES)
     sent = call(
         entry_kernel,
-        jax.ShapeDtypeStruct((N, IN_ROWS, LANES), BF16),
-        [pltpu.VMEM((N * 8, LANES), F32), pltpu.VMEM((N, LANES), F32)],
-        pos, msa.reshape(N, FEATURES), grad.reshape(N, FEATURES), flags.reshape(1, N),
+        jax.ShapeDtypeStruct((CHIPS, IN_ROWS, LANES), BF16),
+        [
+            pltpu.VMEM((N, FEATURES), BF16),
+            pltpu.VMEM((N, FEATURES), BF16),
+            pltpu.VMEM((1, N), jnp.int32),
+            pltpu.VMEM((1, N, LANES), BF16),
+            pltpu.VMEM((1, LANES), F32),
+            pltpu.VMEM((HEADS, LANES), BF16),
+            pltpu.VMEM((N * 4, LANES), F32),
+            pltpu.VMEM((N, LANES), F32),
+            pltpu.SemaphoreType.DMA((6,)),
+        ],
+        msa.reshape(N, FEATURES), grad.reshape(N, FEATURES), flags.reshape(1, N),
         pair, pair_gain, w_bias,
-    )
-    got = exchange(sent)
+        first=HBM, rest=HBM, mib=60,
+    )
+    near = exchange(sent, same_core)
+    far = lax.ppermute(near, "dap", partner)
     part = (CHIPS, PART_ROWS, LANES)
     own, other = call(
         sequence_kernel,
         (jax.ShapeDtypeStruct(part, F32), jax.ShapeDtypeStruct(part, BF16)),
-        [pltpu.VMEM((N * IN_ROWS, LANES), F32)] + [pltpu.VMEM((CHIPS * 8, LANES), F32)] * 2,
-        pos, got, gain, wq, wk, wv, wg, wo,
+        [pltpu.VMEM((CORES, CHIPS * IN_ROWS, LANES), F32)] + [pltpu.VMEM((CHIPS * 8, LANES), F32)] * 2,
+        pos, near, far, gain, wq, wk, wv, wg, wo,
     )
     paired = (own + lax.ppermute(other, "dap", partner).astype(F32)).astype(BF16)
     got = exchange(paired, same_core)

time: 107 us -> 97.8 us (0.914)
  blocking collectives: 81.4 us -> 74.4 us
  Pallas kernels: 16.4 us -> 12.4 us
  starting transfers between devices: 3.73 us -> 6.38 us
  other arithmetic: 2.07 us -> 0.24 us
  waiting for transfers between devices: 1.94 us -> 3.26 us
    all_to_all x3, blocking collectives: 81.4 us -> 74.4 us  [exchange(): lax.all_to_all(x, 'dap', split_axis=0, concat_axis=0, tiled=True, axis_in...]
    pallas_call x5, Pallas kernels: 16.4 us -> 12.4 us  [call(): pl.pallas_call(kernel, out_shape=out_shape, in_specs=[first] + [rest] * (...]
    ppermute x0 -> x1, starting transfers between devices: none -> 2.57 us  [on_device(): far = lax.ppermute(near, 'dap', partner)]
    convert_element_type x1, other arithmetic: 1.47 us -> 0.16 us  [on_device(): (own + lax.ppermute(other, 'dap', partner).astype(F32)).astype(BF16)]
    ppermute x0 -> x1, waiting for transfers between devices: none -> 1.27 us  [on_device(): far = lax.ppermute(near, 'dap', partner)]
  transfers between devices with their start and end apart: 2 -> 3, of which waited for: 1 -> 3; matrix products, arithmetic and copies ran while one was open for 0% -> 0% of each run, Pallas kernels for 2% -> 1%
where the time goes in v3:
time: 97.8 us; the launch traced here: 97.5 us
  blocking collectives  74.4 us (76%)
  Pallas kernels  12.4 us (13%)
  starting transfers between devices  6.38 us (7%)
  waiting for transfers between devices  3.26 us (3%)
    all_to_all x3, blocking collectives, exchange(): lax.all_to_all(x, 'dap', split_axis=0, concat_axis=0, tiled=True, axis_in...  74.4 us
    pallas_call x5, Pallas kernels, call(): pl.pallas_call(kernel, out_shape=out_shape, in_specs=[first] + [rest] * (...  12.4 us
    ppermute x1, starting transfers between devices, on_device(): theirs = lax.ppermute(mine, 'dap', partner)  3.34 us
    ppermute x1, starting transfers between devices, on_device(): far = lax.ppermute(near, 'dap', partner)  2.57 us
  transfers between devices with their start and end apart: 3, of which 3 were waited for; matrix products, arithmetic and copies ran while one was open for 0% of the time, Pallas kernels for 1%

profile of v3, /device:TPU:1, one launch (start us, length us, event | category | flops | bytes accessed | tf_op | source)
XLA Modules:
  0.0 97.5 jit_solution(10428059750733810440)
XLA Ops:
  0.6 0.0 copy-start.4
  0.7 0.0 copy-start.3
  0.7 0.0 copy-start.2
  0.7 0.0 copy-start.1
  0.7 0.0 copy-start
  0.7 0.0 copy-start.8
  0.7 2.0 %shard_map.203 = bf16[64,24,128]{2,1,0:T(8,128)(2,1)} custom-call(bf16[128,256]{1,0:T(8,128)(2,1)} %bitcast.19, bf16[128,256]{1,0:T(8,128)(2,1)} %bitcast.20, s32[1,128]{1,0:T(1,128)} %bitcast.21, bf16[1,128,128]{2,1,0:T(8,128)(2,1)} %pair.1, f32[1,128]{1,0:T(1,128)} %bitcast.16, bf16[8,128]{1,0:T(8,128)(2,1)} %bitcast.14), custom_call_target="tpu_custom_call" | custom-call | tf_op jit(solution)/shard_map/pallas_call | solution.py:74
  2.8 28.0 %all_to_all.15.near = bf16[64,24,128]{2,1,0:T(8,128)(2,1)S(1)} all-to-all(bf16[64,24,128]{2,1,0:T(8,128)(2,1)} %shard_map.203), channel_id=1, replica_groups={{0,4,8,12,16,20,24,28,32,36,40,44,48,52,56,60,64,68,72,76,80,84,88,92,9..., dimensions={0} | all-to-all | bytes 786432 | tf_op jit(solution)/shard_map/all_to_all | solution.py:300
  30.8 2.6 %collective-permute-start = (bf16[64,24,128]{2,1,0:T(8,128)(2,1)S(1)}, bf16[64,24,128]{2,1,0:T(8,128)(2,1)S(1)}, u32[]{:S(2)}, u32[]{:S(2)}) collective-permute-start(bf16[64,24,128]{2,1,0:T(8,128)(2,1)S(1)} %all_to_all.15.near), channel_id=1, source_target_pairs={{0,2},{2,0},{4,6},{6,4},{8,10},{10,8},{12,14},{14,12},{16,18},{18,... | collective-permute-start | bytes 1179656 | tf_op jit(solution)/shard_map/ppermute | solution.py:326
  33.3 0.1 pad_add_fusion.pos
  33.4 1.3 %collective-permute-done.far = bf16[64,24,128]{2,1,0:T(8,128)(2,1)S(1)} collective-permute-done((bf16[64,24,128]{2,1,0:T(8,128)(2,1)S(1)}, bf16[64,24,128]{2,1,0:T(8,128)(2,1)S(1)}, u32[]{:S(2)}, u32[]{:S(2)}) %collective-permute-start) | collective-permute-done | bytes 393248 | tf_op jit(solution)/shard_map/ppermute | solution.py:326
  34.7 0.0 copy-done.3
  34.7 5.8 %shard_map.204 = (f32[64,40,128]{2,1,0:T(8,128)S(1)}, bf16[64,40,128]{2,1,0:T(8,128)(2,1)S(1)}) custom-call(s32[3]{0:T(128)S(1)} %pad_add_fusion.pos, bf16[64,24,128]{2,1,0:T(8,128)(2,1)S(1)} %all_to_all.15.near, bf16[64,24,128]{2,1,0:T(8,128)(2,1)S(1)} %collective-permute-done.far, f32[1,256]{1,0:T(1,128)S(1)} %bitcast.18, bf16[256,256]{1,0:T(8,128)(2,1)S(1)} %copy-done, ...), custom_call_target="tpu_custom_call" | custom-call | tf_op jit(solution)/shard_map/pallas_call | solution.py:74
  40.5 0.5 collective-permute-start.1
  41.0 1.7 %collective-permute-done.1 = bf16[64,40,128]{2,1,0:T(8,128)(2,1)S(1)} collective-permute-done((bf16[64,40,128]{2,1,0:T(8,128)(2,1)S(1)}, bf16[64,40,128]{2,1,0:T(8,128)(2,1)S(1)}, u32[]{:S(2)}, u32[]{:S(2)}) %collective-permute-start.1) | collective-permute-done | bytes 655392 | tf_op jit(solution)/shard_map/ppermute | solution.py:334
  42.7 0.2 add_convert_fusion
  42.9 24.6 %all_to_all.16.got = bf16[64,40,128]{2,1,0:T(8,128)(2,1)S(1)} all-to-all(bf16[64,40,128]{2,1,0:T(8,128)(2,1)S(1)} %add_convert_fusion), channel_id=1, replica_groups={{0,4,8,12,16,20,24,28,32,36,40,44,48,52,56,60,64,68,72,76,80,84,88,92,9..., dimensions={0} | all-to-all | bytes 1310720 | tf_op jit(solution)/shard_map/all_to_all | solution.py:300
  67.5 0.0 copy-done.5
  67.5 1.6 %shard_map.206 = (bf16[1,128,128]{2,1,0:T(8,128)(2,1)}, bf16[64,32,128]{2,1,0:T(8,128)(2,1)S(1)}) custom-call(s32[3]{0:T(128)S(1)} %pad_add_fusion.pos, bf16[64,40,128]{2,1,0:T(8,128)(2,1)S(1)} %all_to_all.16.got, bf16[1,128,128]{2,1,0:T(8,128)(2,1)S(1)} %copy-done.5, f32[1,128]{1,0:T(1,128)S(1)} %bitcast.17, bf16[8,128]{1,0:T(8,128)(2,1)S(1)} %bitcast.15), custom_call_target="tpu_custom_call" | custom-call | tf_op jit(solution)/shard_map/pallas_call | solution.py:74
  69.1 21.8 %all_to_all.17.mine = bf16[64,32,128]{2,1,0:T(8,128)(2,1)S(1)} all-to-all(bf16[64,32,128]{2,1,0:T(8,128)(2,1)S(1)} %get-tuple-element.30), channel_id=1, replica_groups={{0,4,8,12,16,20,24,28,32,36,40,44,48,52,56,60,64,68,72,76,80,84,88,92,9..., dimensions={0} | all-to-all | bytes 1048576 | tf_op jit(solution)/shard_map/all_to_all | solution.py:300
  90.9 3.3 %collective-permute-start.2 = (bf16[64,32,128]{2,1,0:T(8,128)(2,1)S(1)}, bf16[64,32,128]{2,1,0:T(8,128)(2,1)S(1)}, u32[]{:S(2)}, u32[]{:S(2)}) collective-permute-start(bf16[64,32,128]{2,1,0:T(8,128)(2,1)S(1)} %all_to_all.17.mine), channel_id=1, source_target_pairs={{0,2},{2,0},{4,6},{6,4},{8,10},{10,8},{12,14},{14,12},{16,18},{18,... | collective-permute-start | bytes 1572872 | tf_op jit(solution)/shard_map/ppermute | solution.py:353
  94.2 1.3 %shard_map.205 = (bf16[128,256]{1,0:T(8,128)(2,1)}, bf16[128,256]{1,0:T(8,128)(2,1)}) custom-call(s32[3]{0:T(128)S(1)} %pad_add_fusion.pos, bf16[64,40,128]{2,1,0:T(8,128)(2,1)S(1)} %all_to_all.16.got), custom_call_target="tpu_custom_call" | custom-call | tf_op jit(solution)/shard_map/pallas_call | solution.py:74
  95.5 0.3 collective-permute-done.2.theirs
  95.8 1.7 %shard_map.207 = (f32[256,256]{1,0:T(8,128)}, f32[256,256]{1,0:T(8,128)}, f32[256,256]{1,0:T(8,128)}, f32[256,256]{1,0:T(8,128)}, f32[256,256]{1,0:T(8,128)}, /*...) custom-call(s32[3]{0:T(128)S(1)} %pad_add_fusion.pos, bf16[64,32,128]{2,1,0:T(8,128)(2,1)S(1)} %all_to_all.17.mine, ...), custom_call_target="tpu_custom_call" | custom-call | tf_op jit(solution)/shard_map/pallas_call | solution.py:74
  (10 shorter events, 0.0 us)
Async XLA Ops:
  0.6 34.0 %copy-start.4 = (bf16[256,256]{1,0:T(8,128)(2,1)S(1)}, bf16[256,256]{1,0:T(8,128)(2,1)}, u32[]{:S(2)}) copy-start(bf16[256,256]{1,0:T(8,128)(2,1)} %wo_ref.1) | copy-start | bytes 393220
  0.7 34.0 %copy-start.3 = (bf16[256,256]{1,0:T(8,128)(2,1)S(1)}, bf16[256,256]{1,0:T(8,128)(2,1)}, u32[]{:S(2)}) copy-start(bf16[256,256]{1,0:T(8,128)(2,1)} %wg_ref.1) | copy-start | bytes 393220
  0.7 34.0 %copy-start.2 = (bf16[256,256]{1,0:T(8,128)(2,1)S(1)}, bf16[256,256]{1,0:T(8,128)(2,1)}, u32[]{:S(2)}) copy-start(bf16[256,256]{1,0:T(8,128)(2,1)} %wv_ref.1) | copy-start | bytes 393220
  0.7 34.0 %copy-start.1 = (bf16[256,256]{1,0:T(8,128)(2,1)S(1)}, bf16[256,256]{1,0:T(8,128)(2,1)}, u32[]{:S(2)}) copy-start(bf16[256,256]{1,0:T(8,128)(2,1)} %wk_ref.1) | copy-start | bytes 393220
  0.7 34.0 %copy-start = (bf16[256,256]{1,0:T(8,128)(2,1)S(1)}, bf16[256,256]{1,0:T(8,128)(2,1)}, u32[]{:S(2)}) copy-start(bf16[256,256]{1,0:T(8,128)(2,1)} %wq_ref.1) | copy-start | bytes 393220
  0.7 34.0 %copy-start.8 = (f32[256]{0:T(256)S(1)}, f32[256]{0:T(256)}, u32[]{:S(2)}) copy-start(f32[256]{0:T(256)} %param.15) | copy-start | bytes 3076
  30.8 3.9 %collective-permute-start = (bf16[64,24,128]{2,1,0:T(8,128)(2,1)S(1)}, bf16[64,24,128]{2,1,0:T(8,128)(2,1)S(1)}, u32[]{:S(2)}, u32[]{:S(2)}) collective-permute-start(bf16[64,24,128]{2,1,0:T(8,128)(2,1)S(1)} %all_to_all.15.near), channel_id=1, source_target_pairs={{0,2},{2,0},{4,6},{6,4},{8,10},{10,8},{12,14},{14,12},{16,18},{18,... | collective-permute-start | bytes 1179656 | tf_op jit(solution)/shard_map/ppermute | solution.py:326
  40.5 2.2 %collective-permute-start.1 = (bf16[64,40,128]{2,1,0:T(8,128)(2,1)S(1)}, bf16[64,40,128]{2,1,0:T(8,128)(2,1)S(1)}, u32[]{:S(2)}, u32[]{:S(2)}) collective-permute-start(bf16[64,40,128]{2,1,0:T(8,128)(2,1)S(1)} %get-tuple-element.26), channel_id=1, source_target_pairs={{0,2},{2,0},{4,6},{6,4},{8,10},{10,8},{12,14},{14,12},{16,18},{18,... | collective-permute-start | bytes 1966088 | tf_op jit(solution)/shard_map/ppermute | solution.py:334
  42.7 24.8 %copy-start.5 = (bf16[1,128,128]{2,1,0:T(8,128)(2,1)S(1)}, bf16[1,128,128]{2,1,0:T(8,128)(2,1)}, u32[]{:S(2)}) copy-start(bf16[1,128,128]{2,1,0:T(8,128)(2,1)} %pair.1) | copy-start | bytes 98308
  42.7 24.8 %copy-start.6 = (bf16[128,8]{0,1:T(8,128)(2,1)S(1)}, bf16[128,8]{0,1:T(8,128)(2,1)}, u32[]{:S(2)}) copy-start(bf16[128,8]{0,1:T(8,128)(2,1)} %param.22) | copy-start | bytes 6148
  42.7 24.8 %copy-start.7 = (f32[128]{0:T(128)S(1)}, f32[128]{0:T(128)}, u32[]{:S(2)}) copy-start(f32[128]{0:T(128)} %param.16) | copy-start | bytes 1540
  90.9 4.9 %collective-permute-start.2 = (bf16[64,32,128]{2,1,0:T(8,128)(2,1)S(1)}, bf16[64,32,128]{2,1,0:T(8,128)(2,1)S(1)}, u32[]{:S(2)}, u32[]{:S(2)}) collective-permute-start(bf16[64,32,128]{2,1,0:T(8,128)(2,1)S(1)} %all_to_all.17.mine), channel_id=1, source_target_pairs={{0,2},{2,0},{4,6},{6,4},{8,10},{10,8},{12,14},{14,12},{16,18},{18,... | collective-permute-start | bytes 1572872 | tf_op jit(solution)/shard_map/ppermute | solution.py:353

commit v4 on v3

--- a/solution.py
+++ b/solution.py
@@ -4,6 +4,7 @@
 from jax.experimental import pallas as pl
 from jax.experimental.pallas import tpu as pltpu
 from jax.sharding import PartitionSpec as P
+
 
 FEATURES = 256
 HEADS = 8
@@ -12,6 +13,7 @@
 CORES = 2
 CHIPS = 64
 N = CORES * CHIPS
+TILES = CHIPS // 2
 SCALE = HEAD_DIM ** (-0.5)
 EPS = 1e-05
 
@@ -110,7 +112,8 @@
 
 
 def sequence_kernel(
-    pos, near, far, gain_ref, wq_ref, wk_ref, wv_ref, wg_ref, wo_ref, own, other, rows, mine, theirs
+    pos, near, far, gain_ref, wq_ref, wk_ref, wv_ref, wg_ref, wo_ref,
+    own, other, rows, mine, theirs, scores_ref, dp_ref, p_ref, ds_ref
 ):
     core = pos[0]
     first = core == 0
@@ -147,43 +150,50 @@
     gate = jax.nn.sigmoid(dot(x, wg_ref[...]))
     dw = dot_nt(grad, wo)
     d_attn = (dw * gate).astype(BF16)
-    lane = lax.broadcasted_iota(jnp.int32, (1, LANES), 1)
-    q_t = q.T
-    da_t = d_attn.T
-    attn = []
-    d_q = []
-    dk_t = []
-    dv_t = []
-    for g in range(2):
-        cols = slice(g * LANES, (g + 1) * LANES)
-        qg, kg, vg, dg = q[:, cols], k[:, cols], v[:, cols], d_attn[:, cols]
-        attn_g = jnp.zeros((N, LANES), F32)
-        dq_g = jnp.zeros((N, LANES), F32)
-        for s in range(4):
+
+    lane = lax.broadcasted_iota(jnp.int32, (1, FEATURES), 1)
+    slot = (lane % LANES) // HEAD_DIM
+    in_slot = [jnp.where(slot == s, 1.0, 0.0).astype(BF16) for s in range(4)]
+    in_half = [jnp.where(lane // LANES == g, 1.0, 0.0).astype(BF16) for g in range(2)]
+
+    def by_half(value):
+        return jnp.concatenate([value * keep for keep in in_half], axis=0)
+
+    def by_slot(value):
+        return jnp.concatenate([value * keep for keep in in_slot], axis=0)
+
+    k_halves, v_halves = by_half(k), by_half(v)
+    scores_ref[...] = dot_nt(by_slot(q), k_halves)
+    dp_ref[...] = dot_nt(by_slot(d_attn), v_halves)
+    for s in range(4):
+        for g in range(2):
             h = 4 * g + s
-            keep = jnp.where((lane >= s * HEAD_DIM) & (lane < (s + 1) * HEAD_DIM), 1.0, 0.0)
-            keep = keep.astype(BF16)
-            scores = dot_nt(qg * keep, kg) + row(8 + h) + masking
+            span = (slice(s * N, (s + 1) * N), slice(g * LANES, (g + 1) * LANES))
+            flat = slice((2 * s + g) * LANES, (2 * s + g + 1) * LANES)
+            scores = scores_ref[span] + row(8 + h) + masking
             e = jnp.exp(scores - jnp.max(scores, axis=-1, keepdims=True))
             p32 = e * (1.0 / jnp.sum(e, axis=-1, keepdims=True))
-            p = p32.astype(BF16)
-            attn_g += dot(p, vg * keep)
-            d_p = dot_nt(dg * keep, vg)
+            p_ref[:, flat] = p32.astype(BF16)
+            d_p = dp_ref[span]
             d_s = p32 * (d_p - jnp.sum(p32 * d_p, axis=-1, keepdims=True))
             a, b = halves(d_s)
             mine[pl.ds(h, CHIPS, stride=HEADS), :] = a
             theirs[pl.ds(h, CHIPS, stride=HEADS), :] = b
-            d_sb = d_s.astype(BF16)
-            dq_g += dot(d_sb, kg * keep)
-            head = slice(h * HEAD_DIM, (h + 1) * HEAD_DIM)
-            dk_t.append(dot(q_t[head], d_sb))
-            dv_t.append(dot(da_t[head], p))
-        attn.append(attn_g)
-        d_q.append(dq_g)
+            ds_ref[:, flat] = d_s.astype(BF16)
     own[:, 8:16, :] = mine[...].reshape(CHIPS, HEADS, LANES)
     other[:, 8:16, :] = theirs[...].reshape(CHIPS, HEADS, LANES).astype(BF16)
-    attn = jnp.concatenate(attn, axis=1)
-    d_q = (jnp.concatenate(d_q, axis=1) * SCALE).astype(BF16)
+    attn = dot(p_ref[...], by_slot(v_halves))
+    d_q = (dot(ds_ref[...], by_slot(k_halves)) * SCALE).astype(BF16)
+    q_t = q.T
+    da_t = d_attn.T
+    dk_t = []
+    dv_t = []
+    for h in range(HEADS):
+        g, s = divmod(h, 4)
+        flat = slice((2 * s + g) * LANES, (2 * s + g + 1) * LANES)
+        head = slice(h * HEAD_DIM, (h + 1) * HEAD_DIM)
+        dk_t.append(dot(q_t[head], ds_ref[:, flat]))
+        dv_t.append(dot(da_t[head], p_ref[:, flat]))
     d_k = jnp.concatenate(dk_t, axis=0).astype(BF16).T
     d_v = jnp.concatenate(dv_t, axis=0).astype(BF16).T
     weighted = (gate * attn).astype(BF16)
@@ -209,20 +219,20 @@
     other[:, 0:8, :] = theirs[...].reshape(CHIPS, 8, LANES).astype(BF16)
     x_t = x.T
     w_t = weighted.T
+    pairs = ((x_t, d_q), (x_t, d_k), (x_t, d_v), (x_t, d_g), (w_t, grad))
+    mats = []
+    for a, b in pairs:
+        turned = jnp.concatenate([b[:, LANES:], b[:, :LANES]], axis=1)
+        mats.append(dot(a, jnp.where(first, b, turned)))
     d_gain = jnp.broadcast_to(jnp.sum(d_x * hat, axis=0, keepdims=True), (LANES, FEATURES)).T
+    d_gain = d_gain.reshape(TILES, 8, LANES)
     low = lax.broadcasted_iota(jnp.int32, (1, 8, 1), 1) < 4
-    pairs = ((x_t, d_q), (x_t, d_k), (x_t, d_v), (x_t, d_g), (w_t, grad))
-    for ref, is_own in ((own, True), (other, False)):
-        low_half = first == is_own
-        mats = [dot(a, jnp.where(low_half, b[:, :LANES], b[:, LANES:])) for a, b in pairs]
-        mats.append(d_gain)
-        for t in range(3):
-            a = mats[2 * t].reshape(CHIPS // 2, 8, LANES)
-            b = mats[2 * t + 1].reshape(CHIPS // 2, 8, LANES)
-            even = jnp.where(low, a, pltpu.roll(b, 4, 1)).astype(ref.dtype)
-            odd = jnp.where(low, pltpu.roll(a, 4, 1), b).astype(ref.dtype)
+    for ref, cols in ((own, slice(0, LANES)), (other, slice(LANES, FEATURES))):
+        tiles = [m[:, cols].reshape(TILES, 8, LANES) for m in mats]
+        last = (jnp.where(low, tiles[4], d_gain), jnp.where(low, d_gain, tiles[4]))
+        for t, (even, odd) in enumerate(((tiles[0], tiles[2]), (tiles[1], tiles[3]), last)):
             both = jnp.stack([even, odd], axis=1).reshape(CHIPS, 8, LANES)
-            ref[:, 16 + 8 * t : 24 + 8 * t, :] = both
+            ref[:, 16 + 8 * t : 24 + 8 * t, :] = both.astype(ref.dtype)
 
 
 def owner_kernel(pos, got, pair, gain_ref, w_ref, couple, out, rows):
@@ -243,12 +253,15 @@
         rows[pl.ds(c, CHIPS, stride=CORES), :] = adjoint[c * CHIPS : (c + 1) * CHIPS]
     couple[0] = rows[...].astype(BF16)
     pair_gain = jnp.sum(d_pln * hat, axis=0, keepdims=True)
-    lane = lax.broadcasted_iota(jnp.int32, (4, LANES), 1)
-    spot = lax.broadcasted_iota(jnp.int32, (4, LANES), 0) + 4 * pos[2] - LANES * pos[0]
-    msa_gain = jnp.sum(jnp.where(lane == spot, total[28:32], 0.0), axis=0, keepdims=True)
-    shard = jnp.concatenate(
-        [total[8:28], pair_gain, msa_gain, jnp.zeros((2, LANES), F32), head], axis=0
-    )
+    even = pos[2] % 2 == 0
+    sub = lax.broadcasted_iota(jnp.int32, (8, LANES), 0)
+    lane = lax.broadcasted_iota(jnp.int32, (8, LANES), 1)
+    channel = sub + 8 * (pos[2] // 2)
+    kept = (sub < 4) == even
+    here = jnp.logical_not(kept) & (lane + LANES * pos[0] == channel)
+    msa_gain = jnp.sum(jnp.where(here, total[24:32], 0.0), axis=0, keepdims=True)
+    sums = jnp.where(sub % 4 == 0, pair_gain, jnp.where(sub % 4 == 1, msa_gain, 0.0))
+    shard = jnp.concatenate([total[8:24], jnp.where(kept, total[24:32], sums), head], axis=0)
     out[...] = jnp.broadcast_to(shard.astype(BF16)[None], (CHIPS, SUM_ROWS, LANES))
 
 
@@ -269,25 +282,27 @@
     first = pos[0] == 0
     low = lax.broadcasted_iota(jnp.int32, (1, 8, 1), 1) < 4
     weights, (head, msa_gain, pair_gain) = outs[:5], outs[5:]
-    tail = [ref[:, 16:32, :].astype(F32) for ref in (mine, theirs)]
-    sums = [jnp.sum(t[:, 4:], axis=0) for t in tail]
-    head[...] = sums[0][4:12] + sums[1][4:12]
+    blocks, sums, heads = [], [], []
+    for ref in (mine, theirs):
+        tiles = [
+            ref[:, 8 * t : 8 * t + 8, :].astype(F32).reshape(TILES, 2, 8, LANES) for t in range(3)
+        ]
+        even, odd = tiles[2][:, 0], tiles[2][:, 1]
+        blocks.append(
+            (tiles[0][:, 0], tiles[1][:, 0], tiles[0][:, 1], tiles[1][:, 1],
+             jnp.where(low, even, odd))
+        )
+        sums.append(jnp.sum(even, axis=0)[4:8] + jnp.sum(odd, axis=0)[0:4])
+        heads.append(jnp.sum(ref[:, 24:32, :].astype(F32), axis=0))
+    head[...] = heads[0] + heads[1]
     pair_gain[...] = sums[0][0:1] + sums[1][0:1]
     msa_gain[:, :LANES] = jnp.where(first, sums[0][1:2], sums[1][1:2])
     msa_gain[:, LANES:] = jnp.where(first, sums[1][1:2], sums[0][1:2])
-    for t in range(3):
-        blocks = []
-        for ref in (mine, theirs):
-            tile = ref[:, 8 * t : 8 * t + 8, :].astype(F32).reshape(CHIPS // 2, 2, 8, LANES)
-            even, odd = tile[:, 0], tile[:, 1]
-            a = jnp.where(low, even, pltpu.roll(odd, 4, 1)).reshape(FEATURES, LANES)
-            b = jnp.where(low, pltpu.roll(even, 4, 1), odd).reshape(FEATURES, LANES)
-            blocks.append((a, b))
-        for w in range(2):
-            if 2 * t + w < 5:
-                same, cross = blocks[0][w], blocks[1][w]
-                weights[2 * t + w][:, :LANES] = jnp.where(first, same, cross)
-                weights[2 * t + w][:, LANES:] = jnp.where(first, cross, same)
+    for out, same, cross in zip(weights, *blocks):
+        same = same.reshape(FEATURES, LANES)
+        cross = cross.reshape(FEATURES, LANES)
+        out[:, :LANES] = jnp.where(first, same, cross)
+        out[:, LANES:] = jnp.where(first, cross, same)
 
 
 def on_device(msa, flags, pair, gain, pair_gain, wq, wk, wv, wg, wo, w_bias, grad):
@@ -328,7 +343,15 @@
     own, other = call(
         sequence_kernel,
         (jax.ShapeDtypeStruct(part, F32), jax.ShapeDtypeStruct(part, BF16)),
-        [pltpu.VMEM((CORES, CHIPS * IN_ROWS, LANES), F32)] + [pltpu.VMEM((CHIPS * 8, LANES), F32)] * 2,
+        [
+            pltpu.VMEM((CORES, CHIPS * IN_ROWS, LANES), F32),
+            pltpu.VMEM((CHIPS * 8, LANES), F32),
+            pltpu.VMEM((CHIPS * 8, LANES), F32),
+            pltpu.VMEM((4 * N, FEATURES), F32),
+            pltpu.VMEM((4 * N, FEATURES), F32),
+            pltpu.VMEM((N, HEADS * LANES), BF16),
+            pltpu.VMEM((N, HEADS * LANES), BF16),
+        ],
         pos, near, far, gain, wq, wk, wv, wg, wo,
     )
     paired = (own + lax.ppermute(other, "dap", partner).astype(F32)).astype(BF16)

time: 97.8 us -> 94.7 us (0.968)
  Pallas kernels: 12.4 us -> 9.29 us
    pallas_call x5, Pallas kernels: 12.4 us -> 9.29 us  [call(): pl.pallas_call(kernel, out_shape=out_shape, in_specs=[first] + [rest] * (...]
where the time goes in v4:
time: 94.7 us; the launch traced here: 94.4 us
  blocking collectives  74.4 us (79%)
  Pallas kernels  9.29 us (10%)
  starting transfers between devices  6.37 us (7%)
  waiting for transfers between devices  3.26 us (3%)
    all_to_all x3, blocking collectives, exchange(): lax.all_to_all(x, 'dap', split_axis=0, concat_axis=0, tiled=True, axis_in...  74.4 us
    pallas_call x5, Pallas kernels, call(): pl.pallas_call(kernel, out_shape=out_shape, in_specs=[first] + [rest] * (...  9.29 us
    ppermute x1, starting transfers between devices, on_device(): theirs = lax.ppermute(mine, 'dap', partner)  3.34 us
    ppermute x1, starting transfers between devices, on_device(): far = lax.ppermute(near, 'dap', partner)  2.57 us
  transfers between devices with their start and end apart: 3, of which 3 were waited for; matrix products, arithmetic and copies ran while one was open for 0% of the time, Pallas kernels for 1%

profile of v4, /device:TPU:1, one launch (start us, length us, event | category | flops | bytes accessed | tf_op | source)
XLA Modules:
  0.0 94.4 jit_solution(10729249550655769390)
XLA Ops:
  0.6 0.0 copy-start.4
  0.7 0.0 copy-start.3
  0.7 0.0 copy-start.2
  0.7 0.0 copy-start.1
  0.7 0.0 copy-start
  0.7 0.0 copy-start.8
  0.7 2.0 %shard_map.203 = bf16[64,24,128]{2,1,0:T(8,128)(2,1)} custom-call(bf16[128,256]{1,0:T(8,128)(2,1)} %bitcast.19, bf16[128,256]{1,0:T(8,128)(2,1)} %bitcast.20, s32[1,128]{1,0:T(1,128)} %bitcast.21, bf16[1,128,128]{2,1,0:T(8,128)(2,1)} %pair.1, f32[1,128]{1,0:T(1,128)} %bitcast.16, bf16[8,128]{1,0:T(8,128)(2,1)} %bitcast.14), custom_call_target="tpu_custom_call" | custom-call | tf_op jit(solution)/shard_map/pallas_call | solution.py:76
  2.8 28.0 %all_to_all.15.near = bf16[64,24,128]{2,1,0:T(8,128)(2,1)S(1)} all-to-all(bf16[64,24,128]{2,1,0:T(8,128)(2,1)} %shard_map.203), channel_id=1, replica_groups={{0,4,8,12,16,20,24,28,32,36,40,44,48,52,56,60,64,68,72,76,80,84,88,92,9..., dimensions={0} | all-to-all | bytes 786432 | tf_op jit(solution)/shard_map/all_to_all | solution.py:315
  30.8 2.6 %collective-permute-start = (bf16[64,24,128]{2,1,0:T(8,128)(2,1)S(1)}, bf16[64,24,128]{2,1,0:T(8,128)(2,1)S(1)}, u32[]{:S(2)}, u32[]{:S(2)}) collective-permute-start(bf16[64,24,128]{2,1,0:T(8,128)(2,1)S(1)} %all_to_all.15.near), channel_id=1, source_target_pairs={{0,2},{2,0},{4,6},{6,4},{8,10},{10,8},{12,14},{14,12},{16,18},{18,... | collective-permute-start | bytes 1179656 | tf_op jit(solution)/shard_map/ppermute | solution.py:341
  33.3 0.1 pad_add_fusion.pos
  33.4 1.3 %collective-permute-done.far = bf16[64,24,128]{2,1,0:T(8,128)(2,1)S(1)} collective-permute-done((bf16[64,24,128]{2,1,0:T(8,128)(2,1)S(1)}, bf16[64,24,128]{2,1,0:T(8,128)(2,1)S(1)}, u32[]{:S(2)}, u32[]{:S(2)}) %collective-permute-start) | collective-permute-done | bytes 393248 | tf_op jit(solution)/shard_map/ppermute | solution.py:341
  34.7 0.0 copy-done.3
  34.7 2.7 %shard_map.204 = (f32[64,40,128]{2,1,0:T(8,128)S(1)}, bf16[64,40,128]{2,1,0:T(8,128)(2,1)S(1)}) custom-call(s32[3]{0:T(128)S(1)} %pad_add_fusion.pos, bf16[64,24,128]{2,1,0:T(8,128)(2,1)S(1)} %all_to_all.15.near, bf16[64,24,128]{2,1,0:T(8,128)(2,1)S(1)} %collective-permute-done.far, f32[1,256]{1,0:T(1,128)S(1)} %bitcast.18, bf16[256,256]{1,0:T(8,128)(2,1)S(1)} %copy-done, ...), custom_call_target="tpu_custom_call" | custom-call | tf_op jit(solution)/shard_map/pallas_call | solution.py:76
  37.4 0.5 collective-permute-start.1
  37.9 1.7 %collective-permute-done.1 = bf16[64,40,128]{2,1,0:T(8,128)(2,1)S(1)} collective-permute-done((bf16[64,40,128]{2,1,0:T(8,128)(2,1)S(1)}, bf16[64,40,128]{2,1,0:T(8,128)(2,1)S(1)}, u32[]{:S(2)}, u32[]{:S(2)}) %collective-permute-start.1) | collective-permute-done | bytes 655392 | tf_op jit(solution)/shard_map/ppermute | solution.py:357
  39.6 0.2 add_convert_fusion
  39.8 24.6 %all_to_all.16.got = bf16[64,40,128]{2,1,0:T(8,128)(2,1)S(1)} all-to-all(bf16[64,40,128]{2,1,0:T(8,128)(2,1)S(1)} %add_convert_fusion), channel_id=1, replica_groups={{0,4,8,12,16,20,24,28,32,36,40,44,48,52,56,60,64,68,72,76,80,84,88,92,9..., dimensions={0} | all-to-all | bytes 1310720 | tf_op jit(solution)/shard_map/all_to_all | solution.py:315
  64.4 0.0 copy-done.6
  64.4 1.6 %shard_map.206 = (bf16[1,128,128]{2,1,0:T(8,128)(2,1)}, bf16[64,32,128]{2,1,0:T(8,128)(2,1)S(1)}) custom-call(s32[3]{0:T(128)S(1)} %pad_add_fusion.pos, bf16[64,40,128]{2,1,0:T(8,128)(2,1)S(1)} %all_to_all.16.got, bf16[1,128,128]{2,1,0:T(8,128)(2,1)S(1)} %copy-done.5, f32[1,128]{1,0:T(1,128)S(1)} %bitcast.17, bf16[8,128]{1,0:T(8,128)(2,1)S(1)} %bitcast.15), custom_call_target="tpu_custom_call" | custom-call | tf_op jit(solution)/shard_map/pallas_call | solution.py:76
  66.0 21.8 %all_to_all.17.mine = bf16[64,32,128]{2,1,0:T(8,128)(2,1)S(1)} all-to-all(bf16[64,32,128]{2,1,0:T(8,128)(2,1)S(1)} %get-tuple-element.30), channel_id=1, replica_groups={{0,4,8,12,16,20,24,28,32,36,40,44,48,52,56,60,64,68,72,76,80,84,88,92,9..., dimensions={0} | all-to-all | bytes 1048576 | tf_op jit(solution)/shard_map/all_to_all | solution.py:315
  87.8 3.3 %collective-permute-start.2 = (bf16[64,32,128]{2,1,0:T(8,128)(2,1)S(1)}, bf16[64,32,128]{2,1,0:T(8,128)(2,1)S(1)}, u32[]{:S(2)}, u32[]{:S(2)}) collective-permute-start(bf16[64,32,128]{2,1,0:T(8,128)(2,1)S(1)} %all_to_all.17.mine), channel_id=1, source_target_pairs={{0,2},{2,0},{4,6},{6,4},{8,10},{10,8},{12,14},{14,12},{16,18},{18,... | collective-permute-start | bytes 1572872 | tf_op jit(solution)/shard_map/ppermute | solution.py:376
  91.2 1.3 %shard_map.205 = (bf16[128,256]{1,0:T(8,128)(2,1)}, bf16[128,256]{1,0:T(8,128)(2,1)}) custom-call(s32[3]{0:T(128)S(1)} %pad_add_fusion.pos, bf16[64,40,128]{2,1,0:T(8,128)(2,1)S(1)} %all_to_all.16.got), custom_call_target="tpu_custom_call" | custom-call | tf_op jit(solution)/shard_map/pallas_call | solution.py:76
  92.4 0.3 collective-permute-done.2.theirs
  92.7 1.7 %shard_map.207 = (f32[256,256]{1,0:T(8,128)}, f32[256,256]{1,0:T(8,128)}, f32[256,256]{1,0:T(8,128)}, f32[256,256]{1,0:T(8,128)}, f32[256,256]{1,0:T(8,128)}, /*...) custom-call(s32[3]{0:T(128)S(1)} %pad_add_fusion.pos, bf16[64,32,128]{2,1,0:T(8,128)(2,1)S(1)} %all_to_all.17.mine, ...), custom_call_target="tpu_custom_call" | custom-call | tf_op jit(solution)/shard_map/pallas_call | solution.py:76
  (10 shorter events, 0.0 us)
Async XLA Ops:
  0.6 34.0 %copy-start.4 = (bf16[256,256]{1,0:T(8,128)(2,1)S(1)}, bf16[256,256]{1,0:T(8,128)(2,1)}, u32[]{:S(2)}) copy-start(bf16[256,256]{1,0:T(8,128)(2,1)} %wo_ref.1) | copy-start | bytes 393220
  0.7 34.0 %copy-start.3 = (bf16[256,256]{1,0:T(8,128)(2,1)S(1)}, bf16[256,256]{1,0:T(8,128)(2,1)}, u32[]{:S(2)}) copy-start(bf16[256,256]{1,0:T(8,128)(2,1)} %wg_ref.1) | copy-start | bytes 393220
  0.7 34.0 %copy-start.2 = (bf16[256,256]{1,0:T(8,128)(2,1)S(1)}, bf16[256,256]{1,0:T(8,128)(2,1)}, u32[]{:S(2)}) copy-start(bf16[256,256]{1,0:T(8,128)(2,1)} %wv_ref.1) | copy-start | bytes 393220
  0.7 34.0 %copy-start.1 = (bf16[256,256]{1,0:T(8,128)(2,1)S(1)}, bf16[256,256]{1,0:T(8,128)(2,1)}, u32[]{:S(2)}) copy-start(bf16[256,256]{1,0:T(8,128)(2,1)} %wk_ref.1) | copy-start | bytes 393220
  0.7 34.0 %copy-start = (bf16[256,256]{1,0:T(8,128)(2,1)S(1)}, bf16[256,256]{1,0:T(8,128)(2,1)}, u32[]{:S(2)}) copy-start(bf16[256,256]{1,0:T(8,128)(2,1)} %wq_ref.1) | copy-start | bytes 393220
  0.7 34.0 %copy-start.8 = (f32[256]{0:T(256)S(1)}, f32[256]{0:T(256)}, u32[]{:S(2)}) copy-start(f32[256]{0:T(256)} %param.15) | copy-start | bytes 3076
  30.8 3.9 %collective-permute-start = (bf16[64,24,128]{2,1,0:T(8,128)(2,1)S(1)}, bf16[64,24,128]{2,1,0:T(8,128)(2,1)S(1)}, u32[]{:S(2)}, u32[]{:S(2)}) collective-permute-start(bf16[64,24,128]{2,1,0:T(8,128)(2,1)S(1)} %all_to_all.15.near), channel_id=1, source_target_pairs={{0,2},{2,0},{4,6},{6,4},{8,10},{10,8},{12,14},{14,12},{16,18},{18,... | collective-permute-start | bytes 1179656 | tf_op jit(solution)/shard_map/ppermute | solution.py:341
  37.4 2.2 %collective-permute-start.1 = (bf16[64,40,128]{2,1,0:T(8,128)(2,1)S(1)}, bf16[64,40,128]{2,1,0:T(8,128)(2,1)S(1)}, u32[]{:S(2)}, u32[]{:S(2)}) collective-permute-start(bf16[64,40,128]{2,1,0:T(8,128)(2,1)S(1)} %get-tuple-element.26), channel_id=1, source_target_pairs={{0,2},{2,0},{4,6},{6,4},{8,10},{10,8},{12,14},{14,12},{16,18},{18,... | collective-permute-start | bytes 1966088 | tf_op jit(solution)/shard_map/ppermute | solution.py:357
  39.6 24.8 %copy-start.5 = (bf16[1,128,128]{2,1,0:T(8,128)(2,1)S(1)}, bf16[1,128,128]{2,1,0:T(8,128)(2,1)}, u32[]{:S(2)}) copy-start(bf16[1,128,128]{2,1,0:T(8,128)(2,1)} %pair.1) | copy-start | bytes 98308
  39.6 24.8 %copy-start.6 = (bf16[128,8]{0,1:T(8,128)(2,1)S(1)}, bf16[128,8]{0,1:T(8,128)(2,1)}, u32[]{:S(2)}) copy-start(bf16[128,8]{0,1:T(8,128)(2,1)} %param.22) | copy-start | bytes 6148
  39.6 24.8 %copy-start.7 = (f32[128]{0:T(128)S(1)}, f32[128]{0:T(128)}, u32[]{:S(2)}) copy-start(f32[128]{0:T(128)} %param.16) | copy-start | bytes 1540
  87.8 4.9 %collective-permute-start.2 = (bf16[64,32,128]{2,1,0:T(8,128)(2,1)S(1)}, bf16[64,32,128]{2,1,0:T(8,128)(2,1)S(1)}, u32[]{:S(2)}, u32[]{:S(2)}) collective-permute-start(bf16[64,32,128]{2,1,0:T(8,128)(2,1)S(1)} %all_to_all.17.mine), channel_id=1, source_target_pairs={{0,2},{2,0},{4,6},{6,4},{8,10},{10,8},{12,14},{14,12},{16,18},{18,... | collective-permute-start | bytes 1572872 | tf_op jit(solution)/shard_map/ppermute | solution.py:376

commit v5 on v4

v5 whole, which is shorter than its diff:
```python
import jax
import jax.numpy as jnp
from jax import lax
from jax.experimental import pallas as pl
from jax.experimental.pallas import tpu as pltpu
from jax.sharding import PartitionSpec as P


FEATURES = 256
HEADS = 8
HEAD_DIM = 32
LANES = 128
CORES = 2
CHIPS = 64
N = CORES * CHIPS
TILES = CHIPS // 2
SCALE = HEAD_DIM ** (-0.5)
EPS = 1e-05

F32 = jnp.float32
BF16 = jnp.bfloat16

IN_ROWS = 18
PART_ROWS = 36
PART_TILES = 9
SUM_ROWS = 32

VMEM = pl.BlockSpec(memory_space=pltpu.VMEM)
SMEM = pl.BlockSpec(memory_space=pltpu.SMEM)
HBM = pl.BlockSpec(memory_space=pltpu.HBM)


def dot(a, b):
    return jnp.dot(a, b, preferred_element_type=F32)


def dot_nt(a, b):
    return lax.dot_general(a, b, (((1,), (1,)), ((), ())), preferred_element_type=F32)


def dot_tn(a, b):
    return lax.dot_general(a, b, (((0,), (0,)), ((), ())), preferred_element_type=F32)


def layer_norm(value, gain):
    mean = jnp.mean(value, axis=-1, keepdims=True)
    centered = value - mean
    variance = jnp.mean(centered * centered, axis=-1, keepdims=True)
    inv = lax.rsqrt(variance + EPS)
    hat = centered * inv
    return hat, inv, hat * gain


def layer_norm_adjoint(upstream, hat, inv, gain):
    ug = upstream * gain
    return inv * (
        ug
        - jnp.mean(ug, axis=-1, keepdims=True)
        - hat * jnp.mean(ug * hat, axis=-1, keepdims=True)
    )


def split(x):
    high = x.astype(BF16)
    rest = x - high.astype(F32)
    mid = rest.astype(BF16)
    return high, mid, (rest - mid.astype(F32)).astype(BF16)


ORDER = [(c, p) for c in range(CORES) for p in range(2)]


def reordered(rows):
    return jnp.concatenate(
        [rows[pl.ds(2 * p + c, TILES, stride=4), :] for c, p in ORDER], axis=0
    )


def restore(rows, value):
    for n, (c, p) in enumerate(ORDER):
        rows[pl.ds(2 * p + c, TILES, stride=4), :] = value[n * TILES : (n + 1) * TILES]


def bias_row(h):
    return 4 + h if h < 5 else 8 + h


def call(
    kernel, out_shape, scratch, *operands, first=SMEM, rest=VMEM, mib=12, far_in=0, far_out=0
):
    out_specs = jax.tree.map(lambda _: VMEM, out_shape)
    if far_out:
        out_specs = (HBM,) * far_out + out_specs[far_out:]
    count = len(operands)
    return pl.pallas_call(
        kernel,
        out_shape=out_shape,
        in_specs=[first] + [rest] * (count - 1 - far_in) + [HBM] * far_in,
        out_specs=out_specs,
        scratch_shapes=scratch,
        input_output_aliases={count - far_in + i: i for i in range(far_in)},
        compiler_params=pltpu.CompilerParams(vmem_limit_bytes=mib * 1024 * 1024),
    )(*operands)


def entry_kernel(
    msa_hbm, grad_hbm, flags_hbm, pair_hbm, gain_hbm, w_hbm,
    out, msa, grad, flags, pair, gain, w_bias, stage, rows, sems
):
    refs = (
        (pair_hbm, pair), (gain_hbm, gain), (w_hbm, w_bias),
        (msa_hbm, msa), (grad_hbm, grad), (flags_hbm, flags),
    )
    copies = [pltpu.make_async_copy(a, b, sems.at[i]) for i, (a, b) in enumerate(refs)]
    for copy in copies:
        copy.start()
    for copy in copies[:3]:
        copy.wait()
    rows[...] = pair[0].astype(F32)
    _, _, scaled = layer_norm(reordered(rows), gain[...])
    bias = dot_nt(w_bias[...], scaled.astype(BF16))
    for copy in copies[3:]:
        copy.wait()
    for r, ref in enumerate((msa, grad)):
        value = ref[...].astype(F32)
        stage[pl.ds(2 * r, N, stride=9), :] = value[:, :LANES]
        stage[pl.ds(2 * r + 1, N, stride=9), :] = value[:, LANES:]
    lines = [(bias_row(h), bias[h : h + 1]) for h in range(HEADS)]
    lines += [(16, flags[...].astype(F32)), (17, jnp.zeros((1, LANES), F32))]
    for r, value in lines:
        stage[pl.ds(r, CHIPS, stride=IN_ROWS), :] = jnp.broadcast_to(value, (CHIPS, LANES))
    out[...] = stage[...].astype(BF16)


def sequence_kernel(
    pos, near, far, gain_ref, wq_ref, wk_ref, wv_ref, wg_ref, wo_ref,
    own, other, gain_out, rows, mine, theirs, scores_ref, dp_ref, p_ref, ds_ref
):
    core = pos[0]
    first = core == 0
    rows[core] = near[...].astype(F32)
    rows[1 - core] = far[...].astype(F32)

    def row(r):
        return jnp.concatenate(
            [
                rows.at[c][pl.ds(r + p * IN_ROWS, TILES, stride=2 * IN_ROWS), :]
                for c, p in ORDER
            ],
            axis=0,
        )

    def line(r):
        return jnp.where(first, row(r), row(9 + r))

    def halves(value):
        return (
            jnp.where(first, value[:CHIPS], value[CHIPS:]),
            jnp.where(first, value[CHIPS:], value[:CHIPS]),
        )

    gain = gain_ref[...]
    msa = jnp.concatenate([line(0), line(1)], axis=1)
    grad = jnp.concatenate([line(2), line(3)], axis=1).astype(BF16)
    lane = lax.broadcasted_iota(jnp.int32, (8, LANES), 1)
    pick = jnp.where(lane == pos[1], 1.0, 0.0).astype(BF16)
    flags = dot_nt(pick, row(16).astype(BF16))[:1]
    masking = 1e9 * (flags - 1.0)
    hat, inv, scaled = layer_norm(msa, gain)
    x = scaled.astype(BF16)
    wo = wo_ref[...]
    q = (dot(x, wq_ref[...]) * SCALE).astype(BF16)
    k = dot(x, wk_ref[...]).astype(BF16)
    v = dot(x, wv_ref[...]).astype(BF16)
    gate = jax.nn.sigmoid(dot(x, wg_ref[...]))
    dw = dot_nt(grad, wo)
    d_attn = (dw * gate).astype(BF16)

    lane = lax.broadcasted_iota(jnp.int32, (1, FEATURES), 1)
    slot = (lane % LANES) // HEAD_DIM
    in_slot = [jnp.where(slot == s, 1.0, 0.0).astype(BF16) for s in range(4)]
    in_half = [jnp.where(lane // LANES == g, 1.0, 0.0).astype(BF16) for g in range(2)]

    def by_half(value):
        return jnp.concatenate([value * keep for keep in in_half], axis=0)

    def by_slot(value):
        return jnp.concatenate([value * keep for keep in in_slot], axis=0)

    def put(even, odd):
        for ref, rows8 in ((own, mine), (other, theirs)):
            value = rows8[...].astype(ref.dtype).reshape(2, TILES, 8, LANES)
            ref[:, even] = value[0]
            ref[:, odd] = value[1]

    k_halves, v_halves = by_half(k), by_half(v)
    scores_ref[...] = dot_nt(by_slot(q), k_halves)
    dp_ref[...] = dot_nt(by_slot(d_attn), v_halves)
    for s in range(4):
        for g in range(2):
            h = 4 * g + s
            span = (slice(s * N, (s + 1) * N), slice(g * LANES, (g + 1) * LANES))
            flat = slice((2 * s + g) * LANES, (2 * s + g + 1) * LANES)
            scores = scores_ref[span] + row(bias_row(h)) + masking
            e = jnp.exp(scores - jnp.max(scores, axis=-1, keepdims=True))
            p32 = e * (1.0 / jnp.sum(e, axis=-1, keepdims=True))
            p_ref[:, flat] = p32.astype(BF16)
            d_p = dp_ref[span]
            d_s = p32 * (d_p - jnp.sum(p32 * d_p, axis=-1, keepdims=True))
            a, b = halves(d_s)
            mine[pl.ds(h, CHIPS, stride=HEADS), :] = a
            theirs[pl.ds(h, CHIPS, stride=HEADS), :] = b
            ds_ref[:, flat] = d_s.astype(BF16)
    put(1, 6)
    attn = dot(p_ref[...], by_slot(v_halves))
    d_q = (dot(ds_ref[...], by_slot(k_halves)) * SCALE).astype(BF16)
    q_t = q.T
    da_t = d_attn.T
    dk_t = []
    dv_t = []
    for h in range(HEADS):
        g, s = divmod(h, 4)
        flat = slice((2 * s + g) * LANES, (2 * s + g + 1) * LANES)
        head = slice(h * HEAD_DIM, (h + 1) * HEAD_DIM)
        dk_t.append(dot(q_t[head], ds_ref[:, flat]))
        dv_t.append(dot(da_t[head], p_ref[:, flat]))
    d_k = jnp.concatenate(dk_t, axis=0).astype(BF16).T
    d_v = jnp.concatenate(dv_t, axis=0).astype(BF16).T
    weighted = (gate * attn).astype(BF16)
    update = dot(weighted, wo)
    d_g = (dw * attn * gate * (1.0 - gate)).astype(BF16)
    d_x = (
        dot_nt(d_q, wq_ref[...])
        + dot_nt(d_k, wk_ref[...])
        + dot_nt(d_v, wv_ref[...])
        + dot_nt(d_g, wg_ref[...])
    )
    adjoint = layer_norm_adjoint(d_x, hat, inv, gain)
    zeros = jnp.zeros((CHIPS, LANES), F32)
    for r, value in enumerate(
        (update[:, :LANES], update[:, LANES:], adjoint[:, :LANES], adjoint[:, LANES:])
    ):
        a, b = halves(value)
        mine[pl.ds(r, CHIPS, stride=8), :] = a
        mine[pl.ds(4 + r, CHIPS, stride=8), :] = zeros
        theirs[pl.ds(r, CHIPS, stride=8), :] = zeros
        theirs[pl.ds(4 + r, CHIPS, stride=8), :] = b
    put(0, 5)
    gain_out[...] = jnp.sum(d_x * hat, axis=0, keepdims=True)
    x_t = x.T
    w_t = weighted.T
    pairs = ((x_t, d_q), (x_t, d_k), (x_t, d_v), (x_t, d_g), (w_t, grad))
    mats = []
    for a, b in pairs:
        turned = jnp.concatenate([b[:, LANES:], b[:, :LANES]], axis=1)
        mats.append(dot(a, jnp.where(first, b, turned)))
    for ref, cols in ((own, slice(0, LANES)), (other, slice(LANES, FEATURES))):
        for tile, m in zip((2, 3, 7, 8, 4), mats):
            ref[:, tile] = m[:, cols].reshape(TILES, 8, LANES).astype(ref.dtype)


def pair_gradient(d_bias, pair, gain, w_bias, rows):
    rows[...] = pair[0].astype(F32)
    hat, inv, scaled = layer_norm(reordered(rows), gain)
    parts = split(d_bias)[::-1]
    d_pln = sum(dot_tn(part, w_bias) for part in parts)
    head = sum(dot(part, scaled.astype(BF16)) for part in parts)
    return hat, inv, d_pln, head


def owner_kernel(pos, got, pair, gain, w_bias, d_gain, out, d_bias_out, rows, sums):
    value = got[...].astype(F32).reshape(TILES, 2 * PART_ROWS, LANES)
    sums[...] = jnp.sum(value, axis=0)
    total = sums[0:PART_ROWS, :] + sums[PART_ROWS:, :]
    sums[0:PART_ROWS, :] = total
    even = pos[2] % 2 == 0
    d_bias = jnp.where(even, sums[8:16, :], sums[12:20, :])
    weights = jnp.where(even, sums[16:32, :], sums[20:36, :])
    fifth = jnp.where(even, sums[32:36, :], sums[0:4, :])
    d_bias_out[...] = d_bias
    hat, _, d_pln, head = pair_gradient(d_bias, pair, gain[...], w_bias[...], rows)
    shard = jnp.concatenate(
        [
            weights,
            fifth,
            jnp.sum(d_pln * hat, axis=0, keepdims=True),
            d_gain[:, :LANES],
            d_gain[:, LANES:],
            jnp.zeros((1, LANES), F32),
            head,
        ],
        axis=0,
    )
    out[...] = jnp.broadcast_to(shard.astype(BF16)[None], (CHIPS, SUM_ROWS, LANES))


def unpack_kernel(pos, got, d_bias, pair, gain_ref, w_bias, update, adjoint, couple, stage, rows):
    stage[...] = got[...].astype(F32)
    first = pos[0] == 0
    even = pos[2] % 2 == 0

    def line(r):
        a, b = (stage[pl.ds(k, CHIPS, stride=PART_ROWS), :] for k in (r, 4 + r))
        return jnp.where(even, a, b)

    for index, out in enumerate((update, adjoint)):
        for half in range(2):
            r = 2 * index + half
            same, cross = line(r), line(4 + r)
            rows[pl.ds(0, CHIPS, stride=CORES), :] = jnp.where(first, same, cross)
            rows[pl.ds(1, CHIPS, stride=CORES), :] = jnp.where(first, cross, same)
            out[:, half * LANES : (half + 1) * LANES] = rows[...].astype(BF16)
    gain = gain_ref[...]
    hat, inv, d_pln, _ = pair_gradient(d_bias[...], pair, gain, w_bias[...], rows)
    restore(rows, layer_norm_adjoint(d_pln, hat, inv, gain))
    couple[0] = rows[...].astype(BF16)


def half_kernel(side, pos, got, sums_ref, weights, stage, sems):
    column = pl.multiple_of(LANES * jnp.bitwise_xor(pos[0], side), LANES)
    low = lax.broadcasted_iota(jnp.int32, (1, 8, 1), 1) < 4

    def tile(t):
        return got[:, 8 * t : 8 * t + 8, :].astype(F32).reshape(TILES, 2, 8, LANES)

    copies = []

    def put(w, value):
        stage[w] = value.reshape(FEATURES, LANES)
        copy = pltpu.make_async_copy(
            stage.at[w], weights[w].at[:, pl.ds(column, LANES)], sems.at[w]
        )
        copy.start()
        copies.append(copy)

    for t in range(2):
        both = tile(t)
        put(t, both[:, 0])
        put(2 + t, both[:, 1])
    last = tile(2)
    put(4, jnp.where(low, last[:, 0], pltpu.roll(last[:, 1], 4, 1)))
    sums_ref[0] = jnp.sum(got[:, 24:32, :].astype(F32), axis=0)
    sums_ref[1] = jnp.sum(got[:, 16:24, :].astype(F32), axis=0)
    for copy in copies:
        copy.wait()


def near_kernel(pos, got, *refs):
    half_kernel(0, pos, got, refs[5], refs[:5], *refs[6:])


def far_kernel(pos, got, near_sums, *refs):
    weights, (head, msa_gain, pair_gain), (sums, stage, sems) = refs[5:10], refs[10:13], refs[13:]
    half_kernel(1, pos, got, sums, weights, stage, sems)
    head[...] = near_sums[0] + sums[0]
    gains = near_sums[1] + sums[1]
    pair_gain[...] = gains[4:5]
    msa_gain[:, :LANES] = gains[5:6]
    msa_gain[:, LANES:] = gains[6:7]


def on_device(msa, flags, pair, gain, pair_gain, wq, wk, wv, wg, wo, w_bias, grad):
    index = lax.axis_index("dap")
    pos = jnp.stack([index % CORES, index, index // CORES]).astype(jnp.int32)
    same_core = [[CORES * m + c for m in range(CHIPS)] for c in range(CORES)]
    partner = [(i, i ^ 1) for i in range(N)]

    def exchange(x, groups):
        return lax.all_to_all(
            x, "dap", split_axis=0, concat_axis=0, tiled=True, axis_index_groups=groups
        )

    w_bias = w_bias.T
    gain = gain.reshape(1, FEATURES)
    pair_gain = pair_gain.reshape(1, LANES)
    sent = call(
        entry_kernel,
        jax.ShapeDtypeStruct((CHIPS * IN_ROWS, LANES), BF16),
        [
            pltpu.VMEM((N, FEATURES), BF16),
            pltpu.VMEM((N, FEATURES), BF16),
            pltpu.VMEM((1, N), jnp.int32),
            pltpu.VMEM((1, N, LANES), BF16),
            pltpu.VMEM((1, LANES), F32),
            pltpu.VMEM((HEADS, LANES), BF16),
            pltpu.VMEM((CHIPS * IN_ROWS, LANES), F32),
            pltpu.VMEM((N, LANES), F32),
            pltpu.SemaphoreType.DMA((6,)),
        ],
        msa.reshape(N, FEATURES), grad.reshape(N, FEATURES), flags.reshape(1, N),
        pair, pair_gain, w_bias,
        first=HBM, rest=HBM, mib=60,
    )
    near = exchange(sent.reshape(CHIPS, IN_ROWS // 2, 2, LANES), same_core)
    near = near.reshape(CHIPS * IN_ROWS, LANES)
    far = lax.ppermute(near, "dap", partner)
    part = (TILES, PART_TILES, 8, LANES)
    own, other, d_gain = call(
        sequence_kernel,
        (
            jax.ShapeDtypeStruct(part, F32),
            jax.ShapeDtypeStruct(part, BF16),
            jax.ShapeDtypeStruct((1, FEATURES), F32),
        ),
        [
            pltpu.VMEM((CORES, CHIPS * IN_ROWS, LANES), F32),
            pltpu.VMEM((CHIPS * 8, LANES), F32),
            pltpu.VMEM((CHIPS * 8, LANES), F32),
            pltpu.VMEM((4 * N, FEATURES), F32),
            pltpu.VMEM((4 * N, FEATURES), F32),
            pltpu.VMEM((N, HEADS * LANES), BF16),
            pltpu.VMEM((N, HEADS * LANES), BF16),
        ],
        pos, near, far, gain, wq, wk, wv, wg, wo,
    )
    paired = (own + lax.ppermute(other, "dap", partner).astype(F32)).astype(BF16)
    got = exchange(paired.reshape(CHIPS, PART_TILES, 4, LANES), same_core)
    got = got.reshape(CHIPS * PART_ROWS, LANES)
    shard, d_bias = call(
        owner_kernel,
        (
            jax.ShapeDtypeStruct((CHIPS, SUM_ROWS, LANES), BF16),
            jax.ShapeDtypeStruct((HEADS, LANES), F32),
        ),
        [pltpu.VMEM((N, LANES), F32), pltpu.VMEM((2 * PART_ROWS, LANES), F32)],
        pos, got, pair, pair_gain, w_bias, d_gain,
    )
    mine = exchange(shard, same_core)
    row_shape = jax.ShapeDtypeStruct((N, FEATURES), BF16)
    update, adjoint, couple = call(
        unpack_kernel,
        (row_shape, row_shape, jax.ShapeDtypeStruct((1, N, LANES), BF16)),
        [pltpu.VMEM((CHIPS * PART_ROWS, LANES), F32), pltpu.VMEM((N, LANES), F32)],
        pos, got, d_bias, pair, pair_gain, w_bias,
    )
    theirs = lax.ppermute(mine, "dap", partner)
    squares = (jax.ShapeDtypeStruct((FEATURES, FEATURES), F32),) * 5
    sums_shape = (2, 8, LANES)
    scratch = [pltpu.VMEM((5, FEATURES, LANES), F32), pltpu.SemaphoreType.DMA((5,))]
    *weights, sums = call(
        near_kernel, squares + (jax.ShapeDtypeStruct(sums_shape, F32),), scratch, pos, mine, far_out=5
    )
    *weights, head, msa_gain, pair_gain = call(
        far_kernel,
        squares
        + (
            jax.ShapeDtypeStruct((HEADS, LANES), F32),
            jax.ShapeDtypeStruct((1, FEATURES), F32),
            jax.ShapeDtypeStruct((1, LANES), F32),
        ),
        [pltpu.VMEM(sums_shape, F32)] + scratch,
        pos, theirs, sums, *weights,
        far_in=5, far_out=5,
    )
    return (
        update.reshape(N, 1, FEATURES),
        adjoint.reshape(N, 1, FEATURES),
        couple,
        *weights,
        head.T,
        msa_gain.reshape(FEATURES),
        pair_gain.reshape(LANES),
    )


def solution(mesh):
    rows = P("dp", "dap", None)
    pair = P(("dp", "dap"), None, None)
    in_specs = (rows, P("dp", "dap"), pair) + (P(),) * 8 + (rows,)
    out_specs = (rows, rows, pair) + (P("dp", None),) * 6 + (P("dp"), P("dp"))
    return jax.shard_map(
        on_device, mesh=mesh, in_specs=in_specs, out_specs=out_specs, check_vma=False
    )
```

time: 94.7 us -> 92.8 us (0.980)
  blocking collectives: 74.4 us -> 71 us
  Pallas kernels: 9.29 us -> 10.6 us
    all_to_all x3, blocking collectives: 74.4 us -> 71 us  [exchange(): lax.all_to_all(x, 'dap', split_axis=0, concat_axis=0, tiled=True, axis_in...]
    pallas_call x5 -> x6, Pallas kernels: 9.29 us -> 10.6 us  [call(): pl.pallas_call(kernel, out_shape=out_shape, in_specs=[first] + [rest] * (...]
  transfers between devices with their start and end apart: 3 -> 3, of which waited for: 3 -> 2; matrix products, arithmetic and copies ran while one was open for 0% -> 0% of each run, Pallas kernels for 1% -> 3%
where the time goes in v5:
time: 92.8 us; the launch traced here: 92.5 us
  blocking collectives  71 us (77%)
  Pallas kernels  10.6 us (11%)
  starting transfers between devices  6.52 us (7%)
  waiting for transfers between devices  2.77 us (3%)
    all_to_all x3, blocking collectives, exchange(): lax.all_to_all(x, 'dap', split_axis=0, concat_axis=0, tiled=True, axis_in...  71 us
    pallas_call x6, Pallas kernels, call(): pl.pallas_call(kernel, out_shape=out_shape, in_specs=[first] + [rest] * (...  10.6 us
    ppermute x1, starting transfers between devices, on_device(): theirs = lax.ppermute(mine, 'dap', partner)  3.21 us
    ppermute x1, starting transfers between devices, on_device(): far = lax.ppermute(near, 'dap', partner)  2.84 us
  transfers between devices with their start and end apart: 3, of which 2 were waited for; matrix products, arithmetic and copies ran while one was open for 0% of the time, Pallas kernels for 3%

profile of v5, /device:TPU:1, one launch (start us, length us, event | category | flops | bytes accessed | tf_op | source)
XLA Modules:
  0.0 92.5 jit_solution(10423415533325530082)
XLA Ops:
  0.7 2.0 %shard_map.203 = bf16[1152,128]{1,0:T(8,128)(2,1)} custom-call(bf16[128,256]{1,0:T(8,128)(2,1)} %bitcast.31, bf16[128,256]{1,0:T(8,128)(2,1)} %bitcast.32, s32[1,128]{1,0:T(1,128)} %bitcast.33, bf16[1,128,128]{2,1,0:T(8,128)(2,1)} %pair.3, f32[1,128]{1,0:T(1,128)} %bitcast.25, bf16[8,128]{1,0:T(8,128)(2,1)} %bitcast.22), custom_call_target="tpu_custom_call" | custom-call | tf_op jit(solution)/shard_map/pallas_call | solution.py:95
  2.7 25.9 %all_to_all.15 = bf16[64,9,2,128]{3,2,1,0:T(2,128)(2,1)S(1)} all-to-all(bf16[64,9,2,128]{3,2,1,0:T(2,128)(2,1)} %bitcast.30), channel_id=1, replica_groups={{0,4,8,12,16,20,24,28,32,36,40,44,48,52,56,60,64,68,72,76,80,84,88,92,9..., dimensions={0} | all-to-all | bytes 589824 | tf_op jit(solution)/shard_map/all_to_all | solution.py:369
  28.6 2.8 %collective-permute-start = (bf16[1152,128]{1,0:T(8,128)(2,1)S(1)}, bf16[1152,128]{1,0:T(8,128)(2,1)S(1)}, u32[]{:S(2)}, u32[]{:S(2)}) collective-permute-start(bf16[1152,128]{1,0:T(8,128)(2,1)S(1)} %bitcast.20), channel_id=1, source_target_pairs={{0,2},{2,0},{4,6},{6,4},{8,10},{10,8},{12,14},{14,12},{16,18},{18,... | collective-permute-start | bytes 884744 | tf_op jit(solution)/shard_map/ppermute | solution.py:396
  31.5 0.1 pad_add_fusion.pos
  31.5 1.1 %collective-permute-done.far = bf16[1152,128]{1,0:T(8,128)(2,1)S(1)} collective-permute-done((bf16[1152,128]{1,0:T(8,128)(2,1)S(1)}, bf16[1152,128]{1,0:T(8,128)(2,1)S(1)}, u32[]{:S(2)}, u32[]{:S(2)}) %collective-permute-start) | collective-permute-done | bytes 294944 | tf_op jit(solution)/shard_map/ppermute | solution.py:396
  32.7 0.0 copy-done.4
  32.7 0.0 copy-done.2
  32.7 0.0 copy-start.8
  32.7 0.7 copy-done.8
  33.4 2.6 %shard_map.204 = (f32[32,9,8,128]{3,2,1,0:T(8,128)S(1)}, bf16[32,9,8,128]{3,2,1,0:T(8,128)(2,1)S(1)}, f32[1,256]{1,0:T(1,128)S(1)}) custom-call(s32[3]{0:T(128)S(1)} %pad_add_fusion.pos, bf16[1152,128]{1,0:T(8,128)(2,1)S(1)} %bitcast.21, bf16[1152,128]{1,0:T(8,128)(2,1)S(1)} %collective-permute-done.far, f32[1,256]{1,0:T(1,128)S(1)} %bitcast.28, ...), custom_call_target="tpu_custom_call" | custom-call | tf_op jit(solution)/shard_map/pallas_call | solution.py:95
  36.0 0.5 collective-permute-start.1
  36.5 1.6 %collective-permute-done.1 = bf16[32,9,8,128]{3,2,1,0:T(8,128)(2,1)S(1)} collective-permute-done((bf16[32,9,8,128]{3,2,1,0:T(8,128)(2,1)S(1)}, bf16[32,9,8,128]{3,2,1,0:T(8,128)(2,1)S(1)}, u32[]{:S(2)}, u32[]{:S(2)}) %collective-permute-start.1) | collective-permute-done | bytes 589856 | tf_op jit(solution)/shard_map/ppermute | solution.py:416
  38.1 0.1 add_convert_fusion
  38.2 0.0 copy-start
  38.3 0.0 copy-start.6
  38.3 0.0 copy-start.7
  38.3 23.0 %all_to_all.16 = bf16[64,9,4,128]{3,2,1,0:T(4,128)(2,1)S(1)} all-to-all(bf16[64,9,4,128]{3,2,1,0:T(4,128)(2,1)S(1)} %bitcast.29), channel_id=1, replica_groups={{0,4,8,12,16,20,24,28,32,36,40,44,48,52,56,60,64,68,72,76,80,84,88,92,9..., dimensions={0} | all-to-all | bytes 1179648 | tf_op jit(solution)/shard_map/all_to_all | solution.py:369
  61.3 0.9 %shard_map.205 = (bf16[64,32,128]{2,1,0:T(8,128)(2,1)S(1)}, f32[8,128]{1,0:T(8,128)S(1)}) custom-call(s32[3]{0:T(128)S(1)} %pad_add_fusion.pos, bf16[2304,128]{1,0:T(8,128)(2,1)S(1)} %bitcast.18, bf16[1,128,128]{2,1,0:T(8,128)(2,1)S(1)} %copy-done, f32[1,128]{1,0:T(1,128)S(1)} %bitcast.26, bf16[8,128]{1,0:T(8,128)(2,1)S(1)} %bitcast.23, ...), custom_call_target="tpu_custom_call" | custom-call | tf_op jit(solution)/shard_map/pallas_call | solution.py:95
  62.2 22.1 %all_to_all.17.got = bf16[64,32,128]{2,1,0:T(8,128)(2,1)S(1)} all-to-all(bf16[64,32,128]{2,1,0:T(8,128)(2,1)S(1)} %get-tuple-element.40), channel_id=1, replica_groups={{0,4,8,12,16,20,24,28,32,36,40,44,48,52,56,60,64,68,72,76,80,84,88,92,9..., dimensions={0} | all-to-all | bytes 1048576 | tf_op jit(solution)/shard_map/all_to_all | solution.py:369
  84.3 3.2 %collective-permute-start.2 = (bf16[64,32,128]{2,1,0:T(8,128)(2,1)S(1)}, bf16[64,32,128]{2,1,0:T(8,128)(2,1)S(1)}, u32[]{:S(2)}, u32[]{:S(2)}) collective-permute-start(bf16[64,32,128]{2,1,0:T(8,128)(2,1)S(1)} %all_to_all.17.got), channel_id=1, source_target_pairs={{0,2},{2,0},{4,6},{6,4},{8,10},{10,8},{12,14},{14,12},{16,18},{18,... | collective-permute-start | bytes 1572872 | tf_op jit(solution)/shard_map/ppermute | solution.py:436
  87.5 1.6 %shard_map.206 = (bf16[128,256]{1,0:T(8,128)(2,1)}, bf16[128,256]{1,0:T(8,128)(2,1)}, bf16[1,128,128]{2,1,0:T(8,128)(2,1)}) custom-call(s32[3]{0:T(128)S(1)} %pad_add_fusion.pos, bf16[2304,128]{1,0:T(8,128)(2,1)S(1)} %bitcast.19, f32[8,128]{1,0:T(8,128)S(1)} %get-tuple-element.36.d_bias, bf16[1,128,128]{2,1,0:T(8,128)(2,1)S(1)} %copy-done, ...), custom_call_target="tpu_custom_call" | custom-call | tf_op jit(solution)/shard_map/pallas_call | solution.py:95
  89.1 1.4 %shard_map.207 = (f32[256,256]{1,0:T(8,128)}, f32[256,256]{1,0:T(8,128)}, f32[256,256]{1,0:T(8,128)}, f32[256,256]{1,0:T(8,128)}, f32[256,256]{1,0:T(8,128)}, /*index=5*/f32[2,8,128]{2,1,0:T(8,128)S(1)}) custom-call(s32[3]{0:T(128)S(1)} %pad_add_fusion.pos, bf16[64,32,128]{2,1,0:T(8,128)(2,1)S(1)} %all_to_all.17.got), custom_call_target="tpu_custom_call" | custom-call | tf_op jit(solution)/shard_map/pallas_call | solution.py:95
  90.5 0.0 collective-permute-done.2.got
  90.5 2.0 %shard_map.208 = (f32[256,256]{1,0:T(8,128)}, f32[256,256]{1,0:T(8,128)}, f32[256,256]{1,0:T(8,128)}, f32[256,256]{1,0:T(8,128)}, f32[256,256]{1,0:T(8,128)}, /*...) custom-call(s32[3]{0:T(128)S(1)} %pad_add_fusion.pos, ...), custom_call_target="tpu_custom_call", output_to_operand_aliasing={{0}: (3, {}), {1}: (4, {}), {2}: (5, {}), {3}: (6, {}), {4}... | custom-call | tf_op jit(solution)/shard_map/pallas_call | solution.py:95
  (11 shorter events, 0.0 us)
Async XLA Ops:
  0.6 32.0 %copy-start.5 = (bf16[256,256]{1,0:T(8,128)(2,1)S(1)}, bf16[256,256]{1,0:T(8,128)(2,1)}, u32[]{:S(2)}) copy-start(bf16[256,256]{1,0:T(8,128)(2,1)} %wo_ref.1) | copy-start | bytes 393220
  0.7 32.0 %copy-start.4 = (bf16[256,256]{1,0:T(8,128)(2,1)S(1)}, bf16[256,256]{1,0:T(8,128)(2,1)}, u32[]{:S(2)}) copy-start(bf16[256,256]{1,0:T(8,128)(2,1)} %wg_ref.1) | copy-start | bytes 393220
  0.7 32.0 %copy-start.3 = (bf16[256,256]{1,0:T(8,128)(2,1)S(1)}, bf16[256,256]{1,0:T(8,128)(2,1)}, u32[]{:S(2)}) copy-start(bf16[256,256]{1,0:T(8,128)(2,1)} %wv_ref.1) | copy-start | bytes 393220
  0.7 32.0 %copy-start.2 = (bf16[256,256]{1,0:T(8,128)(2,1)S(1)}, bf16[256,256]{1,0:T(8,128)(2,1)}, u32[]{:S(2)}) copy-start(bf16[256,256]{1,0:T(8,128)(2,1)} %wk_ref.1) | copy-start | bytes 393220
  0.7 32.0 %copy-start.1 = (bf16[256,256]{1,0:T(8,128)(2,1)S(1)}, bf16[256,256]{1,0:T(8,128)(2,1)}, u32[]{:S(2)}) copy-start(bf16[256,256]{1,0:T(8,128)(2,1)} %wq_ref.1) | copy-start | bytes 393220
  28.6 4.1 %collective-permute-start = (bf16[1152,128]{1,0:T(8,128)(2,1)S(1)}, bf16[1152,128]{1,0:T(8,128)(2,1)S(1)}, u32[]{:S(2)}, u32[]{:S(2)}) collective-permute-start(bf16[1152,128]{1,0:T(8,128)(2,1)S(1)} %bitcast.20), channel_id=1, source_target_pairs={{0,2},{2,0},{4,6},{6,4},{8,10},{10,8},{12,14},{14,12},{16,18},{18,... | collective-permute-start | bytes 884744 | tf_op jit(solution)/shard_map/ppermute | solution.py:396
  32.7 0.7 copy-start.8
  36.0 2.1 %collective-permute-start.1 = (bf16[32,9,8,128]{3,2,1,0:T(8,128)(2,1)S(1)}, bf16[32,9,8,128]{3,2,1,0:T(8,128)(2,1)S(1)}, u32[]{:S(2)}, u32[]{:S(2)}) collective-permute-start(bf16[32,9,8,128]{3,2,1,0:T(8,128)(2,1)S(1)} %get-tuple-element.34), channel_id=1, source_target_pairs={{0,2},{2,0},{4,6},{6,4},{8,10},{10,8},{12,14},{14,12},{16,18},{18,... | collective-permute-start | bytes 1769480 | tf_op jit(solution)/shard_map/ppermute | solution.py:416
  38.2 23.0 %copy-start = (bf16[1,128,128]{2,1,0:T(8,128)(2,1)S(1)}, bf16[1,128,128]{2,1,0:T(8,128)(2,1)}, u32[]{:S(2)}) copy-start(bf16[1,128,128]{2,1,0:T(8,128)(2,1)} %pair.3) | copy-start | bytes 98308
  38.3 23.0 %copy-start.6 = (bf16[128,8]{0,1:T(8,128)(2,1)S(1)}, bf16[128,8]{0,1:T(8,128)(2,1)}, u32[]{:S(2)}) copy-start(bf16[128,8]{0,1:T(8,128)(2,1)} %param.22) | copy-start | bytes 6148
  38.3 23.0 %copy-start.7 = (f32[128]{0:T(128)S(1)}, f32[128]{0:T(128)}, u32[]{:S(2)}) copy-start(f32[128]{0:T(128)} %param.16) | copy-start | bytes 1540
  84.3 6.2 %collective-permute-start.2 = (bf16[64,32,128]{2,1,0:T(8,128)(2,1)S(1)}, bf16[64,32,128]{2,1,0:T(8,128)(2,1)S(1)}, u32[]{:S(2)}, u32[]{:S(2)}) collective-permute-start(bf16[64,32,128]{2,1,0:T(8,128)(2,1)S(1)} %all_to_all.17.got), channel_id=1, source_target_pairs={{0,2},{2,0},{4,6},{6,4},{8,10},{10,8},{12,14},{14,12},{16,18},{18,... | collective-permute-start | bytes 1572872 | tf_op jit(solution)/shard_map/ppermute | solution.py:436

commit v6 on v5

--- a/solution.py
+++ b/solution.py
@@ -24,6 +24,8 @@
 PART_ROWS = 36
 PART_TILES = 9
 SUM_ROWS = 32
+LINE = 8
+LINE_TILES = 22
 
 VMEM = pl.BlockSpec(memory_space=pltpu.VMEM)
 SMEM = pl.BlockSpec(memory_space=pltpu.SMEM)
@@ -85,20 +87,16 @@
     return 4 + h if h < 5 else 8 + h
 
 
-def call(
-    kernel, out_shape, scratch, *operands, first=SMEM, rest=VMEM, mib=12, far_in=0, far_out=0
-):
+def call(kernel, out_shape, scratch, *operands, first=SMEM, rest=VMEM, mib=12, far_out=0):
     out_specs = jax.tree.map(lambda _: VMEM, out_shape)
     if far_out:
         out_specs = (HBM,) * far_out + out_specs[far_out:]
-    count = len(operands)
     return pl.pallas_call(
         kernel,
         out_shape=out_shape,
-        in_specs=[first] + [rest] * (count - 1 - far_in) + [HBM] * far_in,
+        in_specs=[first] + [rest] * (len(operands) - 1),
         out_specs=out_specs,
         scratch_shapes=scratch,
-        input_output_aliases={count - far_in + i: i for i in range(far_in)},
         compiler_params=pltpu.CompilerParams(vmem_limit_bytes=mib * 1024 * 1024),
     )(*operands)
 
@@ -159,7 +157,7 @@
             jnp.where(first, value[CHIPS:], value[:CHIPS]),
         )
 
-    gain = gain_ref[...]
+    gain = gain_ref[0:1, :]
     msa = jnp.concatenate([line(0), line(1)], axis=1)
     grad = jnp.concatenate([line(2), line(3)], axis=1).astype(BF16)
     lane = lax.broadcasted_iota(jnp.int32, (8, LANES), 1)
@@ -291,7 +289,7 @@
         ],
         axis=0,
     )
-    out[...] = jnp.broadcast_to(shard.astype(BF16)[None], (CHIPS, SUM_ROWS, LANES))
+    out[...] = jnp.broadcast_to(shard.astype(BF16)[None], (LINE, SUM_ROWS, LANES))
 
 
 def unpack_kernel(pos, got, d_bias, pair, gain_ref, w_bias, update, adjoint, couple, stage, rows):
@@ -316,53 +314,50 @@
     couple[0] = rows[...].astype(BF16)
 
 
-def half_kernel(side, pos, got, sums_ref, weights, stage, sems):
-    column = pl.multiple_of(LANES * jnp.bitwise_xor(pos[0], side), LANES)
+def line_kernel(pos, got, out):
     low = lax.broadcasted_iota(jnp.int32, (1, 8, 1), 1) < 4
-
-    def tile(t):
-        return got[:, 8 * t : 8 * t + 8, :].astype(F32).reshape(TILES, 2, 8, LANES)
-
+    tiles = got[...].astype(F32).reshape(LINE // 2, 2, 4, 8, LANES)
+    even, odd = tiles[:, 0], tiles[:, 1]
+    fifth = jnp.where(low, even[:, 2], pltpu.roll(odd[:, 2], 4, 1))
+    sums = jnp.sum(tiles[:, :, 2:], axis=(0, 1))
+    weights = (even[:, 0], even[:, 1], fifth, odd[:, 0], odd[:, 1])
+    for w, value in enumerate(weights):
+        value = value.astype(BF16)
+        for t in range(LINE // 2):
+            out[:, 5 * t + w] = jnp.broadcast_to(value[t][None], (LINE, 8, LANES))
+    for n in range(2):
+        out[:, 20 + n] = jnp.broadcast_to(sums[n].astype(BF16)[None], (LINE, 8, LANES))
+
+
+def final_kernel(pos, mine, theirs, *refs):
+    weights, (head, msa_gain, pair_gain), (stage, sems) = refs[:5], refs[5:8], refs[8:]
     copies = []
-
-    def put(w, value):
-        stage[w] = value.reshape(FEATURES, LANES)
-        copy = pltpu.make_async_copy(
-            stage.at[w], weights[w].at[:, pl.ds(column, LANES)], sems.at[w]
-        )
-        copy.start()
-        copies.append(copy)
-
-    for t in range(2):
-        both = tile(t)
-        put(t, both[:, 0])
-        put(2 + t, both[:, 1])
-    last = tile(2)
-    put(4, jnp.where(low, last[:, 0], pltpu.roll(last[:, 1], 4, 1)))
-    sums_ref[0] = jnp.sum(got[:, 24:32, :].astype(F32), axis=0)
-    sums_ref[1] = jnp.sum(got[:, 16:24, :].astype(F32), axis=0)
+    sums = jnp.zeros((2, 8, LANES), F32)
+    for side, got in enumerate((mine, theirs)):
+        column = pl.multiple_of(LANES * jnp.bitwise_xor(pos[0], side), LANES)
+        for n, w in enumerate((0, 1, 4, 2, 3)):
+            value = jnp.stack([got[:, 5 * t + n] for t in range(LINE // 2)], axis=1)
+            stage[side, w] = value.astype(F32).reshape(FEATURES, LANES)
+            copy = pltpu.make_async_copy(
+                stage.at[side, w], weights[w].at[:, pl.ds(column, LANES)], sems.at[side, w]
+            )
+            copy.start()
+            copies.append(copy)
+        sums += jnp.sum(got[:, 20:].astype(F32), axis=0)
+    head[...] = sums[1]
+    pair_gain[...] = sums[0, 4:5]
+    msa_gain[:, :LANES] = sums[0, 5:6]
+    msa_gain[:, LANES:] = sums[0, 6:7]
     for copy in copies:
         copy.wait()
-
-
-def near_kernel(pos, got, *refs):
-    half_kernel(0, pos, got, refs[5], refs[:5], *refs[6:])
-
-
-def far_kernel(pos, got, near_sums, *refs):
-    weights, (head, msa_gain, pair_gain), (sums, stage, sems) = refs[5:10], refs[10:13], refs[13:]
-    half_kernel(1, pos, got, sums, weights, stage, sems)
-    head[...] = near_sums[0] + sums[0]
-    gains = near_sums[1] + sums[1]
-    pair_gain[...] = gains[4:5]
-    msa_gain[:, :LANES] = gains[5:6]
-    msa_gain[:, LANES:] = gains[6:7]
 
 
 def on_device(msa, flags, pair, gain, pair_gain, wq, wk, wv, wg, wo, w_bias, grad):
     index = lax.axis_index("dap")
     pos = jnp.stack([index % CORES, index, index // CORES]).astype(jnp.int32)
     same_core = [[CORES * m + c for m in range(CHIPS)] for c in range(CORES)]
+    along_z = [[g[LINE * q + z] for z in range(LINE)] for g in same_core for q in range(LINE)]
+    across = [[g[LINE * q + z] for q in range(LINE)] for g in same_core for z in range(LINE)]
     partner = [(i, i ^ 1) for i in range(N)]
 
     def exchange(x, groups):
@@ -371,7 +366,7 @@
         )
 
     w_bias = w_bias.T
-    gain = gain.reshape(1, FEATURES)
+    gain = jnp.broadcast_to(gain.reshape(1, FEATURES), (8, FEATURES))
     pair_gain = pair_gain.reshape(1, LANES)
     sent = call(
         entry_kernel,
@@ -419,13 +414,19 @@
     shard, d_bias = call(
         owner_kernel,
         (
-            jax.ShapeDtypeStruct((CHIPS, SUM_ROWS, LANES), BF16),
+            jax.ShapeDtypeStruct((LINE, SUM_ROWS, LANES), BF16),
             jax.ShapeDtypeStruct((HEADS, LANES), F32),
         ),
         [pltpu.VMEM((N, LANES), F32), pltpu.VMEM((2 * PART_ROWS, LANES), F32)],
         pos, got, pair, pair_gain, w_bias, d_gain,
     )
-    mine = exchange(shard, same_core)
+    line = call(
+        line_kernel,
+        jax.ShapeDtypeStruct((LINE, LINE_TILES, 8, LANES), BF16),
+        [],
+        pos, exchange(shard, along_z),
+    )
+    mine = exchange(line, across)
     row_shape = jax.ShapeDtypeStruct((N, FEATURES), BF16)
     update, adjoint, couple = call(
         unpack_kernel,
@@ -434,23 +435,17 @@
         pos, got, d_bias, pair, pair_gain, w_bias,
     )
     theirs = lax.ppermute(mine, "dap", partner)
-    squares = (jax.ShapeDtypeStruct((FEATURES, FEATURES), F32),) * 5
-    sums_shape = (2, 8, LANES)
-    scratch = [pltpu.VMEM((5, FEATURES, LANES), F32), pltpu.SemaphoreType.DMA((5,))]
-    *weights, sums = call(
-        near_kernel, squares + (jax.ShapeDtypeStruct(sums_shape, F32),), scratch, pos, mine, far_out=5
-    )
     *weights, head, msa_gain, pair_gain = call(
-        far_kernel,
-        squares
+        final_kernel,
+        (jax.ShapeDtypeStruct((FEATURES, FEATURES), F32),) * 5
         + (
             jax.ShapeDtypeStruct((HEADS, LANES), F32),
             jax.ShapeDtypeStruct((1, FEATURES), F32),
             jax.ShapeDtypeStruct((1, LANES), F32),
         ),
-        [pltpu.VMEM(sums_shape, F32)] + scratch,
-        pos, theirs, sums, *weights,
-        far_in=5, far_out=5,
+        [pltpu.VMEM((CORES, 5, FEATURES, LANES), F32), pltpu.SemaphoreType.DMA((CORES, 5))],
+        pos, mine, theirs,
+        far_out=5,
     )
     return (
         update.reshape(N, 1, FEATURES),

time: 92.8 us -> 91.2 us (0.983)
  blocking collectives: 71 us -> 69.1 us
    all_to_all x3 -> x4, blocking collectives: 71 us -> 69.1 us  [exchange(): lax.all_to_all(x, 'dap', split_axis=0, concat_axis=0, tiled=True, axis_in...]
  transfers between devices with their start and end apart: 3 -> 3, of which waited for: 2 -> 2; matrix products, arithmetic and copies ran while one was open for 0% -> 0% of each run, Pallas kernels for 3% -> 2%
where the time goes in v6:
time: 91.2 us; the launch traced here: 90.8 us
  blocking collectives  69.1 us (76%)
  Pallas kernels  9.93 us (11%)
  starting transfers between devices  7.33 us (8%)
  waiting for transfers between devices  2.77 us (3%)
    all_to_all x4, blocking collectives, exchange(): lax.all_to_all(x, 'dap', split_axis=0, concat_axis=0, tiled=True, axis_in...  69.1 us
    pallas_call x6, Pallas kernels, call(): pl.pallas_call(kernel, out_shape=out_shape, in_specs=[first] + [rest] * (...  9.93 us
    ppermute x1, starting transfers between devices, on_device(): theirs = lax.ppermute(mine, 'dap', partner)  4.03 us
    ppermute x1, starting transfers between devices, on_device(): far = lax.ppermute(near, 'dap', partner)  2.84 us
  transfers between devices with their start and end apart: 3, of which 2 were waited for; matrix products, arithmetic and copies ran while one was open for 0% of the time, Pallas kernels for 2%

profile of v6, /device:TPU:1, one launch (start us, length us, event | category | flops | bytes accessed | tf_op | source)
XLA Modules:
  0.0 90.8 jit_solution(4912264040240945905)
XLA Ops:
  0.6 0.0 copy-start.5
  0.7 0.0 copy-start.4
  0.7 2.0 %shard_map.203 = bf16[1152,128]{1,0:T(8,128)(2,1)} custom-call(bf16[128,256]{1,0:T(8,128)(2,1)} %bitcast.29, bf16[128,256]{1,0:T(8,128)(2,1)} %bitcast.30, s32[1,128]{1,0:T(1,128)} %bitcast.31, bf16[1,128,128]{2,1,0:T(8,128)(2,1)} %pair.3, f32[1,128]{1,0:T(1,128)} %bitcast.24, bf16[8,128]{1,0:T(8,128)(2,1)} %bitcast.21), custom_call_target="tpu_custom_call" | custom-call | tf_op jit(solution)/shard_map/pallas_call | solution.py:94
  2.7 25.9 %all_to_all.20 = bf16[64,9,2,128]{3,2,1,0:T(2,128)(2,1)S(1)} all-to-all(bf16[64,9,2,128]{3,2,1,0:T(2,128)(2,1)} %bitcast.28), channel_id=1, replica_groups={{0,4,8,12,16,20,24,28,32,36,40,44,48,52,56,60,64,68,72,76,80,84,88,92,9..., dimensions={0} | all-to-all | bytes 589824 | tf_op jit(solution)/shard_map/all_to_all | solution.py:364
  28.6 2.8 %collective-permute-start = (bf16[1152,128]{1,0:T(8,128)(2,1)S(1)}, bf16[1152,128]{1,0:T(8,128)(2,1)S(1)}, u32[]{:S(2)}, u32[]{:S(2)}) collective-permute-start(bf16[1152,128]{1,0:T(8,128)(2,1)S(1)} %bitcast.19), channel_id=1, source_target_pairs={{0,2},{2,0},{4,6},{6,4},{8,10},{10,8},{12,14},{14,12},{16,18},{18,... | collective-permute-start | bytes 884744 | tf_op jit(solution)/shard_map/ppermute | solution.py:391
  31.5 0.1 pad_add_fusion.pos
  31.5 1.1 %collective-permute-done.far = bf16[1152,128]{1,0:T(8,128)(2,1)S(1)} collective-permute-done((bf16[1152,128]{1,0:T(8,128)(2,1)S(1)}, bf16[1152,128]{1,0:T(8,128)(2,1)S(1)}, u32[]{:S(2)}, u32[]{:S(2)}) %collective-permute-start) | collective-permute-done | bytes 294944 | tf_op jit(solution)/shard_map/ppermute | solution.py:391
  32.7 0.7 broadcast_in_dim.2.gain_ref
  33.4 2.6 %shard_map.204 = (f32[32,9,8,128]{3,2,1,0:T(8,128)S(1)}, bf16[32,9,8,128]{3,2,1,0:T(8,128)(2,1)S(1)}, f32[1,256]{1,0:T(1,128)S(1)}) custom-call(s32[3]{0:T(128)S(1)} %pad_add_fusion.pos, bf16[1152,128]{1,0:T(8,128)(2,1)S(1)} %bitcast.20, bf16[1152,128]{1,0:T(8,128)(2,1)S(1)} %collective-permute-done.far, f32[8,256]{1,0:T(8,128)S(1)} %broadcast_in_dim.2.gain_ref, ...), custom_call_target="tpu_custom_call" | custom-call | tf_op jit(solution)/shard_map/pallas_call | solution.py:94
  36.0 0.5 collective-permute-start.1
  36.5 1.6 %collective-permute-done.1 = bf16[32,9,8,128]{3,2,1,0:T(8,128)(2,1)S(1)} collective-permute-done((bf16[32,9,8,128]{3,2,1,0:T(8,128)(2,1)S(1)}, bf16[32,9,8,128]{3,2,1,0:T(8,128)(2,1)S(1)}, u32[]{:S(2)}, u32[]{:S(2)}) %collective-permute-start.1) | collective-permute-done | bytes 589856 | tf_op jit(solution)/shard_map/ppermute | solution.py:411
  38.1 0.1 add_convert_fusion
  38.2 0.0 copy-start
  38.2 0.0 copy-start.6
  38.3 0.0 copy-start.7
  38.3 23.0 %all_to_all.21 = bf16[64,9,4,128]{3,2,1,0:T(4,128)(2,1)S(1)} all-to-all(bf16[64,9,4,128]{3,2,1,0:T(4,128)(2,1)S(1)} %bitcast.27), channel_id=1, replica_groups={{0,4,8,12,16,20,24,28,32,36,40,44,48,52,56,60,64,68,72,76,80,84,88,92,9..., dimensions={0} | all-to-all | bytes 1179648 | tf_op jit(solution)/shard_map/all_to_all | solution.py:364
  61.3 0.9 %shard_map.205 = (bf16[8,32,128]{2,1,0:T(8,128)(2,1)S(1)}, f32[8,128]{1,0:T(8,128)S(1)}) custom-call(s32[3]{0:T(128)S(1)} %pad_add_fusion.pos, bf16[2304,128]{1,0:T(8,128)(2,1)S(1)} %bitcast.17, bf16[1,128,128]{2,1,0:T(8,128)(2,1)S(1)} %copy-done, f32[1,128]{1,0:T(1,128)S(1)} %bitcast.25, bf16[8,128]{1,0:T(8,128)(2,1)S(1)} %bitcast.22, ...), custom_call_target="tpu_custom_call" | custom-call | tf_op jit(solution)/shard_map/pallas_call | solution.py:94
  62.2 11.1 %all_to_all.22.got = bf16[8,32,128]{2,1,0:T(8,128)(2,1)S(1)} all-to-all(bf16[8,32,128]{2,1,0:T(8,128)(2,1)S(1)} %get-tuple-element.34), channel_id=1, replica_groups={{0,4,8,12,16,20,24,28},{32,36,40,44,48,52,56,60},{64,68,72,76,80,84,88,..., dimensions={0} | all-to-all | bytes 131072 | tf_op jit(solution)/shard_map/all_to_all | solution.py:364
  73.3 0.6 shard_map.207
  73.9 9.1 %all_to_all.23.mine = bf16[8,22,8,128]{3,2,1,0:T(8,128)(2,1)S(1)} all-to-all(bf16[8,22,8,128]{3,2,1,0:T(8,128)(2,1)S(1)} %shard_map.207), channel_id=1, replica_groups={{0,32,64,96,128,160,192,224},{4,36,68,100,132,164,196,228},{8,40,72,104..., dimensions={0} | all-to-all | bytes 720896 | tf_op jit(solution)/shard_map/all_to_all | solution.py:364
  83.0 4.0 %collective-permute-start.2 = (bf16[8,22,8,128]{3,2,1,0:T(8,128)(2,1)S(1)}, bf16[8,22,8,128]{3,2,1,0:T(8,128)(2,1)S(1)}, u32[]{:S(2)}, u32[]{:S(2)}) collective-permute-start(bf16[8,22,8,128]{3,2,1,0:T(8,128)(2,1)S(1)} %all_to_all.23.mine), channel_id=1, source_target_pairs={{0,2},{2,0},{4,6},{6,4},{8,10},{10,8},{12,14},{14,12},{16,18},{18,... | collective-permute-start | bytes 1081352 | tf_op jit(solution)/shard_map/ppermute | solution.py:437
  87.0 1.6 %shard_map.206 = (bf16[128,256]{1,0:T(8,128)(2,1)}, bf16[128,256]{1,0:T(8,128)(2,1)}, bf16[1,128,128]{2,1,0:T(8,128)(2,1)}) custom-call(s32[3]{0:T(128)S(1)} %pad_add_fusion.pos, bf16[2304,128]{1,0:T(8,128)(2,1)S(1)} %bitcast.18, f32[8,128]{1,0:T(8,128)S(1)} %get-tuple-element.30.d_bias, bf16[1,128,128]{2,1,0:T(8,128)(2,1)S(1)} %copy-done, ...), custom_call_target="tpu_custom_call" | custom-call | tf_op jit(solution)/shard_map/pallas_call | solution.py:94
  88.6 0.0 collective-permute-done.2.theirs
  88.6 2.3 %shard_map.208 = (f32[256,256]{1,0:T(8,128)}, f32[256,256]{1,0:T(8,128)}, f32[256,256]{1,0:T(8,128)}, f32[256,256]{1,0:T(8,128)}, f32[256,256]{1,0:T(8,128)}, /*...) custom-call(s32[3]{0:T(128)S(1)} %pad_add_fusion.pos, bf16[8,22,8,128]{3,2,1,0:T(8,128)(2,1)S(1)} %all_to_all.23.mine, ...), custom_call_target="tpu_custom_call" | custom-call | tf_op jit(solution)/shard_map/pallas_call | solution.py:94
  (11 shorter events, 0.0 us)
Async XLA Ops:
  0.6 32.7 %copy-start.5 = (bf16[256,256]{1,0:T(8,128)(2,1)S(1)}, bf16[256,256]{1,0:T(8,128)(2,1)}, u32[]{:S(2)}) copy-start(bf16[256,256]{1,0:T(8,128)(2,1)} %wo_ref.1) | copy-start | bytes 393220
  0.7 32.7 %copy-start.4 = (bf16[256,256]{1,0:T(8,128)(2,1)S(1)}, bf16[256,256]{1,0:T(8,128)(2,1)}, u32[]{:S(2)}) copy-start(bf16[256,256]{1,0:T(8,128)(2,1)} %wg_ref.1) | copy-start | bytes 393220
  0.7 32.7 %copy-start.3 = (bf16[256,256]{1,0:T(8,128)(2,1)S(1)}, bf16[256,256]{1,0:T(8,128)(2,1)}, u32[]{:S(2)}) copy-start(bf16[256,256]{1,0:T(8,128)(2,1)} %wv_ref.1) | copy-start | bytes 393220
  0.7 32.7 %copy-start.2 = (bf16[256,256]{1,0:T(8,128)(2,1)S(1)}, bf16[256,256]{1,0:T(8,128)(2,1)}, u32[]{:S(2)}) copy-start(bf16[256,256]{1,0:T(8,128)(2,1)} %wk_ref.1) | copy-start | bytes 393220
  0.7 32.7 %copy-start.1 = (bf16[256,256]{1,0:T(8,128)(2,1)S(1)}, bf16[256,256]{1,0:T(8,128)(2,1)}, u32[]{:S(2)}) copy-start(bf16[256,256]{1,0:T(8,128)(2,1)} %wq_ref.1) | copy-start | bytes 393220
  28.6 4.1 %collective-permute-start = (bf16[1152,128]{1,0:T(8,128)(2,1)S(1)}, bf16[1152,128]{1,0:T(8,128)(2,1)S(1)}, u32[]{:S(2)}, u32[]{:S(2)}) collective-permute-start(bf16[1152,128]{1,0:T(8,128)(2,1)S(1)} %bitcast.19), channel_id=1, source_target_pairs={{0,2},{2,0},{4,6},{6,4},{8,10},{10,8},{12,14},{14,12},{16,18},{18,... | collective-permute-start | bytes 884744 | tf_op jit(solution)/shard_map/ppermute | solution.py:391
  36.0 2.1 %collective-permute-start.1 = (bf16[32,9,8,128]{3,2,1,0:T(8,128)(2,1)S(1)}, bf16[32,9,8,128]{3,2,1,0:T(8,128)(2,1)S(1)}, u32[]{:S(2)}, u32[]{:S(2)}) collective-permute-start(bf16[32,9,8,128]{3,2,1,0:T(8,128)(2,1)S(1)} %get-tuple-element.28), channel_id=1, source_target_pairs={{0,2},{2,0},{4,6},{6,4},{8,10},{10,8},{12,14},{14,12},{16,18},{18,... | collective-permute-start | bytes 1769480 | tf_op jit(solution)/shard_map/ppermute | solution.py:411
  38.2 23.0 %copy-start = (bf16[1,128,128]{2,1,0:T(8,128)(2,1)S(1)}, bf16[1,128,128]{2,1,0:T(8,128)(2,1)}, u32[]{:S(2)}) copy-start(bf16[1,128,128]{2,1,0:T(8,128)(2,1)} %pair.3) | copy-start | bytes 98308
  38.2 23.0 %copy-start.6 = (bf16[128,8]{0,1:T(8,128)(2,1)S(1)}, bf16[128,8]{0,1:T(8,128)(2,1)}, u32[]{:S(2)}) copy-start(bf16[128,8]{0,1:T(8,128)(2,1)} %param.22) | copy-start | bytes 6148
  38.3 23.0 %copy-start.7 = (f32[128]{0:T(128)S(1)}, f32[128]{0:T(128)}, u32[]{:S(2)}) copy-start(f32[128]{0:T(128)} %param.16) | copy-start | bytes 1540
  83.0 5.6 %collective-permute-start.2 = (bf16[8,22,8,128]{3,2,1,0:T(8,128)(2,1)S(1)}, bf16[8,22,8,128]{3,2,1,0:T(8,128)(2,1)S(1)}, u32[]{:S(2)}, u32[]{:S(2)}) collective-permute-start(bf16[8,22,8,128]{3,2,1,0:T(8,128)(2,1)S(1)} %all_to_all.23.mine), channel_id=1, source_target_pairs={{0,2},{2,0},{4,6},{6,4},{8,10},{10,8},{12,14},{14,12},{16,18},{18,... | collective-permute-start | bytes 1081352 | tf_op jit(solution)/shard_map/ppermute | solution.py:437

commit v7 on v6

--- a/solution.py
+++ b/solution.py
@@ -4,7 +4,6 @@
 from jax.experimental import pallas as pl
 from jax.experimental.pallas import tpu as pltpu
 from jax.sharding import PartitionSpec as P
-
 
 FEATURES = 256
 HEADS = 8
@@ -87,17 +86,22 @@
     return 4 + h if h < 5 else 8 + h
 
 
-def call(kernel, out_shape, scratch, *operands, first=SMEM, rest=VMEM, mib=12, far_out=0):
+def call(kernel, out_shape, scratch, *operands, far_in=(), far_out=0):
+    in_specs = [SMEM] + [VMEM] * (len(operands) - 1)
+    operands = list(operands)
+    for n in far_in:
+        in_specs[n] = HBM
+        operands[n] = pltpu.with_memory_space_constraint(operands[n], pltpu.HBM)
     out_specs = jax.tree.map(lambda _: VMEM, out_shape)
     if far_out:
         out_specs = (HBM,) * far_out + out_specs[far_out:]
     return pl.pallas_call(
         kernel,
         out_shape=out_shape,
-        in_specs=[first] + [rest] * (len(operands) - 1),
+        in_specs=in_specs,
         out_specs=out_specs,
         scratch_shapes=scratch,
-        compiler_params=pltpu.CompilerParams(vmem_limit_bytes=mib * 1024 * 1024),
+        compiler_params=pltpu.CompilerParams(vmem_limit_bytes=12 * 1024 * 1024),
     )(*operands)
 
 
@@ -131,9 +135,11 @@
 
 
 def sequence_kernel(
-    pos, near, far, gain_ref, wq_ref, wk_ref, wv_ref, wg_ref, wo_ref,
-    own, other, gain_out, rows, mine, theirs, scores_ref, dp_ref, p_ref, ds_ref
+    pos, near, far, gain_hbm, wq_ref, wk_ref, wv_ref, wg_ref, wo_ref,
+    own, other, gain_out, rows, mine, theirs, scores_ref, dp_ref, p_ref, ds_ref, gain_ref, sem
 ):
+    gain_copy = pltpu.make_async_copy(gain_hbm, gain_ref, sem)
+    gain_copy.start()
     core = pos[0]
     first = core == 0
     rows[core] = near[...].astype(F32)
@@ -157,7 +163,8 @@
             jnp.where(first, value[CHIPS:], value[:CHIPS]),
         )
 
-    gain = gain_ref[0:1, :]
+    gain_copy.wait()
+    gain = gain_ref[...]
     msa = jnp.concatenate([line(0), line(1)], axis=1)
     grad = jnp.concatenate([line(2), line(3)], axis=1).astype(BF16)
     lane = lax.broadcasted_iota(jnp.int32, (8, LANES), 1)
@@ -332,18 +339,16 @@
 def final_kernel(pos, mine, theirs, *refs):
     weights, (head, msa_gain, pair_gain), (stage, sems) = refs[:5], refs[5:8], refs[8:]
     copies = []
-    sums = jnp.zeros((2, 8, LANES), F32)
-    for side, got in enumerate((mine, theirs)):
-        column = pl.multiple_of(LANES * jnp.bitwise_xor(pos[0], side), LANES)
-        for n, w in enumerate((0, 1, 4, 2, 3)):
+    for n, w in enumerate((0, 1, 4, 2, 3)):
+        for side, got in enumerate((mine, theirs)):
+            column = pl.multiple_of(LANES * jnp.bitwise_xor(pos[0], side), LANES)
             value = jnp.stack([got[:, 5 * t + n] for t in range(LINE // 2)], axis=1)
-            stage[side, w] = value.astype(F32).reshape(FEATURES, LANES)
-            copy = pltpu.make_async_copy(
-                stage.at[side, w], weights[w].at[:, pl.ds(column, LANES)], sems.at[side, w]
-            )
-            copy.start()
-            copies.append(copy)
-        sums += jnp.sum(got[:, 20:].astype(F32), axis=0)
+            value = value.astype(F32).reshape(FEATURES, LANES)
+            stage.at[w][:, pl.ds(column, LANES)] = value
+        copy = pltpu.make_async_copy(stage.at[w], weights[w], sems.at[w])
+        copy.start()
+        copies.append(copy)
+    sums = sum(jnp.sum(got[:, 20:].astype(F32), axis=0) for got in (mine, theirs))
     head[...] = sums[1]
     pair_gain[...] = sums[0, 4:5]
     msa_gain[:, :LANES] = sums[0, 5:6]
@@ -366,7 +371,7 @@
         )
 
     w_bias = w_bias.T
-    gain = jnp.broadcast_to(gain.reshape(1, FEATURES), (8, FEATURES))
+    gain = gain.reshape(1, FEATURES)
     pair_gain = pair_gain.reshape(1, LANES)
     sent = call(
         entry_kernel,
@@ -384,7 +389,7 @@
         ],
         msa.reshape(N, FEATURES), grad.reshape(N, FEATURES), flags.reshape(1, N),
         pair, pair_gain, w_bias,
-        first=HBM, rest=HBM, mib=60,
+        far_in=(0, 1, 2, 3, 4, 5),
     )
     near = exchange(sent.reshape(CHIPS, IN_ROWS // 2, 2, LANES), same_core)
     near = near.reshape(CHIPS * IN_ROWS, LANES)
@@ -405,8 +410,11 @@
             pltpu.VMEM((4 * N, FEATURES), F32),
             pltpu.VMEM((N, HEADS * LANES), BF16),
             pltpu.VMEM((N, HEADS * LANES), BF16),
+            pltpu.VMEM((1, FEATURES), F32),
+            pltpu.SemaphoreType.DMA,
         ],
         pos, near, far, gain, wq, wk, wv, wg, wo,
+        far_in=(3,),
     )
     paired = (own + lax.ppermute(other, "dap", partner).astype(F32)).astype(BF16)
     got = exchange(paired.reshape(CHIPS, PART_TILES, 4, LANES), same_core)
@@ -443,7 +451,7 @@
             jax.ShapeDtypeStruct((1, FEATURES), F32),
             jax.ShapeDtypeStruct((1, LANES), F32),
         ),
-        [pltpu.VMEM((CORES, 5, FEATURES, LANES), F32), pltpu.SemaphoreType.DMA((CORES, 5))],
+        [pltpu.VMEM((5, FEATURES, FEATURES), F32), pltpu.SemaphoreType.DMA((5,))],
         pos, mine, theirs,
         far_out=5,
     )

time: 91.2 us -> 90.1 us (0.988)
  no operation moved by 1% of the time
where the time goes in v7:
time: 90.1 us; the launch traced here: 89.8 us
  blocking collectives  68.9 us (76%)
  Pallas kernels  9.82 us (11%)
  starting transfers between devices  7.33 us (8%)
  waiting for transfers between devices  2.77 us (3%)
    all_to_all x4, blocking collectives, exchange(): lax.all_to_all(x, 'dap', split_axis=0, concat_axis=0, tiled=True, axis_in...  68.9 us
    pallas_call x6, Pallas kernels, call(): pl.pallas_call(kernel, out_shape=out_shape, in_specs=in_specs, out_specs=...  9.82 us
    ppermute x1, starting transfers between devices, on_device(): theirs = lax.ppermute(mine, 'dap', partner)  4.03 us
    ppermute x1, starting transfers between devices, on_device(): far = lax.ppermute(near, 'dap', partner)  2.84 us
  transfers between devices with their start and end apart: 3, of which 2 were waited for; matrix products, arithmetic and copies ran while one was open for 0% of the time, Pallas kernels for 2%

profile of v7, /device:TPU:1, one launch (start us, length us, event | category | flops | bytes accessed | tf_op | source)
XLA Modules:
  0.0 89.8 jit_solution(16114206171303175031)
XLA Ops:
  0.6 0.0 copy-start.5
  0.7 0.0 copy-start.4
  0.7 0.0 copy-start.3
  0.7 1.3 %shard_map.203 = bf16[1152,128]{1,0:T(8,128)(2,1)S(1)} custom-call(bf16[128,256]{1,0:T(8,128)(2,1)} %bitcast.30, bf16[128,256]{1,0:T(8,128)(2,1)} %bitcast.31, s32[1,128]{1,0:T(1,128)} %bitcast.33, bf16[1,128,128]{2,1,0:T(8,128)(2,1)} %pair.3, f32[1,128]{1,0:T(1,128)} %bitcast.26, bf16[8,128]{1,0:T(8,128)(2,1)} %bitcast.23), custom_call_target="tpu_custom_call" | custom-call | tf_op jit(solution)/shard_map/pallas_call | solution.py:98
  2.0 25.7 %all_to_all.20 = bf16[64,9,2,128]{3,2,1,0:T(2,128)(2,1)S(1)} all-to-all(bf16[64,9,2,128]{3,2,1,0:T(2,128)(2,1)S(1)} %bitcast.20), channel_id=1, replica_groups={{0,4,8,12,16,20,24,28,32,36,40,44,48,52,56,60,64,68,72,76,80,84,88,92,9..., dimensions={0} | all-to-all | bytes 589824 | tf_op jit(solution)/shard_map/all_to_all | solution.py:369
  27.7 2.8 %collective-permute-start = (bf16[1152,128]{1,0:T(8,128)(2,1)S(1)}, bf16[1152,128]{1,0:T(8,128)(2,1)S(1)}, u32[]{:S(2)}, u32[]{:S(2)}) collective-permute-start(bf16[1152,128]{1,0:T(8,128)(2,1)S(1)} %bitcast.21), channel_id=1, source_target_pairs={{0,2},{2,0},{4,6},{6,4},{8,10},{10,8},{12,14},{14,12},{16,18},{18,... | collective-permute-start | bytes 884744 | tf_op jit(solution)/shard_map/ppermute | solution.py:396
  30.5 0.1 pad_add_fusion.pos
  30.6 1.1 %collective-permute-done.far = bf16[1152,128]{1,0:T(8,128)(2,1)S(1)} collective-permute-done((bf16[1152,128]{1,0:T(8,128)(2,1)S(1)}, bf16[1152,128]{1,0:T(8,128)(2,1)S(1)}, u32[]{:S(2)}, u32[]{:S(2)}) %collective-permute-start) | collective-permute-done | bytes 294944 | tf_op jit(solution)/shard_map/ppermute | solution.py:396
  31.8 3.2 %shard_map.204 = (f32[32,9,8,128]{3,2,1,0:T(8,128)S(1)}, bf16[32,9,8,128]{3,2,1,0:T(8,128)(2,1)S(1)}, f32[1,256]{1,0:T(1,128)S(1)}) custom-call(s32[3]{0:T(128)S(1)} %pad_add_fusion.pos, bf16[1152,128]{1,0:T(8,128)(2,1)S(1)} %bitcast.22, bf16[1152,128]{1,0:T(8,128)(2,1)S(1)} %collective-permute-done.far, f32[1,256]{1,0:T(1,128)} %bitcast.32, ...), custom_call_target="tpu_custom_call" | custom-call | tf_op jit(solution)/shard_map/pallas_call | solution.py:98
  35.0 0.5 collective-permute-start.1
  35.5 1.6 %collective-permute-done.1 = bf16[32,9,8,128]{3,2,1,0:T(8,128)(2,1)S(1)} collective-permute-done((bf16[32,9,8,128]{3,2,1,0:T(8,128)(2,1)S(1)}, bf16[32,9,8,128]{3,2,1,0:T(8,128)(2,1)S(1)}, u32[]{:S(2)}, u32[]{:S(2)}) %collective-permute-start.1) | collective-permute-done | bytes 589856 | tf_op jit(solution)/shard_map/ppermute | solution.py:419
  37.1 0.1 add_convert_fusion
  37.3 0.0 copy-start
  37.3 0.0 copy-start.6
  37.3 0.0 copy-start.7
  37.3 23.0 %all_to_all.21 = bf16[64,9,4,128]{3,2,1,0:T(4,128)(2,1)S(1)} all-to-all(bf16[64,9,4,128]{3,2,1,0:T(4,128)(2,1)S(1)} %bitcast.29), channel_id=1, replica_groups={{0,4,8,12,16,20,24,28,32,36,40,44,48,52,56,60,64,68,72,76,80,84,88,92,9..., dimensions={0} | all-to-all | bytes 1179648 | tf_op jit(solution)/shard_map/all_to_all | solution.py:369
  60.3 0.9 %shard_map.205 = (bf16[8,32,128]{2,1,0:T(8,128)(2,1)S(1)}, f32[8,128]{1,0:T(8,128)S(1)}) custom-call(s32[3]{0:T(128)S(1)} %pad_add_fusion.pos, bf16[2304,128]{1,0:T(8,128)(2,1)S(1)} %bitcast.18, bf16[1,128,128]{2,1,0:T(8,128)(2,1)S(1)} %copy-done, f32[1,128]{1,0:T(1,128)S(1)} %bitcast.27, bf16[8,128]{1,0:T(8,128)(2,1)S(1)} %bitcast.24, ...), custom_call_target="tpu_custom_call" | custom-call | tf_op jit(solution)/shard_map/pallas_call | solution.py:98
  61.2 11.1 %all_to_all.22.got = bf16[8,32,128]{2,1,0:T(8,128)(2,1)S(1)} all-to-all(bf16[8,32,128]{2,1,0:T(8,128)(2,1)S(1)} %get-tuple-element.34), channel_id=1, replica_groups={{0,4,8,12,16,20,24,28},{32,36,40,44,48,52,56,60},{64,68,72,76,80,84,88,..., dimensions={0} | all-to-all | bytes 131072 | tf_op jit(solution)/shard_map/all_to_all | solution.py:369
  72.3 0.6 shard_map.207
  72.9 9.1 %all_to_all.23.mine = bf16[8,22,8,128]{3,2,1,0:T(8,128)(2,1)S(1)} all-to-all(bf16[8,22,8,128]{3,2,1,0:T(8,128)(2,1)S(1)} %shard_map.207), channel_id=1, replica_groups={{0,32,64,96,128,160,192,224},{4,36,68,100,132,164,196,228},{8,40,72,104..., dimensions={0} | all-to-all | bytes 720896 | tf_op jit(solution)/shard_map/all_to_all | solution.py:369
  82.0 4.0 %collective-permute-start.2 = (bf16[8,22,8,128]{3,2,1,0:T(8,128)(2,1)S(1)}, bf16[8,22,8,128]{3,2,1,0:T(8,128)(2,1)S(1)}, u32[]{:S(2)}, u32[]{:S(2)}) collective-permute-start(bf16[8,22,8,128]{3,2,1,0:T(8,128)(2,1)S(1)} %all_to_all.23.mine), channel_id=1, source_target_pairs={{0,2},{2,0},{4,6},{6,4},{8,10},{10,8},{12,14},{14,12},{16,18},{18,... | collective-permute-start | bytes 1081352 | tf_op jit(solution)/shard_map/ppermute | solution.py:445
  86.0 1.6 %shard_map.206 = (bf16[128,256]{1,0:T(8,128)(2,1)}, bf16[128,256]{1,0:T(8,128)(2,1)}, bf16[1,128,128]{2,1,0:T(8,128)(2,1)}) custom-call(s32[3]{0:T(128)S(1)} %pad_add_fusion.pos, bf16[2304,128]{1,0:T(8,128)(2,1)S(1)} %bitcast.19, f32[8,128]{1,0:T(8,128)S(1)} %get-tuple-element.30.d_bias, bf16[1,128,128]{2,1,0:T(8,128)(2,1)S(1)} %copy-done, ...), custom_call_target="tpu_custom_call" | custom-call | tf_op jit(solution)/shard_map/pallas_call | solution.py:98
  87.6 0.0 collective-permute-done.2.theirs
  87.6 2.2 %shard_map.208 = (f32[256,256]{1,0:T(8,128)}, f32[256,256]{1,0:T(8,128)}, f32[256,256]{1,0:T(8,128)}, f32[256,256]{1,0:T(8,128)}, f32[256,256]{1,0:T(8,128)}, /*...) custom-call(s32[3]{0:T(128)S(1)} %pad_add_fusion.pos, bf16[8,22,8,128]{3,2,1,0:T(8,128)(2,1)S(1)} %all_to_all.23.mine, ...), custom_call_target="tpu_custom_call" | custom-call | tf_op jit(solution)/shard_map/pallas_call | solution.py:98
  (10 shorter events, 0.0 us)
Async XLA Ops:
  0.6 31.1 %copy-start.5 = (bf16[256,256]{1,0:T(8,128)(2,1)S(1)}, bf16[256,256]{1,0:T(8,128)(2,1)}, u32[]{:S(2)}) copy-start(bf16[256,256]{1,0:T(8,128)(2,1)} %wo_ref.1) | copy-start | bytes 393220
  0.7 31.1 %copy-start.4 = (bf16[256,256]{1,0:T(8,128)(2,1)S(1)}, bf16[256,256]{1,0:T(8,128)(2,1)}, u32[]{:S(2)}) copy-start(bf16[256,256]{1,0:T(8,128)(2,1)} %wg_ref.1) | copy-start | bytes 393220
  0.7 31.1 %copy-start.3 = (bf16[256,256]{1,0:T(8,128)(2,1)S(1)}, bf16[256,256]{1,0:T(8,128)(2,1)}, u32[]{:S(2)}) copy-start(bf16[256,256]{1,0:T(8,128)(2,1)} %wv_ref.1) | copy-start | bytes 393220
  0.7 31.1 %copy-start.2 = (bf16[256,256]{1,0:T(8,128)(2,1)S(1)}, bf16[256,256]{1,0:T(8,128)(2,1)}, u32[]{:S(2)}) copy-start(bf16[256,256]{1,0:T(8,128)(2,1)} %wk_ref.1) | copy-start | bytes 393220
  0.7 31.1 %copy-start.1 = (bf16[256,256]{1,0:T(8,128)(2,1)S(1)}, bf16[256,256]{1,0:T(8,128)(2,1)}, u32[]{:S(2)}) copy-start(bf16[256,256]{1,0:T(8,128)(2,1)} %wq_ref.1) | copy-start | bytes 393220
  27.7 4.1 %collective-permute-start = (bf16[1152,128]{1,0:T(8,128)(2,1)S(1)}, bf16[1152,128]{1,0:T(8,128)(2,1)S(1)}, u32[]{:S(2)}, u32[]{:S(2)}) collective-permute-start(bf16[1152,128]{1,0:T(8,128)(2,1)S(1)} %bitcast.21), channel_id=1, source_target_pairs={{0,2},{2,0},{4,6},{6,4},{8,10},{10,8},{12,14},{14,12},{16,18},{18,... | collective-permute-start | bytes 884744 | tf_op jit(solution)/shard_map/ppermute | solution.py:396
  35.0 2.1 %collective-permute-start.1 = (bf16[32,9,8,128]{3,2,1,0:T(8,128)(2,1)S(1)}, bf16[32,9,8,128]{3,2,1,0:T(8,128)(2,1)S(1)}, u32[]{:S(2)}, u32[]{:S(2)}) collective-permute-start(bf16[32,9,8,128]{3,2,1,0:T(8,128)(2,1)S(1)} %get-tuple-element.28), channel_id=1, source_target_pairs={{0,2},{2,0},{4,6},{6,4},{8,10},{10,8},{12,14},{14,12},{16,18},{18,... | collective-permute-start | bytes 1769480 | tf_op jit(solution)/shard_map/ppermute | solution.py:419
  37.3 23.0 %copy-start = (bf16[1,128,128]{2,1,0:T(8,128)(2,1)S(1)}, bf16[1,128,128]{2,1,0:T(8,128)(2,1)}, u32[]{:S(2)}) copy-start(bf16[1,128,128]{2,1,0:T(8,128)(2,1)} %pair.3) | copy-start | bytes 98308
  37.3 23.0 %copy-start.6 = (bf16[128,8]{0,1:T(8,128)(2,1)S(1)}, bf16[128,8]{0,1:T(8,128)(2,1)}, u32[]{:S(2)}) copy-start(bf16[128,8]{0,1:T(8,128)(2,1)} %param.22) | copy-start | bytes 6148
  37.3 23.0 %copy-start.7 = (f32[128]{0:T(128)S(1)}, f32[128]{0:T(128)}, u32[]{:S(2)}) copy-start(f32[128]{0:T(128)} %param.16) | copy-start | bytes 1540
  82.0 5.6 %collective-permute-start.2 = (bf16[8,22,8,128]{3,2,1,0:T(8,128)(2,1)S(1)}, bf16[8,22,8,128]{3,2,1,0:T(8,128)(2,1)S(1)}, u32[]{:S(2)}, u32[]{:S(2)}) collective-permute-start(bf16[8,22,8,128]{3,2,1,0:T(8,128)(2,1)S(1)} %all_to_all.23.mine), channel_id=1, source_target_pairs={{0,2},{2,0},{4,6},{6,4},{8,10},{10,8},{12,14},{14,12},{16,18},{18,... | collective-permute-start | bytes 1081352 | tf_op jit(solution)/shard_map/ppermute | solution.py:445

commit v8 on v7

--- a/solution.py
+++ b/solution.py
@@ -86,42 +86,39 @@
     return 4 + h if h < 5 else 8 + h
 
 
-def call(kernel, out_shape, scratch, *operands, far_in=(), far_out=0):
+def call(kernel, out_shape, scratch, *operands, far_in=()):
     in_specs = [SMEM] + [VMEM] * (len(operands) - 1)
     operands = list(operands)
     for n in far_in:
         in_specs[n] = HBM
         operands[n] = pltpu.with_memory_space_constraint(operands[n], pltpu.HBM)
-    out_specs = jax.tree.map(lambda _: VMEM, out_shape)
-    if far_out:
-        out_specs = (HBM,) * far_out + out_specs[far_out:]
     return pl.pallas_call(
         kernel,
         out_shape=out_shape,
         in_specs=in_specs,
-        out_specs=out_specs,
+        out_specs=jax.tree.map(lambda _: VMEM, out_shape),
         scratch_shapes=scratch,
         compiler_params=pltpu.CompilerParams(vmem_limit_bytes=12 * 1024 * 1024),
     )(*operands)
 
 
-def entry_kernel(
-    msa_hbm, grad_hbm, flags_hbm, pair_hbm, gain_hbm, w_hbm,
-    out, msa, grad, flags, pair, gain, w_bias, stage, rows, sems
-):
-    refs = (
-        (pair_hbm, pair), (gain_hbm, gain), (w_hbm, w_bias),
-        (msa_hbm, msa), (grad_hbm, grad), (flags_hbm, flags),
-    )
-    copies = [pltpu.make_async_copy(a, b, sems.at[i]) for i, (a, b) in enumerate(refs)]
-    for copy in copies:
-        copy.start()
+def entry_kernel(*refs):
+    sources, out, kept, (msa, grad, flags, stage, rows, sems) = (
+        refs[:12], refs[12], refs[13:22], refs[22:]
+    )
+    targets = kept + (msa, grad, flags)
+    copies = [
+        pltpu.make_async_copy(a, b, sems.at[i]) for i, (a, b) in enumerate(zip(sources, targets))
+    ]
+    for n in (0, 1, 2, 9, 10, 11, 3, 4, 5, 6, 7, 8):
+        copies[n].start()
+    pair, gain, w_bias = kept[:3]
     for copy in copies[:3]:
         copy.wait()
     rows[...] = pair[0].astype(F32)
     _, _, scaled = layer_norm(reordered(rows), gain[...])
     bias = dot_nt(w_bias[...], scaled.astype(BF16))
-    for copy in copies[3:]:
+    for copy in copies[9:]:
         copy.wait()
     for r, ref in enumerate((msa, grad)):
         value = ref[...].astype(F32)
@@ -132,14 +129,14 @@
     for r, value in lines:
         stage[pl.ds(r, CHIPS, stride=IN_ROWS), :] = jnp.broadcast_to(value, (CHIPS, LANES))
     out[...] = stage[...].astype(BF16)
+    for copy in copies[3:9]:
+        copy.wait()
 
 
 def sequence_kernel(
-    pos, near, far, gain_hbm, wq_ref, wk_ref, wv_ref, wg_ref, wo_ref,
-    own, other, gain_out, rows, mine, theirs, scores_ref, dp_ref, p_ref, ds_ref, gain_ref, sem
+    pos, near, far, gain_ref, wq_ref, wk_ref, wv_ref, wg_ref, wo_ref,
+    own, other, gain_out, rows, mine, theirs, scores_ref, dp_ref, p_ref, ds_ref
 ):
-    gain_copy = pltpu.make_async_copy(gain_hbm, gain_ref, sem)
-    gain_copy.start()
     core = pos[0]
     first = core == 0
     rows[core] = near[...].astype(F32)
@@ -163,7 +160,6 @@
             jnp.where(first, value[CHIPS:], value[:CHIPS]),
         )
 
-    gain_copy.wait()
     gain = gain_ref[...]
     msa = jnp.concatenate([line(0), line(1)], axis=1)
     grad = jnp.concatenate([line(2), line(3)], axis=1).astype(BF16)
@@ -337,24 +333,18 @@
 
 
 def final_kernel(pos, mine, theirs, *refs):
-    weights, (head, msa_gain, pair_gain), (stage, sems) = refs[:5], refs[5:8], refs[8:]
-    copies = []
+    weights, (head, msa_gain, pair_gain) = refs[:5], refs[5:]
     for n, w in enumerate((0, 1, 4, 2, 3)):
         for side, got in enumerate((mine, theirs)):
             column = pl.multiple_of(LANES * jnp.bitwise_xor(pos[0], side), LANES)
             value = jnp.stack([got[:, 5 * t + n] for t in range(LINE // 2)], axis=1)
             value = value.astype(F32).reshape(FEATURES, LANES)
-            stage.at[w][:, pl.ds(column, LANES)] = value
-        copy = pltpu.make_async_copy(stage.at[w], weights[w], sems.at[w])
-        copy.start()
-        copies.append(copy)
+            weights[w][:, pl.ds(column, LANES)] = value
     sums = sum(jnp.sum(got[:, 20:].astype(F32), axis=0) for got in (mine, theirs))
     head[...] = sums[1]
     pair_gain[...] = sums[0, 4:5]
     msa_gain[:, :LANES] = sums[0, 5:6]
     msa_gain[:, LANES:] = sums[0, 6:7]
-    for copy in copies:
-        copy.wait()
 
 
 def on_device(msa, flags, pair, gain, pair_gain, wq, wk, wv, wg, wo, w_bias, grad):
@@ -373,24 +363,23 @@
     w_bias = w_bias.T
     gain = gain.reshape(1, FEATURES)
     pair_gain = pair_gain.reshape(1, LANES)
-    sent = call(
+    kept = (pair, pair_gain, w_bias, wq, wk, wv, wg, wo, gain)
+    sent, *kept = call(
         entry_kernel,
-        jax.ShapeDtypeStruct((CHIPS * IN_ROWS, LANES), BF16),
+        (jax.ShapeDtypeStruct((CHIPS * IN_ROWS, LANES), BF16),)
+        + tuple(jax.ShapeDtypeStruct(v.shape, v.dtype) for v in kept),
         [
             pltpu.VMEM((N, FEATURES), BF16),
             pltpu.VMEM((N, FEATURES), BF16),
             pltpu.VMEM((1, N), jnp.int32),
-            pltpu.VMEM((1, N, LANES), BF16),
-            pltpu.VMEM((1, LANES), F32),
-            pltpu.VMEM((HEADS, LANES), BF16),
             pltpu.VMEM((CHIPS * IN_ROWS, LANES), F32),
             pltpu.VMEM((N, LANES), F32),
-            pltpu.SemaphoreType.DMA((6,)),
+            pltpu.SemaphoreType.DMA((12,)),
         ],
-        msa.reshape(N, FEATURES), grad.reshape(N, FEATURES), flags.reshape(1, N),
-        pair, pair_gain, w_bias,
-        far_in=(0, 1, 2, 3, 4, 5),
-    )
+        *kept, msa.reshape(N, FEATURES), grad.reshape(N, FEATURES), flags.reshape(1, N),
+        far_in=range(12),
+    )
+    pair, pair_gain, w_bias, wq, wk, wv, wg, wo, gain = kept
     near = exchange(sent.reshape(CHIPS, IN_ROWS // 2, 2, LANES), same_core)
     near = near.reshape(CHIPS * IN_ROWS, LANES)
     far = lax.ppermute(near, "dap", partner)
@@ -410,11 +399,8 @@
             pltpu.VMEM((4 * N, FEATURES), F32),
             pltpu.VMEM((N, HEADS * LANES), BF16),
             pltpu.VMEM((N, HEADS * LANES), BF16),
-            pltpu.VMEM((1, FEATURES), F32),
-            pltpu.SemaphoreType.DMA,
         ],
         pos, near, far, gain, wq, wk, wv, wg, wo,
-        far_in=(3,),
     )
     paired = (own + lax.ppermute(other, "dap", partner).astype(F32)).astype(BF16)
     got = exchange(paired.reshape(CHIPS, PART_TILES, 4, LANES), same_core)
@@ -451,9 +437,8 @@
             jax.ShapeDtypeStruct((1, FEATURES), F32),
             jax.ShapeDtypeStruct((1, LANES), F32),
         ),
-        [pltpu.VMEM((5, FEATURES, FEATURES), F32), pltpu.SemaphoreType.DMA((5,))],
+        [],
         pos, mine, theirs,
-        far_out=5,
     )
     return (
         update.reshape(N, 1, FEATURES),

time: 90.1 us -> 88.7 us (0.984)
  Pallas kernels: 9.82 us -> 8.71 us
    pallas_call x6, Pallas kernels: 9.82 us -> 8.71 us  [call(): pl.pallas_call(kernel, out_shape=out_shape, in_specs=in_specs, out_specs=...]
where the time goes in v8:
time: 88.7 us; the launch traced here: 88.5 us
  blocking collectives  68.8 us (78%)
  Pallas kernels  8.71 us (10%)
  starting transfers between devices  7.33 us (8%)
  waiting for transfers between devices  2.77 us (3%)
    all_to_all x4, blocking collectives, exchange(): lax.all_to_all(x, 'dap', split_axis=0, concat_axis=0, tiled=True, axis_in...  68.8 us
    pallas_call x6, Pallas kernels, call(): pl.pallas_call(kernel, out_shape=out_shape, in_specs=in_specs, out_specs=...  8.71 us
    ppermute x1, starting transfers between devices, on_device(): theirs = lax.ppermute(mine, 'dap', partner)  4.03 us
    ppermute x1, starting transfers between devices, on_device(): far = lax.ppermute(near, 'dap', partner)  2.84 us
  transfers between devices with their start and end apart: 3, of which 2 were waited for; matrix products, arithmetic and copies ran while one was open for 0% of the time, Pallas kernels for 2%

profile of v8, /device:TPU:1, one launch (start us, length us, event | category | flops | bytes accessed | tf_op | source)
XLA Modules:
  0.0 88.5 jit_solution(11993002481929388152)
XLA Ops:
  0.6 1.4 %shard_map.203 = (bf16[1152,128]{1,0:T(8,128)(2,1)S(1)}, bf16[1,128,128]{2,1,0:T(8,128)(2,1)S(1)}, f32[1,128]{1,0:T(1,128)S(1)}, bf16[8,128]{1,0:T(8,128)(2,1)S(...) custom-call(bf16[1,128,128]{2,1,0:T(8,128)(2,1)} %refs_0_.1, ...), custom_call_target="tpu_custom_call" | custom-call | tf_op jit(solution)/shard_map/pallas_call | solution.py:95
  2.0 25.7 %all_to_all.20 = bf16[64,9,2,128]{3,2,1,0:T(2,128)(2,1)S(1)} all-to-all(bf16[64,9,2,128]{3,2,1,0:T(2,128)(2,1)S(1)} %bitcast.22), channel_id=1, replica_groups={{0,4,8,12,16,20,24,28,32,36,40,44,48,52,56,60,64,68,72,76,80,84,88,92,9..., dimensions={0} | all-to-all | bytes 589824 | tf_op jit(solution)/shard_map/all_to_all | solution.py:359
  27.7 2.8 %collective-permute-start = (bf16[1152,128]{1,0:T(8,128)(2,1)S(1)}, bf16[1152,128]{1,0:T(8,128)(2,1)S(1)}, u32[]{:S(2)}, u32[]{:S(2)}) collective-permute-start(bf16[1152,128]{1,0:T(8,128)(2,1)S(1)} %bitcast.20), channel_id=1, source_target_pairs={{0,2},{2,0},{4,6},{6,4},{8,10},{10,8},{12,14},{14,12},{16,18},{18,... | collective-permute-start | bytes 884744 | tf_op jit(solution)/shard_map/ppermute | solution.py:385
  30.6 0.1 pad_add_fusion.pos
  30.7 1.1 %collective-permute-done.far = bf16[1152,128]{1,0:T(8,128)(2,1)S(1)} collective-permute-done((bf16[1152,128]{1,0:T(8,128)(2,1)S(1)}, bf16[1152,128]{1,0:T(8,128)(2,1)S(1)}, u32[]{:S(2)}, u32[]{:S(2)}) %collective-permute-start) | collective-permute-done | bytes 294944 | tf_op jit(solution)/shard_map/ppermute | solution.py:385
  31.8 2.6 %shard_map.204 = (f32[32,9,8,128]{3,2,1,0:T(8,128)S(1)}, bf16[32,9,8,128]{3,2,1,0:T(8,128)(2,1)S(1)}, f32[1,256]{1,0:T(1,128)S(1)}) custom-call(s32[3]{0:T(128)S(1)} %pad_add_fusion.pos, bf16[1152,128]{1,0:T(8,128)(2,1)S(1)} %bitcast.21, bf16[1152,128]{1,0:T(8,128)(2,1)S(1)} %collective-permute-done.far, f32[1,256]{1,0:T(1,128)S(1)} %get-tuple-element.38.gain_ref, ...), custom_call_target="tpu_custom_call" | custom-call | tf_op jit(solution)/shard_map/pallas_call | solution.py:95
  34.4 0.5 collective-permute-start.1
  34.9 1.6 %collective-permute-done.1 = bf16[32,9,8,128]{3,2,1,0:T(8,128)(2,1)S(1)} collective-permute-done((bf16[32,9,8,128]{3,2,1,0:T(8,128)(2,1)S(1)}, bf16[32,9,8,128]{3,2,1,0:T(8,128)(2,1)S(1)}, u32[]{:S(2)}, u32[]{:S(2)}) %collective-permute-start.1) | collective-permute-done | bytes 589856 | tf_op jit(solution)/shard_map/ppermute | solution.py:405
  36.5 0.1 add_convert_fusion
  36.7 22.9 %all_to_all.21 = bf16[64,9,4,128]{3,2,1,0:T(4,128)(2,1)S(1)} all-to-all(bf16[64,9,4,128]{3,2,1,0:T(4,128)(2,1)S(1)} %bitcast.23), channel_id=1, replica_groups={{0,4,8,12,16,20,24,28,32,36,40,44,48,52,56,60,64,68,72,76,80,84,88,92,9..., dimensions={0} | all-to-all | bytes 1179648 | tf_op jit(solution)/shard_map/all_to_all | solution.py:359
  59.5 0.9 %shard_map.205 = (bf16[8,32,128]{2,1,0:T(8,128)(2,1)S(1)}, f32[8,128]{1,0:T(8,128)S(1)}) custom-call(s32[3]{0:T(128)S(1)} %pad_add_fusion.pos, bf16[2304,128]{1,0:T(8,128)(2,1)S(1)} %bitcast.18, bf16[1,128,128]{2,1,0:T(8,128)(2,1)S(1)} %get-tuple-element.46.pair, f32[1,128]{1,0:T(1,128)S(1)} %get-tuple-element.47.gain.gain_ref, ...), custom_call_target="tpu_custom_call" | custom-call | tf_op jit(solution)/shard_map/pallas_call | solution.py:95
  60.4 11.1 %all_to_all.22.got = bf16[8,32,128]{2,1,0:T(8,128)(2,1)S(1)} all-to-all(bf16[8,32,128]{2,1,0:T(8,128)(2,1)S(1)} %get-tuple-element.54), channel_id=1, replica_groups={{0,4,8,12,16,20,24,28},{32,36,40,44,48,52,56,60},{64,68,72,76,80,84,88,..., dimensions={0} | all-to-all | bytes 131072 | tf_op jit(solution)/shard_map/all_to_all | solution.py:359
  71.5 0.6 shard_map.207
  72.1 9.1 %all_to_all.23.mine = bf16[8,22,8,128]{3,2,1,0:T(8,128)(2,1)S(1)} all-to-all(bf16[8,22,8,128]{3,2,1,0:T(8,128)(2,1)S(1)} %shard_map.207), channel_id=1, replica_groups={{0,32,64,96,128,160,192,224},{4,36,68,100,132,164,196,228},{8,40,72,104..., dimensions={0} | all-to-all | bytes 720896 | tf_op jit(solution)/shard_map/all_to_all | solution.py:359
  81.2 4.0 %collective-permute-start.2 = (bf16[8,22,8,128]{3,2,1,0:T(8,128)(2,1)S(1)}, bf16[8,22,8,128]{3,2,1,0:T(8,128)(2,1)S(1)}, u32[]{:S(2)}, u32[]{:S(2)}) collective-permute-start(bf16[8,22,8,128]{3,2,1,0:T(8,128)(2,1)S(1)} %all_to_all.23.mine), channel_id=1, source_target_pairs={{0,2},{2,0},{4,6},{6,4},{8,10},{10,8},{12,14},{14,12},{16,18},{18,... | collective-permute-start | bytes 1081352 | tf_op jit(solution)/shard_map/ppermute | solution.py:431
  85.2 1.6 %shard_map.206 = (bf16[128,256]{1,0:T(8,128)(2,1)}, bf16[128,256]{1,0:T(8,128)(2,1)}, bf16[1,128,128]{2,1,0:T(8,128)(2,1)}) custom-call(s32[3]{0:T(128)S(1)} %pad_add_fusion.pos, bf16[2304,128]{1,0:T(8,128)(2,1)S(1)} %bitcast.19, f32[8,128]{1,0:T(8,128)S(1)} %get-tuple-element.50.d_bias, bf16[1,128,128]{2,1,0:T(8,128)(2,1)S(1)} %get-tuple-element.46.pair, ...), custom_call_target="tpu_custom_call" | custom-call | tf_op jit(solution)/shard_map/pallas_call | solution.py:95
  86.8 0.0 collective-permute-done.2.theirs
  86.8 1.7 %shard_map.208 = (f32[256,256]{1,0:T(8,128)}, f32[256,256]{1,0:T(8,128)}, f32[256,256]{1,0:T(8,128)}, f32[256,256]{1,0:T(8,128)}, f32[256,256]{1,0:T(8,128)}, /*...) custom-call(s32[3]{0:T(128)S(1)} %pad_add_fusion.pos, bf16[8,22,8,128]{3,2,1,0:T(8,128)(2,1)S(1)} %all_to_all.23.mine, ...), custom_call_target="tpu_custom_call" | custom-call | tf_op jit(solution)/shard_map/pallas_call | solution.py:95
Async XLA Ops:
  27.7 4.1 %collective-permute-start = (bf16[1152,128]{1,0:T(8,128)(2,1)S(1)}, bf16[1152,128]{1,0:T(8,128)(2,1)S(1)}, u32[]{:S(2)}, u32[]{:S(2)}) collective-permute-start(bf16[1152,128]{1,0:T(8,128)(2,1)S(1)} %bitcast.20), channel_id=1, source_target_pairs={{0,2},{2,0},{4,6},{6,4},{8,10},{10,8},{12,14},{14,12},{16,18},{18,... | collective-permute-start | bytes 884744 | tf_op jit(solution)/shard_map/ppermute | solution.py:385
  34.4 2.1 %collective-permute-start.1 = (bf16[32,9,8,128]{3,2,1,0:T(8,128)(2,1)S(1)}, bf16[32,9,8,128]{3,2,1,0:T(8,128)(2,1)S(1)}, u32[]{:S(2)}, u32[]{:S(2)}) collective-permute-start(bf16[32,9,8,128]{3,2,1,0:T(8,128)(2,1)S(1)} %get-tuple-element.45), channel_id=1, source_target_pairs={{0,2},{2,0},{4,6},{6,4},{8,10},{10,8},{12,14},{14,12},{16,18},{18,... | collective-permute-start | bytes 1769480 | tf_op jit(solution)/shard_map/ppermute | solution.py:405
  81.2 5.6 %collective-permute-start.2 = (bf16[8,22,8,128]{3,2,1,0:T(8,128)(2,1)S(1)}, bf16[8,22,8,128]{3,2,1,0:T(8,128)(2,1)S(1)}, u32[]{:S(2)}, u32[]{:S(2)}) collective-permute-start(bf16[8,22,8,128]{3,2,1,0:T(8,128)(2,1)S(1)} %all_to_all.23.mine), channel_id=1, source_target_pairs={{0,2},{2,0},{4,6},{6,4},{8,10},{10,8},{12,14},{14,12},{16,18},{18,... | collective-permute-start | bytes 1081352 | tf_op jit(solution)/shard_map/ppermute | solution.py:431

commit v9 on v8

--- a/solution.py
+++ b/solution.py
@@ -69,6 +69,21 @@
 
 
 ORDER = [(c, p) for c in range(CORES) for p in range(2)]
+
+
+LINES = (7, 4, 5, 6, 3, 0, 1, 2)
+LINE_ROWS = 2 * 8
+
+
+def listed(value):
+    return jnp.concatenate(
+        [value[q * LINE_ROWS : (q + 1) * LINE_ROWS] for q in LINES], axis=0
+    )
+
+
+def natural(value):
+    at = [LINES.index(q) * LINE_ROWS for q in range(8)]
+    return jnp.concatenate([value[a : a + LINE_ROWS] for a in at], axis=0)
 
 
 def reordered(rows):
@@ -115,13 +130,13 @@
     pair, gain, w_bias = kept[:3]
     for copy in copies[:3]:
         copy.wait()
-    rows[...] = pair[0].astype(F32)
+    rows[...] = listed(pair[0].astype(F32))
     _, _, scaled = layer_norm(reordered(rows), gain[...])
     bias = dot_nt(w_bias[...], scaled.astype(BF16))
     for copy in copies[9:]:
         copy.wait()
     for r, ref in enumerate((msa, grad)):
-        value = ref[...].astype(F32)
+        value = listed(ref[...].astype(F32))
         stage[pl.ds(2 * r, N, stride=9), :] = value[:, :LANES]
         stage[pl.ds(2 * r + 1, N, stride=9), :] = value[:, LANES:]
     lines = [(bias_row(h), bias[h : h + 1]) for h in range(HEADS)]
@@ -261,7 +276,7 @@
 
 
 def pair_gradient(d_bias, pair, gain, w_bias, rows):
-    rows[...] = pair[0].astype(F32)
+    rows[...] = listed(pair[0].astype(F32))
     hat, inv, scaled = layer_norm(reordered(rows), gain)
     parts = split(d_bias)[::-1]
     d_pln = sum(dot_tn(part, w_bias) for part in parts)
@@ -310,11 +325,11 @@
             same, cross = line(r), line(4 + r)
             rows[pl.ds(0, CHIPS, stride=CORES), :] = jnp.where(first, same, cross)
             rows[pl.ds(1, CHIPS, stride=CORES), :] = jnp.where(first, cross, same)
-            out[:, half * LANES : (half + 1) * LANES] = rows[...].astype(BF16)
+            out[:, half * LANES : (half + 1) * LANES] = natural(rows[...]).astype(BF16)
     gain = gain_ref[...]
     hat, inv, d_pln, _ = pair_gradient(d_bias[...], pair, gain, w_bias[...], rows)
     restore(rows, layer_norm_adjoint(d_pln, hat, inv, gain))
-    couple[0] = rows[...].astype(BF16)
+    couple[0] = natural(rows[...]).astype(BF16)
 
 
 def line_kernel(pos, got, out):
@@ -350,9 +365,10 @@
 def on_device(msa, flags, pair, gain, pair_gain, wq, wk, wv, wg, wo, w_bias, grad):
     index = lax.axis_index("dap")
     pos = jnp.stack([index % CORES, index, index // CORES]).astype(jnp.int32)
-    same_core = [[CORES * m + c for m in range(CHIPS)] for c in range(CORES)]
-    along_z = [[g[LINE * q + z] for z in range(LINE)] for g in same_core for q in range(LINE)]
-    across = [[g[LINE * q + z] for q in range(LINE)] for g in same_core for z in range(LINE)]
+    chips = [LINE * q + z for q in LINES for z in range(LINE)]
+    same_core = [[CORES * m + c for m in chips] for c in range(CORES)]
+    along_z = [g[LINE * q : LINE * (q + 1)] for g in same_core for q in range(LINE)]
+    across = [g[z::LINE] for g in same_core for z in range(LINE)]
     partner = [(i, i ^ 1) for i in range(N)]
 
     def exchange(x, groups):

time: 88.7 us -> 86.9 us (0.980)
  blocking collectives: 68.8 us -> 67.2 us
    all_to_all x4, blocking collectives: 68.8 us -> 67.2 us  [exchange(): lax.all_to_all(x, 'dap', split_axis=0, concat_axis=0, tiled=True, axis_in...]
where the time goes in v9:
time: 86.9 us; the launch traced here: 86.7 us
  blocking collectives  67.2 us (77%)
  Pallas kernels  8.71 us (10%)
  starting transfers between devices  7.04 us (8%)
  waiting for transfers between devices  2.77 us (3%)
    all_to_all x4, blocking collectives, exchange(): lax.all_to_all(x, 'dap', split_axis=0, concat_axis=0, tiled=True, axis_in...  67.2 us
    pallas_call x6, Pallas kernels, call(): pl.pallas_call(kernel, out_shape=out_shape, in_specs=in_specs, out_specs=...  8.71 us
    ppermute x1, starting transfers between devices, on_device(): theirs = lax.ppermute(mine, 'dap', partner)  4 us
    ppermute x1, starting transfers between devices, on_device(): far = lax.ppermute(near, 'dap', partner)  2.58 us
  transfers between devices with their start and end apart: 3, of which 2 were waited for; matrix products, arithmetic and copies ran while one was open for 0% of the time, Pallas kernels for 2%

profile of v9, /device:TPU:1, one launch (start us, length us, event | category | flops | bytes accessed | tf_op | source)
XLA Modules:
  0.0 86.7 jit_solution(15369911126900372697)
XLA Ops:
  0.6 1.4 %shard_map.203 = (bf16[1152,128]{1,0:T(8,128)(2,1)S(1)}, bf16[1,128,128]{2,1,0:T(8,128)(2,1)S(1)}, f32[1,128]{1,0:T(1,128)S(1)}, bf16[8,128]{1,0:T(8,128)(2,1)S(...) custom-call(bf16[1,128,128]{2,1,0:T(8,128)(2,1)} %refs_0_.1, ...), custom_call_target="tpu_custom_call" | custom-call | tf_op jit(solution)/shard_map/pallas_call | solution.py:110
  2.0 25.0 %all_to_all.20 = bf16[64,9,2,128]{3,2,1,0:T(2,128)(2,1)S(1)} all-to-all(bf16[64,9,2,128]{3,2,1,0:T(2,128)(2,1)S(1)} %bitcast.22), channel_id=1, replica_groups={{224,228,232,236,240,244,248,252,128,132,136,140,144,148,152,156,160,16..., dimensions={0} | all-to-all | bytes 589824 | tf_op jit(solution)/shard_map/all_to_all | solution.py:375
  27.0 2.6 %collective-permute-start = (bf16[1152,128]{1,0:T(8,128)(2,1)S(1)}, bf16[1152,128]{1,0:T(8,128)(2,1)S(1)}, u32[]{:S(2)}, u32[]{:S(2)}) collective-permute-start(bf16[1152,128]{1,0:T(8,128)(2,1)S(1)} %bitcast.20), channel_id=1, source_target_pairs={{0,2},{2,0},{4,6},{6,4},{8,10},{10,8},{12,14},{14,12},{16,18},{18,... | collective-permute-start | bytes 884744 | tf_op jit(solution)/shard_map/ppermute | solution.py:401
  29.6 0.1 pad_add_fusion.pos
  29.7 1.1 %collective-permute-done.far = bf16[1152,128]{1,0:T(8,128)(2,1)S(1)} collective-permute-done((bf16[1152,128]{1,0:T(8,128)(2,1)S(1)}, bf16[1152,128]{1,0:T(8,128)(2,1)S(1)}, u32[]{:S(2)}, u32[]{:S(2)}) %collective-permute-start) | collective-permute-done | bytes 294944 | tf_op jit(solution)/shard_map/ppermute | solution.py:401
  30.8 2.6 %shard_map.204 = (f32[32,9,8,128]{3,2,1,0:T(8,128)S(1)}, bf16[32,9,8,128]{3,2,1,0:T(8,128)(2,1)S(1)}, f32[1,256]{1,0:T(1,128)S(1)}) custom-call(s32[3]{0:T(128)S(1)} %pad_add_fusion.pos, bf16[1152,128]{1,0:T(8,128)(2,1)S(1)} %bitcast.21, bf16[1152,128]{1,0:T(8,128)(2,1)S(1)} %collective-permute-done.far, f32[1,256]{1,0:T(1,128)S(1)} %get-tuple-element.38.gain_ref, ...), custom_call_target="tpu_custom_call" | custom-call | tf_op jit(solution)/shard_map/pallas_call | solution.py:110
  33.4 0.5 collective-permute-start.1
  33.9 1.6 %collective-permute-done.1 = bf16[32,9,8,128]{3,2,1,0:T(8,128)(2,1)S(1)} collective-permute-done((bf16[32,9,8,128]{3,2,1,0:T(8,128)(2,1)S(1)}, bf16[32,9,8,128]{3,2,1,0:T(8,128)(2,1)S(1)}, u32[]{:S(2)}, u32[]{:S(2)}) %collective-permute-start.1) | collective-permute-done | bytes 589856 | tf_op jit(solution)/shard_map/ppermute | solution.py:421
  35.5 0.1 add_convert_fusion
  35.7 23.1 %all_to_all.21 = bf16[64,9,4,128]{3,2,1,0:T(4,128)(2,1)S(1)} all-to-all(bf16[64,9,4,128]{3,2,1,0:T(4,128)(2,1)S(1)} %bitcast.23), channel_id=1, replica_groups={{224,228,232,236,240,244,248,252,128,132,136,140,144,148,152,156,160,16..., dimensions={0} | all-to-all | bytes 1179648 | tf_op jit(solution)/shard_map/all_to_all | solution.py:375
  58.8 0.9 %shard_map.205 = (bf16[8,32,128]{2,1,0:T(8,128)(2,1)S(1)}, f32[8,128]{1,0:T(8,128)S(1)}) custom-call(s32[3]{0:T(128)S(1)} %pad_add_fusion.pos, bf16[2304,128]{1,0:T(8,128)(2,1)S(1)} %bitcast.18, bf16[1,128,128]{2,1,0:T(8,128)(2,1)S(1)} %get-tuple-element.46.pair, f32[1,128]{1,0:T(1,128)S(1)} %get-tuple-element.47.gain.gain_ref, ...), custom_call_target="tpu_custom_call" | custom-call | tf_op jit(solution)/shard_map/pallas_call | solution.py:110
  59.7 9.9 %all_to_all.22.got = bf16[8,32,128]{2,1,0:T(8,128)(2,1)S(1)} all-to-all(bf16[8,32,128]{2,1,0:T(8,128)(2,1)S(1)} %get-tuple-element.54), channel_id=1, replica_groups={{224,228,232,236,240,244,248,252},{128,132,136,140,144,148,152,156},{16..., dimensions={0} | all-to-all | bytes 131072 | tf_op jit(solution)/shard_map/all_to_all | solution.py:375
  69.6 0.6 shard_map.207
  70.2 9.3 %all_to_all.23.mine = bf16[8,22,8,128]{3,2,1,0:T(8,128)(2,1)S(1)} all-to-all(bf16[8,22,8,128]{3,2,1,0:T(8,128)(2,1)S(1)} %shard_map.207), channel_id=1, replica_groups={{224,128,160,192,96,0,32,64},{228,132,164,196,100,4,36,68},{232,136,168..., dimensions={0} | all-to-all | bytes 720896 | tf_op jit(solution)/shard_map/all_to_all | solution.py:375
  79.4 4.0 %collective-permute-start.2 = (bf16[8,22,8,128]{3,2,1,0:T(8,128)(2,1)S(1)}, bf16[8,22,8,128]{3,2,1,0:T(8,128)(2,1)S(1)}, u32[]{:S(2)}, u32[]{:S(2)}) collective-permute-start(bf16[8,22,8,128]{3,2,1,0:T(8,128)(2,1)S(1)} %all_to_all.23.mine), channel_id=1, source_target_pairs={{0,2},{2,0},{4,6},{6,4},{8,10},{10,8},{12,14},{14,12},{16,18},{18,... | collective-permute-start | bytes 1081352 | tf_op jit(solution)/shard_map/ppermute | solution.py:447
  83.4 1.6 %shard_map.206 = (bf16[128,256]{1,0:T(8,128)(2,1)}, bf16[128,256]{1,0:T(8,128)(2,1)}, bf16[1,128,128]{2,1,0:T(8,128)(2,1)}) custom-call(s32[3]{0:T(128)S(1)} %pad_add_fusion.pos, bf16[2304,128]{1,0:T(8,128)(2,1)S(1)} %bitcast.19, f32[8,128]{1,0:T(8,128)S(1)} %get-tuple-element.50.d_bias, bf16[1,128,128]{2,1,0:T(8,128)(2,1)S(1)} %get-tuple-element.46.pair, ...), custom_call_target="tpu_custom_call" | custom-call | tf_op jit(solution)/shard_map/pallas_call | solution.py:110
  85.0 0.0 collective-permute-done.2.theirs
  85.0 1.7 %shard_map.208 = (f32[256,256]{1,0:T(8,128)}, f32[256,256]{1,0:T(8,128)}, f32[256,256]{1,0:T(8,128)}, f32[256,256]{1,0:T(8,128)}, f32[256,256]{1,0:T(8,128)}, /*...) custom-call(s32[3]{0:T(128)S(1)} %pad_add_fusion.pos, bf16[8,22,8,128]{3,2,1,0:T(8,128)(2,1)S(1)} %all_to_all.23.mine, ...), custom_call_target="tpu_custom_call" | custom-call | tf_op jit(solution)/shard_map/pallas_call | solution.py:110
Async XLA Ops:
  27.0 3.8 %collective-permute-start = (bf16[1152,128]{1,0:T(8,128)(2,1)S(1)}, bf16[1152,128]{1,0:T(8,128)(2,1)S(1)}, u32[]{:S(2)}, u32[]{:S(2)}) collective-permute-start(bf16[1152,128]{1,0:T(8,128)(2,1)S(1)} %bitcast.20), channel_id=1, source_target_pairs={{0,2},{2,0},{4,6},{6,4},{8,10},{10,8},{12,14},{14,12},{16,18},{18,... | collective-permute-start | bytes 884744 | tf_op jit(solution)/shard_map/ppermute | solution.py:401
  33.4 2.1 %collective-permute-start.1 = (bf16[32,9,8,128]{3,2,1,0:T(8,128)(2,1)S(1)}, bf16[32,9,8,128]{3,2,1,0:T(8,128)(2,1)S(1)}, u32[]{:S(2)}, u32[]{:S(2)}) collective-permute-start(bf16[32,9,8,128]{3,2,1,0:T(8,128)(2,1)S(1)} %get-tuple-element.45), channel_id=1, source_target_pairs={{0,2},{2,0},{4,6},{6,4},{8,10},{10,8},{12,14},{14,12},{16,18},{18,... | collective-permute-start | bytes 1769480 | tf_op jit(solution)/shard_map/ppermute | solution.py:421
  79.4 5.6 %collective-permute-start.2 = (bf16[8,22,8,128]{3,2,1,0:T(8,128)(2,1)S(1)}, bf16[8,22,8,128]{3,2,1,0:T(8,128)(2,1)S(1)}, u32[]{:S(2)}, u32[]{:S(2)}) collective-permute-start(bf16[8,22,8,128]{3,2,1,0:T(8,128)(2,1)S(1)} %all_to_all.23.mine), channel_id=1, source_target_pairs={{0,2},{2,0},{4,6},{6,4},{8,10},{10,8},{12,14},{14,12},{16,18},{18,... | collective-permute-start | bytes 1081352 | tf_op jit(solution)/shard_map/ppermute | solution.py:447

commit v10 on v9

--- a/solution.py
+++ b/solution.py
@@ -72,18 +72,27 @@
 
 
 LINES = (7, 4, 5, 6, 3, 0, 1, 2)
-LINE_ROWS = 2 * 8
+FIRST_Z = 6
+
+
+def turned(value):
+    blocks = value.reshape(8, 2, 8, value.shape[-1])
+    low = lax.broadcasted_iota(jnp.int32, (1, 8, 1), 1) < 4
+    upper, lower = (pltpu.roll(blocks[:, n], 4, 1) for n in range(2))
+    both = (jnp.where(low, lower, upper), jnp.where(low, upper, lower))
+    return both
 
 
 def listed(value):
+    first, second = turned(value)
+    return jnp.concatenate([v for q in LINES for v in (first[q], second[q])], axis=0)
+
+
+def natural(value):
+    first, second = turned(value)
     return jnp.concatenate(
-        [value[q * LINE_ROWS : (q + 1) * LINE_ROWS] for q in LINES], axis=0
-    )
-
-
-def natural(value):
-    at = [LINES.index(q) * LINE_ROWS for q in range(8)]
-    return jnp.concatenate([value[a : a + LINE_ROWS] for a in at], axis=0)
+        [v for q in range(8) for v in (second[LINES.index(q)], first[LINES.index(q)])], axis=0
+    )
 
 
 def reordered(rows):
@@ -365,7 +374,7 @@
 def on_device(msa, flags, pair, gain, pair_gain, wq, wk, wv, wg, wo, w_bias, grad):
     index = lax.axis_index("dap")
     pos = jnp.stack([index % CORES, index, index // CORES]).astype(jnp.int32)
-    chips = [LINE * q + z for q in LINES for z in range(LINE)]
+    chips = [LINE * q + (FIRST_Z + z) % LINE for q in LINES for z in range(LINE)]
     same_core = [[CORES * m + c for m in chips] for c in range(CORES)]
     along_z = [g[LINE * q : LINE * (q + 1)] for g in same_core for q in range(LINE)]
     across = [g[z::LINE] for g in same_core for z in range(LINE)]

time: 86.9 us -> 83.8 us (0.964)
  blocking collectives: 67.2 us -> 64.8 us
    all_to_all x4, blocking collectives: 67.2 us -> 64.8 us  [exchange(): lax.all_to_all(x, 'dap', split_axis=0, concat_axis=0, tiled=True, axis_in...]
    ppermute x1, starting transfers between devices: 2.58 us -> 1.7 us  [on_device(): far = lax.ppermute(near, 'dap', partner)]
where the time goes in v10:
time: 83.8 us; the launch traced here: 83.5 us
  blocking collectives  64.8 us (77%)
  Pallas kernels  8.71 us (10%)
  starting transfers between devices  6.3 us (8%)
  waiting for transfers between devices  2.77 us (3%)
    all_to_all x4, blocking collectives, exchange(): lax.all_to_all(x, 'dap', split_axis=0, concat_axis=0, tiled=True, axis_in...  64.8 us
    pallas_call x6, Pallas kernels, call(): pl.pallas_call(kernel, out_shape=out_shape, in_specs=in_specs, out_specs=...  8.71 us
    ppermute x1, starting transfers between devices, on_device(): theirs = lax.ppermute(mine, 'dap', partner)  4.14 us
    ppermute x1, starting transfers between devices, on_device(): far = lax.ppermute(near, 'dap', partner)  1.7 us
  transfers between devices with their start and end apart: 3, of which 2 were waited for; matrix products, arithmetic and copies ran while one was open for 0% of the time, Pallas kernels for 2%

profile of v10, /device:TPU:1, one launch (start us, length us, event | category | flops | bytes accessed | tf_op | source)
XLA Modules:
  0.0 83.5 jit_solution(460314309245191206)
XLA Ops:
  0.6 1.4 %shard_map.203 = (bf16[1152,128]{1,0:T(8,128)(2,1)S(1)}, bf16[1,128,128]{2,1,0:T(8,128)(2,1)S(1)}, f32[1,128]{1,0:T(1,128)S(1)}, bf16[8,128]{1,0:T(8,128)(2,1)S(...) custom-call(bf16[1,128,128]{2,1,0:T(8,128)(2,1)} %refs_0_.1, ...), custom_call_target="tpu_custom_call" | custom-call | tf_op jit(solution)/shard_map/pallas_call | solution.py:119
  2.0 21.9 %all_to_all.20 = bf16[64,9,2,128]{3,2,1,0:T(2,128)(2,1)S(1)} all-to-all(bf16[64,9,2,128]{3,2,1,0:T(2,128)(2,1)S(1)} %bitcast.22), channel_id=1, replica_groups={{248,252,224,228,232,236,240,244,152,156,128,132,136,140,144,148,184,18..., dimensions={0} | all-to-all | bytes 589824 | tf_op jit(solution)/shard_map/all_to_all | solution.py:384
  23.9 1.7 %collective-permute-start = (bf16[1152,128]{1,0:T(8,128)(2,1)S(1)}, bf16[1152,128]{1,0:T(8,128)(2,1)S(1)}, u32[]{:S(2)}, u32[]{:S(2)}) collective-permute-start(bf16[1152,128]{1,0:T(8,128)(2,1)S(1)} %bitcast.20), channel_id=1, source_target_pairs={{0,2},{2,0},{4,6},{6,4},{8,10},{10,8},{12,14},{14,12},{16,18},{18,... | collective-permute-start | bytes 884744 | tf_op jit(solution)/shard_map/ppermute | solution.py:410
  25.6 0.1 pad_add_fusion.pos
  25.7 1.1 %collective-permute-done.far = bf16[1152,128]{1,0:T(8,128)(2,1)S(1)} collective-permute-done((bf16[1152,128]{1,0:T(8,128)(2,1)S(1)}, bf16[1152,128]{1,0:T(8,128)(2,1)S(1)}, u32[]{:S(2)}, u32[]{:S(2)}) %collective-permute-start) | collective-permute-done | bytes 294944 | tf_op jit(solution)/shard_map/ppermute | solution.py:410
  26.9 2.6 %shard_map.204 = (f32[32,9,8,128]{3,2,1,0:T(8,128)S(1)}, bf16[32,9,8,128]{3,2,1,0:T(8,128)(2,1)S(1)}, f32[1,256]{1,0:T(1,128)S(1)}) custom-call(s32[3]{0:T(128)S(1)} %pad_add_fusion.pos, bf16[1152,128]{1,0:T(8,128)(2,1)S(1)} %bitcast.21, bf16[1152,128]{1,0:T(8,128)(2,1)S(1)} %collective-permute-done.far, f32[1,256]{1,0:T(1,128)S(1)} %get-tuple-element.38.gain_ref, ...), custom_call_target="tpu_custom_call" | custom-call | tf_op jit(solution)/shard_map/pallas_call | solution.py:119
  29.5 0.5 collective-permute-start.1
  29.9 1.6 %collective-permute-done.1 = bf16[32,9,8,128]{3,2,1,0:T(8,128)(2,1)S(1)} collective-permute-done((bf16[32,9,8,128]{3,2,1,0:T(8,128)(2,1)S(1)}, bf16[32,9,8,128]{3,2,1,0:T(8,128)(2,1)S(1)}, u32[]{:S(2)}, u32[]{:S(2)}) %collective-permute-start.1) | collective-permute-done | bytes 589856 | tf_op jit(solution)/shard_map/ppermute | solution.py:430
  31.6 0.1 add_convert_fusion
  31.7 24.1 %all_to_all.21 = bf16[64,9,4,128]{3,2,1,0:T(4,128)(2,1)S(1)} all-to-all(bf16[64,9,4,128]{3,2,1,0:T(4,128)(2,1)S(1)} %bitcast.23), channel_id=1, replica_groups={{248,252,224,228,232,236,240,244,152,156,128,132,136,140,144,148,184,18..., dimensions={0} | all-to-all | bytes 1179648 | tf_op jit(solution)/shard_map/all_to_all | solution.py:384
  55.9 0.9 %shard_map.205 = (bf16[8,32,128]{2,1,0:T(8,128)(2,1)S(1)}, f32[8,128]{1,0:T(8,128)S(1)}) custom-call(s32[3]{0:T(128)S(1)} %pad_add_fusion.pos, bf16[2304,128]{1,0:T(8,128)(2,1)S(1)} %bitcast.18, bf16[1,128,128]{2,1,0:T(8,128)(2,1)S(1)} %get-tuple-element.46.pair, f32[1,128]{1,0:T(1,128)S(1)} %get-tuple-element.47.gain.gain_ref, ...), custom_call_target="tpu_custom_call" | custom-call | tf_op jit(solution)/shard_map/pallas_call | solution.py:119
  56.8 10.1 %all_to_all.22.got = bf16[8,32,128]{2,1,0:T(8,128)(2,1)S(1)} all-to-all(bf16[8,32,128]{2,1,0:T(8,128)(2,1)S(1)} %get-tuple-element.54), channel_id=1, replica_groups={{248,252,224,228,232,236,240,244},{152,156,128,132,136,140,144,148},{18..., dimensions={0} | all-to-all | bytes 131072 | tf_op jit(solution)/shard_map/all_to_all | solution.py:384
  66.9 0.6 shard_map.207
  67.5 8.7 %all_to_all.23.mine = bf16[8,22,8,128]{3,2,1,0:T(8,128)(2,1)S(1)} all-to-all(bf16[8,22,8,128]{3,2,1,0:T(8,128)(2,1)S(1)} %shard_map.207), channel_id=1, replica_groups={{248,152,184,216,120,24,56,88},{252,156,188,220,124,28,60,92},{224,128,..., dimensions={0} | all-to-all | bytes 720896 | tf_op jit(solution)/shard_map/all_to_all | solution.py:384
  76.1 4.1 %collective-permute-start.2 = (bf16[8,22,8,128]{3,2,1,0:T(8,128)(2,1)S(1)}, bf16[8,22,8,128]{3,2,1,0:T(8,128)(2,1)S(1)}, u32[]{:S(2)}, u32[]{:S(2)}) collective-permute-start(bf16[8,22,8,128]{3,2,1,0:T(8,128)(2,1)S(1)} %all_to_all.23.mine), channel_id=1, source_target_pairs={{0,2},{2,0},{4,6},{6,4},{8,10},{10,8},{12,14},{14,12},{16,18},{18,... | collective-permute-start | bytes 1081352 | tf_op jit(solution)/shard_map/ppermute | solution.py:456
  80.3 1.6 %shard_map.206 = (bf16[128,256]{1,0:T(8,128)(2,1)}, bf16[128,256]{1,0:T(8,128)(2,1)}, bf16[1,128,128]{2,1,0:T(8,128)(2,1)}) custom-call(s32[3]{0:T(128)S(1)} %pad_add_fusion.pos, bf16[2304,128]{1,0:T(8,128)(2,1)S(1)} %bitcast.19, f32[8,128]{1,0:T(8,128)S(1)} %get-tuple-element.50.d_bias, bf16[1,128,128]{2,1,0:T(8,128)(2,1)S(1)} %get-tuple-element.46.pair, ...), custom_call_target="tpu_custom_call" | custom-call | tf_op jit(solution)/shard_map/pallas_call | solution.py:119
  81.8 0.0 collective-permute-done.2.theirs
  81.8 1.7 %shard_map.208 = (f32[256,256]{1,0:T(8,128)}, f32[256,256]{1,0:T(8,128)}, f32[256,256]{1,0:T(8,128)}, f32[256,256]{1,0:T(8,128)}, f32[256,256]{1,0:T(8,128)}, /*...) custom-call(s32[3]{0:T(128)S(1)} %pad_add_fusion.pos, bf16[8,22,8,128]{3,2,1,0:T(8,128)(2,1)S(1)} %all_to_all.23.mine, ...), custom_call_target="tpu_custom_call" | custom-call | tf_op jit(solution)/shard_map/pallas_call | solution.py:119
Async XLA Ops:
  23.9 2.9 %collective-permute-start = (bf16[1152,128]{1,0:T(8,128)(2,1)S(1)}, bf16[1152,128]{1,0:T(8,128)(2,1)S(1)}, u32[]{:S(2)}, u32[]{:S(2)}) collective-permute-start(bf16[1152,128]{1,0:T(8,128)(2,1)S(1)} %bitcast.20), channel_id=1, source_target_pairs={{0,2},{2,0},{4,6},{6,4},{8,10},{10,8},{12,14},{14,12},{16,18},{18,... | collective-permute-start | bytes 884744 | tf_op jit(solution)/shard_map/ppermute | solution.py:410
  29.5 2.1 %collective-permute-start.1 = (bf16[32,9,8,128]{3,2,1,0:T(8,128)(2,1)S(1)}, bf16[32,9,8,128]{3,2,1,0:T(8,128)(2,1)S(1)}, u32[]{:S(2)}, u32[]{:S(2)}) collective-permute-start(bf16[32,9,8,128]{3,2,1,0:T(8,128)(2,1)S(1)} %get-tuple-element.45), channel_id=1, source_target_pairs={{0,2},{2,0},{4,6},{6,4},{8,10},{10,8},{12,14},{14,12},{16,18},{18,... | collective-permute-start | bytes 1769480 | tf_op jit(solution)/shard_map/ppermute | solution.py:430
  76.1 5.7 %collective-permute-start.2 = (bf16[8,22,8,128]{3,2,1,0:T(8,128)(2,1)S(1)}, bf16[8,22,8,128]{3,2,1,0:T(8,128)(2,1)S(1)}, u32[]{:S(2)}, u32[]{:S(2)}) collective-permute-start(bf16[8,22,8,128]{3,2,1,0:T(8,128)(2,1)S(1)} %all_to_all.23.mine), channel_id=1, source_target_pairs={{0,2},{2,0},{4,6},{6,4},{8,10},{10,8},{12,14},{14,12},{16,18},{18,... | collective-permute-start | bytes 1081352 | tf_op jit(solution)/shard_map/ppermute | solution.py:456

commit v11 on v10

--- a/solution.py
+++ b/solution.py
@@ -241,14 +241,17 @@
     d_q = (dot(ds_ref[...], by_slot(k_halves)) * SCALE).astype(BF16)
     q_t = q.T
     da_t = d_attn.T
-    dk_t = []
-    dv_t = []
-    for h in range(HEADS):
-        g, s = divmod(h, 4)
-        flat = slice((2 * s + g) * LANES, (2 * s + g + 1) * LANES)
-        head = slice(h * HEAD_DIM, (h + 1) * HEAD_DIM)
-        dk_t.append(dot(q_t[head], ds_ref[:, flat]))
-        dv_t.append(dot(da_t[head], p_ref[:, flat]))
+    dk_t = [None] * HEADS
+    dv_t = [None] * HEADS
+    for s in range(4):
+        flat = slice(2 * s * LANES, 2 * (s + 1) * LANES)
+        for out, left, right in ((dk_t, q_t, ds_ref), (dv_t, da_t, p_ref)):
+            both = jnp.concatenate(
+                [left[h * HEAD_DIM : (h + 1) * HEAD_DIM] for h in (s, 4 + s)], axis=0
+            )
+            both = dot(both, right[:, flat])
+            out[s] = both[:HEAD_DIM, :LANES]
+            out[4 + s] = both[HEAD_DIM:, LANES:]
     d_k = jnp.concatenate(dk_t, axis=0).astype(BF16).T
     d_v = jnp.concatenate(dv_t, axis=0).astype(BF16).T
     weighted = (gate * attn).astype(BF16)

time: 83.8 us -> 83.7 us (level)
  no operation moved by 1% of the time
where the time goes in v11:
time: 83.7 us; the launch traced here: 83.5 us
  blocking collectives  64.8 us (77%)
  Pallas kernels  8.65 us (10%)
  starting transfers between devices  6.3 us (8%)
  waiting for transfers between devices  2.77 us (3%)
    all_to_all x4, blocking collectives, exchange(): lax.all_to_all(x, 'dap', split_axis=0, concat_axis=0, tiled=True, axis_in...  64.8 us
    pallas_call x6, Pallas kernels, call(): pl.pallas_call(kernel, out_shape=out_shape, in_specs=in_specs, out_specs=...  8.65 us
    ppermute x1, starting transfers between devices, on_device(): theirs = lax.ppermute(mine, 'dap', partner)  4.14 us
    ppermute x1, starting transfers between devices, on_device(): far = lax.ppermute(near, 'dap', partner)  1.7 us
  transfers between devices with their start and end apart: 3, of which 2 were waited for; matrix products, arithmetic and copies ran while one was open for 0% of the time, Pallas kernels for 2%

profile of v11, /device:TPU:1, one launch (start us, length us, event | category | flops | bytes accessed | tf_op | source)
XLA Modules:
  0.0 83.5 jit_solution(17883554845720281995)
XLA Ops:
  0.6 1.4 %shard_map.203 = (bf16[1152,128]{1,0:T(8,128)(2,1)S(1)}, bf16[1,128,128]{2,1,0:T(8,128)(2,1)S(1)}, f32[1,128]{1,0:T(1,128)S(1)}, bf16[8,128]{1,0:T(8,128)(2,1)S(...) custom-call(bf16[1,128,128]{2,1,0:T(8,128)(2,1)} %refs_0_.1, ...), custom_call_target="tpu_custom_call" | custom-call | tf_op jit(solution)/shard_map/pallas_call | solution.py:119
  2.0 21.9 %all_to_all.20 = bf16[64,9,2,128]{3,2,1,0:T(2,128)(2,1)S(1)} all-to-all(bf16[64,9,2,128]{3,2,1,0:T(2,128)(2,1)S(1)} %bitcast.22), channel_id=1, replica_groups={{248,252,224,228,232,236,240,244,152,156,128,132,136,140,144,148,184,18..., dimensions={0} | all-to-all | bytes 589824 | tf_op jit(solution)/shard_map/all_to_all | solution.py:387
  23.9 1.7 %collective-permute-start = (bf16[1152,128]{1,0:T(8,128)(2,1)S(1)}, bf16[1152,128]{1,0:T(8,128)(2,1)S(1)}, u32[]{:S(2)}, u32[]{:S(2)}) collective-permute-start(bf16[1152,128]{1,0:T(8,128)(2,1)S(1)} %bitcast.20), channel_id=1, source_target_pairs={{0,2},{2,0},{4,6},{6,4},{8,10},{10,8},{12,14},{14,12},{16,18},{18,... | collective-permute-start | bytes 884744 | tf_op jit(solution)/shard_map/ppermute | solution.py:413
  25.6 0.1 pad_add_fusion.pos
  25.7 1.1 %collective-permute-done.far = bf16[1152,128]{1,0:T(8,128)(2,1)S(1)} collective-permute-done((bf16[1152,128]{1,0:T(8,128)(2,1)S(1)}, bf16[1152,128]{1,0:T(8,128)(2,1)S(1)}, u32[]{:S(2)}, u32[]{:S(2)}) %collective-permute-start) | collective-permute-done | bytes 294944 | tf_op jit(solution)/shard_map/ppermute | solution.py:413
  26.9 2.5 %shard_map.204 = (f32[32,9,8,128]{3,2,1,0:T(8,128)S(1)}, bf16[32,9,8,128]{3,2,1,0:T(8,128)(2,1)S(1)}, f32[1,256]{1,0:T(1,128)S(1)}) custom-call(s32[3]{0:T(128)S(1)} %pad_add_fusion.pos, bf16[1152,128]{1,0:T(8,128)(2,1)S(1)} %bitcast.21, bf16[1152,128]{1,0:T(8,128)(2,1)S(1)} %collective-permute-done.far, f32[1,256]{1,0:T(1,128)S(1)} %get-tuple-element.38.gain_ref, ...), custom_call_target="tpu_custom_call" | custom-call | tf_op jit(solution)/shard_map/pallas_call | solution.py:119
  29.4 0.5 collective-permute-start.1
  29.9 1.6 %collective-permute-done.1 = bf16[32,9,8,128]{3,2,1,0:T(8,128)(2,1)S(1)} collective-permute-done((bf16[32,9,8,128]{3,2,1,0:T(8,128)(2,1)S(1)}, bf16[32,9,8,128]{3,2,1,0:T(8,128)(2,1)S(1)}, u32[]{:S(2)}, u32[]{:S(2)}) %collective-permute-start.1) | collective-permute-done | bytes 589856 | tf_op jit(solution)/shard_map/ppermute | solution.py:433
  31.5 0.1 add_convert_fusion
  31.7 24.1 %all_to_all.21 = bf16[64,9,4,128]{3,2,1,0:T(4,128)(2,1)S(1)} all-to-all(bf16[64,9,4,128]{3,2,1,0:T(4,128)(2,1)S(1)} %bitcast.23), channel_id=1, replica_groups={{248,252,224,228,232,236,240,244,152,156,128,132,136,140,144,148,184,18..., dimensions={0} | all-to-all | bytes 1179648 | tf_op jit(solution)/shard_map/all_to_all | solution.py:387
  55.8 0.9 %shard_map.205 = (bf16[8,32,128]{2,1,0:T(8,128)(2,1)S(1)}, f32[8,128]{1,0:T(8,128)S(1)}) custom-call(s32[3]{0:T(128)S(1)} %pad_add_fusion.pos, bf16[2304,128]{1,0:T(8,128)(2,1)S(1)} %bitcast.18, bf16[1,128,128]{2,1,0:T(8,128)(2,1)S(1)} %get-tuple-element.46.pair, f32[1,128]{1,0:T(1,128)S(1)} %get-tuple-element.47.gain.gain_ref, ...), custom_call_target="tpu_custom_call" | custom-call | tf_op jit(solution)/shard_map/pallas_call | solution.py:119
  56.7 10.1 %all_to_all.22.got = bf16[8,32,128]{2,1,0:T(8,128)(2,1)S(1)} all-to-all(bf16[8,32,128]{2,1,0:T(8,128)(2,1)S(1)} %get-tuple-element.54), channel_id=1, replica_groups={{248,252,224,228,232,236,240,244},{152,156,128,132,136,140,144,148},{18..., dimensions={0} | all-to-all | bytes 131072 | tf_op jit(solution)/shard_map/all_to_all | solution.py:387
  66.8 0.6 shard_map.207
  67.4 8.7 %all_to_all.23.mine = bf16[8,22,8,128]{3,2,1,0:T(8,128)(2,1)S(1)} all-to-all(bf16[8,22,8,128]{3,2,1,0:T(8,128)(2,1)S(1)} %shard_map.207), channel_id=1, replica_groups={{248,152,184,216,120,24,56,88},{252,156,188,220,124,28,60,92},{224,128,..., dimensions={0} | all-to-all | bytes 720896 | tf_op jit(solution)/shard_map/all_to_all | solution.py:387
  76.1 4.1 %collective-permute-start.2 = (bf16[8,22,8,128]{3,2,1,0:T(8,128)(2,1)S(1)}, bf16[8,22,8,128]{3,2,1,0:T(8,128)(2,1)S(1)}, u32[]{:S(2)}, u32[]{:S(2)}) collective-permute-start(bf16[8,22,8,128]{3,2,1,0:T(8,128)(2,1)S(1)} %all_to_all.23.mine), channel_id=1, source_target_pairs={{0,2},{2,0},{4,6},{6,4},{8,10},{10,8},{12,14},{14,12},{16,18},{18,... | collective-permute-start | bytes 1081352 | tf_op jit(solution)/shard_map/ppermute | solution.py:459
  80.2 1.6 %shard_map.206 = (bf16[128,256]{1,0:T(8,128)(2,1)}, bf16[128,256]{1,0:T(8,128)(2,1)}, bf16[1,128,128]{2,1,0:T(8,128)(2,1)}) custom-call(s32[3]{0:T(128)S(1)} %pad_add_fusion.pos, bf16[2304,128]{1,0:T(8,128)(2,1)S(1)} %bitcast.19, f32[8,128]{1,0:T(8,128)S(1)} %get-tuple-element.50.d_bias, bf16[1,128,128]{2,1,0:T(8,128)(2,1)S(1)} %get-tuple-element.46.pair, ...), custom_call_target="tpu_custom_call" | custom-call | tf_op jit(solution)/shard_map/pallas_call | solution.py:119
  81.8 0.0 collective-permute-done.2.theirs
  81.8 1.7 %shard_map.208 = (f32[256,256]{1,0:T(8,128)}, f32[256,256]{1,0:T(8,128)}, f32[256,256]{1,0:T(8,128)}, f32[256,256]{1,0:T(8,128)}, f32[256,256]{1,0:T(8,128)}, /*...) custom-call(s32[3]{0:T(128)S(1)} %pad_add_fusion.pos, bf16[8,22,8,128]{3,2,1,0:T(8,128)(2,1)S(1)} %all_to_all.23.mine, ...), custom_call_target="tpu_custom_call" | custom-call | tf_op jit(solution)/shard_map/pallas_call | solution.py:119
Async XLA Ops:
  23.9 2.9 %collective-permute-start = (bf16[1152,128]{1,0:T(8,128)(2,1)S(1)}, bf16[1152,128]{1,0:T(8,128)(2,1)S(1)}, u32[]{:S(2)}, u32[]{:S(2)}) collective-permute-start(bf16[1152,128]{1,0:T(8,128)(2,1)S(1)} %bitcast.20), channel_id=1, source_target_pairs={{0,2},{2,0},{4,6},{6,4},{8,10},{10,8},{12,14},{14,12},{16,18},{18,... | collective-permute-start | bytes 884744 | tf_op jit(solution)/shard_map/ppermute | solution.py:413
  29.4 2.1 %collective-permute-start.1 = (bf16[32,9,8,128]{3,2,1,0:T(8,128)(2,1)S(1)}, bf16[32,9,8,128]{3,2,1,0:T(8,128)(2,1)S(1)}, u32[]{:S(2)}, u32[]{:S(2)}) collective-permute-start(bf16[32,9,8,128]{3,2,1,0:T(8,128)(2,1)S(1)} %get-tuple-element.45), channel_id=1, source_target_pairs={{0,2},{2,0},{4,6},{6,4},{8,10},{10,8},{12,14},{14,12},{16,18},{18,... | collective-permute-start | bytes 1769480 | tf_op jit(solution)/shard_map/ppermute | solution.py:433
  76.1 5.7 %collective-permute-start.2 = (bf16[8,22,8,128]{3,2,1,0:T(8,128)(2,1)S(1)}, bf16[8,22,8,128]{3,2,1,0:T(8,128)(2,1)S(1)}, u32[]{:S(2)}, u32[]{:S(2)}) collective-permute-start(bf16[8,22,8,128]{3,2,1,0:T(8,128)(2,1)S(1)} %all_to_all.23.mine), channel_id=1, source_target_pairs={{0,2},{2,0},{4,6},{6,4},{8,10},{10,8},{12,14},{14,12},{16,18},{18,... | collective-permute-start | bytes 1081352 | tf_op jit(solution)/shard_map/ppermute | solution.py:459
